TPU v7x, 32 devices: a whole 2x2x4 slice. The times are simulated.
32 devices in a mesh: gx: 8 (over y, x, core), gy: 4 (over z).
Axes of the slice: x: 2, y: 2, z: 4, core: 2. Of those that a mesh axis runs over, the one named last changes fastest.
Arguments:
- state: float32 [54, 64, 4096], P(None, 'gx', 'gy'), may hold values from 0.05 to 3, as said below
- diffusivity: float32 [54], replicated, may hold values from 0.02 to 0.1
- log_prefactor: float32 [325], replicated, may hold values from -1 to 1
- activation: float32 [325], replicated, may hold values from 0.5 to 4
- heat: float32 [325], replicated, may hold values from 0.005 to 0.05
- reactants: float32 [650, 53], replicated, may hold values from 0 to 1, as said below
- products: float32 [53, 325], replicated, may hold values from 0 to 2, as said below
- substeps: int32 [64, 32], P('gx', 'gy'), may hold values from 1 to 4
- flame: int32 [64, 32], P('gx', 'gy'), may hold values from 0 to 1, as said below
Outputs:
- next_state: float32 [54, 64, 4096], P(None, 'gx', 'gy')
Inputs may be any that keep to these rules, and one draw needn't show every extreme that they name: `state`: component 0 is the temperature, from 1 to 3; the other components are concentrations from 0.05 to 2. `reactants`: each row is one-hot: it names one species. `products`: column r is the sum of two one-hot columns, the two products of reaction r. `flame`: within the 8 x (8) entries that one device holds, at most 4 are 1. In every draw there is one index along the first mesh axis where every device holds exactly 4; elsewhere a device holds 4 with probability 1/4 and otherwise 0 to 2.
All inputs are finite; a program needn't handle non-finite values.
Results may differ from a plain program's by a relative error of at most 0.0001.
Values sent between devices are 32-bit elements; how exact they have to be, the bound alone decides.
No kernel may reach another device: no remote copies, remote signals or barrier semaphores. Data moves between devices by JAX's collectives and lax.ppermute only.
A program may use at most 128 MiB of HBM per device.

v0:
```python
import functools

import jax
import jax.numpy as jnp
import numpy as np
from jax import lax
from jax.experimental import pallas as pl
from jax.experimental.pallas import tpu as pltpu
from jax.sharding import PartitionSpec as P

NZ = 32
LANES = 128
near_weight = 4.0 / 3.0
far_weight = 1.0 / 12.0
LOG2E = 1.4426950408889634
GROUP = 4
FIRST_CHUNK = 34
PIECE = 64

VMEM = pltpu.VMEM
SMEM = pltpu.SMEM


def params(mib):
    return pltpu.CompilerParams(vmem_limit_bytes=mib << 20)


def high_side(parity_flip):
    odd = lax.rem(lax.axis_index("gx"), 2)
    return odd if not parity_flip else 1 - odd


def pack_kernel(comps, planes, tiles, split, s_ref, a0_ref, a1_ref, b_ref, lo_ref, hi_ref):
    rows = planes * tiles
    far_side = high_side(False)
    lane = lax.broadcasted_iota(jnp.int32, (planes, LANES), 1)

    def plane(c, x):
        return s_ref[pl.ds(c * rows + x, tiles, stride=planes), :]

    off_a = far_side * (planes - 2)
    off_b = (1 - far_side) * (planes - 2)
    for c in range(comps):
        for p in range(2):
            if c < split:
                a0_ref[c, p] = plane(c, off_a + p)
            else:
                a1_ref[c - split, p] = plane(c, off_a + p)
    for c in range(comps):
        for p in range(2):
            b_ref[c, p] = plane(c, off_b + p)
    for k in range(comps // 2):
        even, odd = 2 * k * rows, (2 * k + 1) * rows
        last = (tiles - 1) * planes
        first_even = s_ref[even : even + planes, :]
        first_odd = s_ref[odd : odd + planes, :]
        last_even = s_ref[even + last : even + last + planes, :]
        last_odd = s_ref[odd + last : odd + last + planes, :]
        lo_ref[k] = jnp.where(lane < 64, first_even, pltpu.roll(first_odd, 64, 1))
        hi_ref[k] = jnp.where(lane < 64, pltpu.roll(last_even, 64, 1), last_odd)


def split3(value):
    high = value.astype(jnp.bfloat16)
    rest = value - high.astype(jnp.float32)
    middle = rest.astype(jnp.bfloat16)
    low = (rest - middle.astype(jnp.float32)).astype(jnp.bfloat16)
    return high, middle, low


def main_kernel(
    comps,
    planes,
    tiles,
    nreact,
    s_ref,
    d_ref,
    shift_ref,
    lp_hbm,
    act_hbm,
    heat_hbm,
    rt_hbm,
    pr_hbm,
    sub_ref,
    flame_ref,
    o_ref,
    lp_ref,
    act_ref,
    heat_ref,
    rt_ref,
    pr_ref,
    q_ref,
    p_ref,
    w1_ref,
    w2_ref,
    a_ref,
    t_ref,
    st_ref,
    pos_ref,
    sem,
):
    rows = planes * tiles
    species = comps - 1
    block_rows = planes * tiles
    loads = [
        pltpu.make_async_copy(source, target, sem.at[i])
        for i, (source, target) in enumerate(
            (
                (lp_hbm, lp_ref),
                (act_hbm, act_ref),
                (heat_hbm, heat_ref),
                (rt_hbm, rt_ref),
                (pr_hbm, pr_ref),
            )
        )
    ]
    for load in loads:
        load.start()

    count = jnp.int32(0)
    for x in range(planes):
        for b in range(tiles):
            pos_ref[count] = b * planes + x
            count = count + flame_ref[x, b]

    many = max(n for n in range(1, 7) if comps % n == 0)
    shape = (many, tiles, planes, LANES)
    lane = lax.broadcasted_iota(jnp.int32, (1, 1, planes, LANES), 3)
    x = lax.broadcasted_iota(jnp.int32, (1, 1, planes, LANES), 2)
    zero = jnp.zeros((many, 1, planes, LANES), jnp.float32)
    near, far = near_weight * 12.0, -far_weight * 12.0
    up1 = jnp.where(x > 0, near, 0.0)
    down1 = jnp.where(x < planes - 1, near, 0.0)
    up2 = jnp.where(x > 1, far, 0.0)
    down2 = jnp.where(x < planes - 2, far, 0.0)
    shifts = shift_ref[...]

    def components(i, carry):
        start = pl.multiple_of(i * many * rows, many * rows)
        flat = s_ref[pl.ds(start, many * rows), :]
        high = flat.astype(jnp.bfloat16)
        low = (flat - high.astype(jnp.float32)).astype(jnp.bfloat16)
        both = jnp.concatenate([high, low], 1)
        out = jnp.dot(both, shifts, preferred_element_type=jnp.float32)
        v = flat.reshape(shape)
        own = out[:, :LANES].reshape(shape)
        cross = out[:, LANES:].reshape(shape)
        before = jnp.concatenate([zero, cross[:, :-1]], 1)
        after = jnp.concatenate([cross[:, 1:], zero], 1)
        own = own + jnp.where(lane < 64, before, after)
        own = own + (pltpu.roll(v, 1, 2) * up1 + pltpu.roll(v, planes - 1, 2) * down1)
        own = own + (pltpu.roll(v, 2, 2) * up2 + pltpu.roll(v, planes - 2, 2) * down2)
        for j in range(many):
            where = pl.ds(pl.multiple_of(start + j * rows, rows), rows)
            scale = d_ref[i * many + j] * (1.0 / 12.0)
            o_ref[where, :] = (v[j] + scale * own[j]).reshape(rows, LANES)
        return carry

    lax.fori_loop(0, comps // many, components, 0)
    for load in loads:
        load.wait()

    @pl.when(count > 0)
    def _():
        padded = q_ref.shape[1]
        wide = w1_ref.shape[0]
        q_ref[...] = jnp.zeros_like(q_ref)
        p_ref[...] = jnp.zeros_like(p_ref)
        q_ref[0:species, 0:nreact] = rt_ref[:, 0:nreact] + rt_ref[:, nreact : 2 * nreact]
        p_ref[0:species, 0:nreact] = pr_ref[...]
        p_ref[PIECE : PIECE + species, 0:nreact] = q_ref[0:species, 0:nreact]
        for i, piece in enumerate(split3(act_ref[...].reshape(1, nreact) * (-LOG2E))):
            q_ref[species + i : species + i + 1, 0:nreact] = piece.astype(jnp.float32)
        for i, piece in enumerate(split3(lp_ref[...].reshape(1, nreact) * LOG2E)):
            q_ref[species + 3 + i : species + 4 + i, 0:nreact] = piece.astype(jnp.float32)
        for i, piece in enumerate(split3(heat_ref[...].reshape(1, nreact))):
            p_ref[species + i : species + i + 1, 0:nreact] = piece.astype(jnp.float32)
        q = q_ref[...]
        w1 = jnp.transpose(jnp.concatenate([q, q, q], 0))
        w1_ref[...] = w1[0:wide].astype(jnp.bfloat16)
        w = p_ref[...].astype(jnp.bfloat16)
        head, rest = w[:, :256], w[:, 256:padded]
        w2_ref[...] = jnp.concatenate([head, head, rest, rest], 1)

        a_ref[...] = jnp.ones_like(a_ref)
        arow = lax.broadcasted_iota(jnp.int32, a_ref.shape, 0)

        def group(g, carry):
            most = jnp.int32(0)
            pieces = []
            for i in range(GROUP):
                slot = g * GROUP + i
                here = jnp.where(slot < count, slot, 0)
                at = pos_ref[here]
                n = jnp.where(
                    slot < count, sub_ref[lax.rem(at, planes), lax.div(at, planes)], 0
                )
                most = jnp.maximum(most, n)
                cols = slice(i * LANES, (i + 1) * LANES)
                a_ref[0:species, cols] = s_ref[pl.ds(block_rows + at, species, stride=rows), :]
                t_ref[:, cols] = s_ref[pl.ds(at, 1), :]
                pieces.append(jnp.full((1, LANES), n, jnp.int32))
            counts = jnp.concatenate(pieces, 1)
            st_ref[...] = 1.0 / jnp.maximum(counts, 1).astype(jnp.float32)

            def substep(k, inner):
                step = jnp.where(counts > k, st_ref[...], 0.0)
                amounts = a_ref[...]
                thermal = t_ref[...]
                inverse = 1.0 / thermal
                terms = jnp.where(
                    arow < species,
                    jnp.log2(amounts),
                    jnp.where(
                        arow < species + 3, inverse, jnp.where(arow < species + 6, 1.0, 0.0)
                    ),
                )
                rhs = jnp.concatenate(split3(terms), 0)
                exponent = jnp.dot(w1_ref[...], rhs, preferred_element_type=jnp.float32)
                progress = jnp.exp2(exponent)
                high = progress.astype(jnp.bfloat16)
                low = (progress - high.astype(jnp.float32)).astype(jnp.bfloat16)
                gap = 2 * LANES - wide + LANES
                rhs = jnp.concatenate(
                    [high[:256], low[:256], high[256:], high[:gap], low[256:], low[:gap]], 0
                )
                out = jnp.dot(w2_ref[...], rhs, preferred_element_type=jnp.float32)
                produced = out[:PIECE]
                loss = out[PIECE:]
                warm = out[species : species + 1] + (
                    out[species + 1 : species + 2] + out[species + 2 : species + 3]
                )
                a_ref[...] = (amounts + step * produced) * (amounts / (amounts + step * loss))
                t_ref[...] = thermal + step * warm
                return inner

            lax.fori_loop(0, most, substep, 0)

            for i in range(GROUP):
                slot = g * GROUP + i

                @pl.when(slot < count)
                def _(i=i, slot=slot):
                    at = pos_ref[slot]
                    cols = slice(i * LANES, (i + 1) * LANES)
                    where = pl.ds(block_rows + at, species, stride=rows)
                    o_ref[where, :] = o_ref[where, :] + (a_ref[0:species, cols] - s_ref[where, :])
                    top = pl.ds(at, 1)
                    o_ref[top, :] = o_ref[top, :] + (t_ref[:, cols] - s_ref[top, :])

            return carry

        lax.fori_loop(0, (count + (GROUP - 1)) // GROUP, group, 0)


def add_plane(planes, tiles, work, weight, c, h_ref, index, side):
    rows = planes * tiles
    near = h_ref[index, 1 - side]
    far = h_ref[index, side]
    first = pl.ds(c * rows + side * (planes - 1), tiles, stride=planes)
    second = pl.ds(c * rows + 1 + side * (planes - 3), tiles, stride=planes)
    work[first, :] = work[first, :] + weight * (near_weight * near - far_weight * far)
    work[second, :] = work[second, :] - weight * (far_weight * near)


def send_out(rows, begin, end, work, out_hbm, sem):
    where = pl.ds(begin * rows, (end - begin) * rows)
    copy = pltpu.make_async_copy(work.at[where, :], out_hbm.at[where, :], sem)
    copy.start()
    return copy


def inner_edges_kernel(
    comps, planes, tiles, split, part_ref, d_ref, ha_ref, hb_ref, zl_ref, zh_ref, work, out, sem
):
    rows = planes * tiles
    lane = lax.broadcasted_iota(jnp.int32, (planes, LANES), 1)
    side_a = high_side(False)
    side_b = 1 - side_a
    last = (tiles - 1) * planes
    copies = []
    done = 0
    for k in range(comps // 2):
        low = zl_ref[k]
        high = zh_ref[k]
        low = near_weight * jnp.where(lane % 64 < NZ, pltpu.roll(low, LANES - NZ, 1), 0.0) - (
            far_weight * low
        )
        high = near_weight * jnp.where(lane % 64 >= NZ, pltpu.roll(high, NZ, 1), 0.0) - (
            far_weight * high
        )
        other_low = pltpu.roll(low, 64, 1)
        other_high = pltpu.roll(high, 64, 1)
        for j in range(2):
            c = 2 * k + j
            weight = d_ref[c]
            mine_low = low if j == 0 else other_low
            mine_high = high if j == 1 else other_high
            top = slice(c * rows, c * rows + planes)
            work[top, :] = work[top, :] + jnp.where(lane < 64, weight * mine_low, 0.0)
            end = slice(c * rows + last, c * rows + last + planes)
            work[end, :] = work[end, :] + jnp.where(lane >= 64, weight * mine_high, 0.0)
            add_plane(planes, tiles, work, weight, c, hb_ref, c, side_b)
            if c < split:
                add_plane(planes, tiles, work, weight, c, ha_ref, c, side_a)
        now = 2 * k + 2
        if now <= split and (now - done >= 10 or now == split):
            copies.append(send_out(rows, done, now, work, out, sem.at[len(copies)]))
            done = now
    for copy in copies:
        copy.wait()


def outer_edges_kernel(comps, planes, tiles, split, part_ref, d_ref, ha_ref, prev, work, out, sem):
    rows = planes * tiles
    side = high_side(False)
    copies = []
    done = split
    for c in range(split, comps):
        add_plane(planes, tiles, work, d_ref[c], c, ha_ref, c - split, side)
        now = c + 1
        if now - done >= 5 or now == comps:
            copies.append(send_out(rows, done, now, work, out, sem.at[len(copies)]))
            done = now
    for copy in copies:
        copy.wait()


def shift_matrix():
    source = np.arange(LANES)[:, None]
    target = np.arange(LANES)[None, :]
    weights = {1: 16.0, 2: -1.0}
    ys, yt, zs, zt = source // NZ, target // NZ, source % NZ, target % NZ
    rows = LANES // NZ
    own = np.where(source == target, -90.0, 0.0)
    cross = np.zeros_like(own)
    for distance, weight in weights.items():
        turn = (zt - zs) % NZ
        own += np.where((ys == yt) & ((turn == distance) | (turn == NZ - distance)), weight, 0.0)
        own += np.where((zs == zt) & (abs(yt - ys) == distance), weight, 0.0)
        to_next = (target < 64) & (zs == zt) & (yt + rows - ys == distance)
        to_previous = (target >= 64) & (zs == zt) & (ys + rows - yt == distance)
        cross += np.where(to_next | to_previous, weight, 0.0)
    one = np.concatenate([own, cross], 1)
    return jnp.asarray(np.concatenate([one, one], 0), jnp.bfloat16)


def per_device(
    state, diffusivity, log_prefactor, activation, heat, reactants, products, substeps, flame
):
    comps, planes, cells = state.shape
    tiles = cells // LANES
    rows = planes * tiles
    nreact = log_prefactor.shape[0]
    split = FIRST_CHUNK
    gx, gy = lax.axis_size("gx"), lax.axis_size("gy")
    f32 = jnp.float32
    flat = (
        state.reshape(comps, planes, tiles, LANES)
        .transpose(0, 2, 1, 3)
        .reshape(comps * rows, LANES)
    )
    vmem = pl.BlockSpec(memory_space=VMEM)
    smem = pl.BlockSpec(memory_space=SMEM)
    anywhere = pl.BlockSpec(memory_space=pl.ANY)

    sds = jax.ShapeDtypeStruct
    a0, a1, b, lo, hi = pl.pallas_call(
        functools.partial(pack_kernel, comps, planes, tiles, split),
        out_shape=(
            sds((split, 2, tiles, LANES), f32),
            sds((comps - split, 2, tiles, LANES), f32),
            sds((comps, 2, tiles, LANES), f32),
            sds((comps // 2, planes, LANES), f32),
            sds((comps // 2, planes, LANES), f32),
        ),
        in_specs=[vmem],
        out_specs=[vmem] * 5,
        compiler_params=params(16),
        name="pack",
    )(flat)

    outer = [(i, (i + 1) % gx) for i in range(1, gx, 2)]
    outer = outer + [(t, s) for s, t in outer]
    inner = [(i, i + 1) for i in range(0, gx, 2)]
    inner = inner + [(t, s) for s, t in inner]
    forward = [(i, (i + 1) % gy) for i in range(gy)]
    backward = [(t, s) for s, t in forward]
    ha0 = lax.ppermute(a0, "gx", outer)
    ha1 = lax.ppermute(a1, "gx", outer)
    hb = lax.ppermute(b, "gx", inner)
    zl = lax.ppermute(hi, "gy", forward)
    zh = lax.ppermute(lo, "gy", backward)

    padded = pl.cdiv(nreact, LANES) * LANES
    wide = pl.cdiv(nreact, 16) * 16
    part = pl.pallas_call(
        functools.partial(main_kernel, comps, planes, tiles, nreact),
        out_shape=sds((comps * rows, LANES), f32),
        in_specs=[vmem, smem, vmem] + [anywhere] * 5 + [smem, smem],
        out_specs=vmem,
        scratch_shapes=[
            VMEM((nreact,), f32),
            VMEM((nreact,), f32),
            VMEM((nreact,), f32),
            VMEM((comps - 1, 2 * nreact), f32),
            VMEM((comps - 1, nreact), f32),
            VMEM((PIECE, padded), f32),
            VMEM((2 * PIECE, padded), f32),
            VMEM((wide, 3 * PIECE), jnp.bfloat16),
            VMEM((2 * PIECE, 2 * padded), jnp.bfloat16),
            VMEM((PIECE, GROUP * LANES), f32),
            VMEM((1, GROUP * LANES), f32),
            VMEM((1, GROUP * LANES), f32),
            SMEM((rows + 1,), jnp.int32),
            pltpu.SemaphoreType.DMA((5,)),
        ],
        compiler_params=params(24),
        cost_estimate=pl.CostEstimate(
            flops=2_000_000_000, bytes_accessed=16_000_000, transcendentals=1_000_000
        ),
        name="main",
    )(
        flat,
        diffusivity,
        shift_matrix(),
        log_prefactor,
        activation,
        heat,
        reactants.T,
        products,
        substeps,
        flame,
    )

    whole = sds((comps * rows, LANES), f32)
    cost = pl.CostEstimate(flops=1_000_000, bytes_accessed=3_000_000, transcendentals=0)
    part, out = pl.pallas_call(
        functools.partial(inner_edges_kernel, comps, planes, tiles, split),
        out_shape=(whole, whole),
        in_specs=[vmem, smem, vmem, vmem, vmem, vmem],
        out_specs=(vmem, anywhere),
        scratch_shapes=[pltpu.SemaphoreType.DMA((8,))],
        input_output_aliases={0: 0},
        compiler_params=params(16),
        cost_estimate=cost,
        name="inner_edges",
    )(part, diffusivity, ha0, hb, zl, zh)
    part, out = pl.pallas_call(
        functools.partial(outer_edges_kernel, comps, planes, tiles, split),
        out_shape=(whole, whole),
        in_specs=[vmem, smem, vmem, anywhere],
        out_specs=(vmem, anywhere),
        scratch_shapes=[pltpu.SemaphoreType.DMA((8,))],
        input_output_aliases={0: 0, 3: 1},
        compiler_params=params(16),
        cost_estimate=cost,
        name="outer_edges",
    )(part, diffusivity, ha1, out)
    return (
        out.reshape(comps, tiles, planes, LANES).transpose(0, 2, 1, 3).reshape(comps, planes, cells)
    )


def solution(mesh):
    in_specs = (P(None, "gx", "gy"), P(), P(), P(), P(), P(), P(), P("gx", "gy"), P("gx", "gy"))
    out_specs = P(None, "gx", "gy")

    return jax.shard_map(
        per_device, mesh=mesh, in_specs=in_specs, out_specs=out_specs, check_vma=False
    )
```

profile of v0, /device:TPU:7, one launch (start us, length us, event | category | flops | bytes accessed | tf_op | source)
XLA Modules:
  0.0 22.6 jit_solution(5534694991773552620)
XLA Ops:
  0.0 0.0 copy-start.2
  0.0 0.0 copy-start
  0.0 1.5 %copy-done = f32[54,8,1024]{2,1,0:T(8,128)S(1)} copy-done((f32[54,8,1024]{2,1,0:T(8,128)S(1)}, f32[54,8,1024]{2,1,0:T(8,128)}, u32[]{:S(2)}) %copy-start) | copy-done | bytes 1769496
  1.5 0.0 copy-start.1
  1.5 0.0 copy-start.5
  1.5 0.0 copy-start.6
  1.5 0.0 copy-start.7
  1.5 0.2 pack.1
  1.7 0.7 %collective-permute-start.1 = (f32[54,2,8,128]{3,2,1,0:T(8,128)S(1)}, f32[54,2,8,128]{3,2,1,0:T(8,128)S(1)}, u32[]{:S(2)}, u32[]{:S(2)}) collective-permute-start(f32[54,2,8,128]{3,2,1,0:T(8,128)S(1)} %get-tuple-element.14), channel_id=1, source_target_pairs={{0,4},{8,12},{16,20},{24,28},{4,0},{12,8},{20,16},{28,24},{1,5},{9... | collective-permute-start | bytes 1327112 | tf_op jit(solution)/shard_map/ppermute | solution.py:391
  2.5 0.0 collective-permute-start
  2.5 1.5 %collective-permute-start.2 = (f32[27,8,128]{2,1,0:T(8,128)S(1)}, f32[27,8,128]{2,1,0:T(8,128)S(1)}, u32[]{:S(2)}, u32[]{:S(2)}) collective-permute-start(f32[27,8,128]{2,1,0:T(8,128)S(1)} %get-tuple-element.15), channel_id=1, source_target_pairs={{0,1},{1,2},{2,3},{3,0},{4,5},{5,6},{6,7},{7,4},{8,9},{9,10},{10,1... | collective-permute-start | bytes 331784 | tf_op jit(solution)/shard_map/ppermute | solution.py:392
  3.9 2.0 %collective-permute-start.3 = (f32[27,8,128]{2,1,0:T(8,128)S(1)}, f32[27,8,128]{2,1,0:T(8,128)S(1)}, u32[]{:S(2)}, u32[]{:S(2)}) collective-permute-start(f32[27,8,128]{2,1,0:T(8,128)S(1)} %get-tuple-element.16), channel_id=1, source_target_pairs={{1,0},{2,1},{3,2},{0,3},{5,4},{6,5},{7,6},{4,7},{9,8},{10,9},{11,1... | collective-permute-start | bytes 331784 | tf_op jit(solution)/shard_map/ppermute | solution.py:393
  5.9 3.0 %collective-permute-start.4 = (f32[20,2,8,128]{3,2,1,0:T(8,128)S(1)}, f32[20,2,8,128]{3,2,1,0:T(8,128)S(1)}, u32[]{:S(2)}, u32[]{:S(2)}) collective-permute-start(f32[20,2,8,128]{3,2,1,0:T(8,128)S(1)} %get-tuple-element.18), channel_id=1, source_target_pairs={{4,8},{12,16},{20,24},{28,0},{8,4},{16,12},{24,20},{0,28},{5,9},{1... | collective-permute-start | bytes 491528 | tf_op jit(solution)/shard_map/ppermute | solution.py:390
  8.9 0.0 copy-done.2
  8.9 0.0 copy-done.1
  8.9 0.0 copy-done.5
  8.9 0.0 copy-done.6
  8.9 0.0 copy-done.7
  9.0 0.0 copy-start.3
  9.0 0.9 %copy-done.3 = f32[650,53]{0,1:T(8,128)S(1)} copy-done((f32[650,53]{0,1:T(8,128)S(1)}, f32[650,53]{0,1:T(8,128)}, u32[]{:S(2)}) %copy-start.3) | copy-done | bytes 137824
  9.9 0.0 copy-start.4
  9.9 0.9 %copy-done.4 = f32[53,325]{1,0:T(8,128)S(1)} copy-done((f32[53,325]{1,0:T(8,128)S(1)}, f32[53,325]{1,0:T(8,128)}, u32[]{:S(2)}) %copy-start.4) | copy-done | bytes 68924
  10.8 0.0 copy-start.8
  10.8 0.7 %copy-done.8 = f32[325]{0:T(512)S(1)} copy-done((f32[325]{0:T(512)S(1)}, f32[325]{0:T(512)}, u32[]{:S(2)}) %copy-start.8) | copy-done | bytes 1324
  11.4 0.0 copy-start.9
  11.4 0.7 %copy-done.9 = f32[325]{0:T(512)S(1)} copy-done((f32[325]{0:T(512)S(1)}, f32[325]{0:T(512)}, u32[]{:S(2)}) %copy-start.9) | copy-done | bytes 1324
  12.1 0.0 copy-start.10
  12.1 0.9 %copy-done.10 = bf16[256,256]{1,0:T(8,128)(2,1)S(1)} copy-done((bf16[256,256]{1,0:T(8,128)(2,1)S(1)}, bf16[256,256]{1,0:T(8,128)(2,1)}, u32[]{:S(2)}) %copy-start.10) | copy-done | bytes 131096
  13.0 5.9 %main.1.part_ref = f32[3456,128]{1,0:T(8,128)S(1)} custom-call(f32[3456,128]{1,0:T(8,128)S(1)} %bitcast.12, f32[54]{0:T(128)S(1)} %copy-done.2, bf16[256,256]{1,0:T(8,128)(2,1)S(1)} %copy-done.10, f32[325]{0:T(512)S(1)} %copy-done.7, f32[325]{0:T(512)S(1)} %copy-done.8, f32[325]{0:T(512)S(1)} %copy-done.9, f32[53,650]{1,0:T(8,128)S(1)} %bitcast.13, ...), custom_call_target="tpu_custom_call" | custom-call | flops 2000000000 | bytes 16000000 | tf_op jit(solution)/shard_map/main/pallas_call | solution.py:397
  18.9 0.0 collective-permute-done.2.zl_ref
  18.9 0.0 collective-permute-done.3.zh_ref
  18.9 0.0 collective-permute-done.ha_ref
  18.9 0.0 collective-permute-done.1.hb_ref
  18.9 2.1 %inner_edges.1 = (f32[3456,128]{1,0:T(8,128)S(1)}, f32[3456,128]{1,0:T(8,128)}) custom-call(f32[3456,128]{1,0:T(8,128)S(1)} %main.1.part_ref, f32[54]{0:T(128)S(1)} %copy-done.2, f32[34,2,8,128]{3,2,1,0:T(8,128)S(1)} %collective-permute-done.ha_ref, f32[54,2,8,128]{3,2,1,0:T(8,128)S(1)} %collective-permute-done.1.hb_ref, ...), custom_call_target="tpu_custom_call", output_to_operand_aliasing={{0}: (0, {})} | custom-call | flops 1000000 | bytes 3000000 | tf_op jit(solution)/shard_map/inner_edges/pallas_call | solution.py:438
  21.1 0.0 collective-permute-done.4.ha_ref
  21.1 1.5 %outer_edges.1 = (f32[3456,128]{1,0:T(8,128)S(1)}, f32[3456,128]{1,0:T(8,128)}) custom-call(f32[3456,128]{1,0:T(8,128)S(1)} %get-tuple-element.17.part_ref, f32[54]{0:T(128)S(1)} %copy-done.2, f32[20,2,8,128]{3,2,1,0:T(8,128)S(1)} %collective-permute-done.4.ha_ref, f32[3456,128]{1,0:T(8,128)} %get-tuple-element.19.prev), custom_call_target="tpu_custom_call", output_to_operand_aliasing={{0}: (0, {}), {1}: (3, {})} | custom-call | flops 1000000 | bytes 3000000 | tf_op jit(solution)/shard_map/outer_edges/pallas_call | solution.py:449
Async XLA Ops:
  0.0 8.9 %copy-start.2 = (f32[54]{0:T(128)S(1)}, f32[54]{0:T(128)}, u32[]{:S(2)}) copy-start(f32[54]{0:T(128)} %d_ref.5) | copy-start | bytes 652
  0.0 1.5 %copy-start = (f32[54,8,1024]{2,1,0:T(8,128)S(1)}, f32[54,8,1024]{2,1,0:T(8,128)}, u32[]{:S(2)}) copy-start(f32[54,8,1024]{2,1,0:T(8,128)} %param.10) | copy-start | bytes 5308420
  1.5 7.4 %copy-start.1 = (f32[54,8,1024]{2,1,0:T(8,128)S(1)}, f32[54,8,1024]{2,1,0:T(8,128)}, u32[]{:S(2)}) copy-start(f32[54,8,1024]{2,1,0:T(8,128)} %param.10) | copy-start | bytes 5308420
  1.5 7.4 %copy-start.5 = (s32[8,8]{1,0:T(8,128)S(1)}, s32[8,8]{1,0:T(8,128)}, u32[]{:S(2)}) copy-start(s32[8,8]{1,0:T(8,128)} %sub_ref.1) | copy-start | bytes 772
  1.5 7.4 %copy-start.6 = (s32[8,8]{1,0:T(8,128)S(1)}, s32[8,8]{1,0:T(8,128)}, u32[]{:S(2)}) copy-start(s32[8,8]{1,0:T(8,128)} %flame_ref.1) | copy-start | bytes 772
  1.5 7.4 %copy-start.7 = (f32[325]{0:T(512)S(1)}, f32[325]{0:T(512)}, u32[]{:S(2)}) copy-start(f32[325]{0:T(512)} %lp_hbm.1) | copy-start | bytes 3904
  1.7 17.2 %collective-permute-start.1 = (f32[54,2,8,128]{3,2,1,0:T(8,128)S(1)}, f32[54,2,8,128]{3,2,1,0:T(8,128)S(1)}, u32[]{:S(2)}, u32[]{:S(2)}) collective-permute-start(f32[54,2,8,128]{3,2,1,0:T(8,128)S(1)} %get-tuple-element.14), channel_id=1, source_target_pairs={{0,4},{8,12},{16,20},{24,28},{4,0},{12,8},{20,16},{28,24},{1,5},{9... | collective-permute-start | bytes 1327112 | tf_op jit(solution)/shard_map/ppermute | solution.py:391
  2.5 16.5 %collective-permute-start = (f32[34,2,8,128]{3,2,1,0:T(8,128)S(1)}, f32[34,2,8,128]{3,2,1,0:T(8,128)S(1)}, u32[]{:S(2)}, u32[]{:S(2)}) collective-permute-start(f32[34,2,8,128]{3,2,1,0:T(8,128)S(1)} %get-tuple-element.13), channel_id=1, source_target_pairs={{4,8},{12,16},{20,24},{28,0},{8,4},{16,12},{24,20},{0,28},{5,9},{1... | collective-permute-start | bytes 835592 | tf_op jit(solution)/shard_map/ppermute | solution.py:389
  2.5 16.4 %collective-permute-start.2 = (f32[27,8,128]{2,1,0:T(8,128)S(1)}, f32[27,8,128]{2,1,0:T(8,128)S(1)}, u32[]{:S(2)}, u32[]{:S(2)}) collective-permute-start(f32[27,8,128]{2,1,0:T(8,128)S(1)} %get-tuple-element.15), channel_id=1, source_target_pairs={{0,1},{1,2},{2,3},{3,0},{4,5},{5,6},{6,7},{7,4},{8,9},{9,10},{10,1... | collective-permute-start | bytes 331784 | tf_op jit(solution)/shard_map/ppermute | solution.py:392
  3.9 15.0 %collective-permute-start.3 = (f32[27,8,128]{2,1,0:T(8,128)S(1)}, f32[27,8,128]{2,1,0:T(8,128)S(1)}, u32[]{:S(2)}, u32[]{:S(2)}) collective-permute-start(f32[27,8,128]{2,1,0:T(8,128)S(1)} %get-tuple-element.16), channel_id=1, source_target_pairs={{1,0},{2,1},{3,2},{0,3},{5,4},{6,5},{7,6},{4,7},{9,8},{10,9},{11,1... | collective-permute-start | bytes 331784 | tf_op jit(solution)/shard_map/ppermute | solution.py:393
  5.9 15.2 %collective-permute-start.4 = (f32[20,2,8,128]{3,2,1,0:T(8,128)S(1)}, f32[20,2,8,128]{3,2,1,0:T(8,128)S(1)}, u32[]{:S(2)}, u32[]{:S(2)}) collective-permute-start(f32[20,2,8,128]{3,2,1,0:T(8,128)S(1)} %get-tuple-element.18), channel_id=1, source_target_pairs={{4,8},{12,16},{20,24},{28,0},{8,4},{16,12},{24,20},{0,28},{5,9},{1... | collective-permute-start | bytes 491528 | tf_op jit(solution)/shard_map/ppermute | solution.py:390
  9.0 0.9 %copy-start.3 = (f32[650,53]{0,1:T(8,128)S(1)}, f32[650,53]{0,1:T(8,128)}, u32[]{:S(2)}) copy-start(f32[650,53]{0,1:T(8,128)} %param.15) | copy-start | bytes 413404
  9.9 0.9 %copy-start.4 = (f32[53,325]{1,0:T(8,128)S(1)}, f32[53,325]{1,0:T(8,128)}, u32[]{:S(2)}) copy-start(f32[53,325]{1,0:T(8,128)} %pr_hbm.1) | copy-start | bytes 206704
  10.8 0.7 %copy-start.8 = (f32[325]{0:T(512)S(1)}, f32[325]{0:T(512)}, u32[]{:S(2)}) copy-start(f32[325]{0:T(512)} %act_hbm.1) | copy-start | bytes 3904
  11.4 0.7 %copy-start.9 = (f32[325]{0:T(512)S(1)}, f32[325]{0:T(512)}, u32[]{:S(2)}) copy-start(f32[325]{0:T(512)} %heat_hbm.1) | copy-start | bytes 3904
  12.1 0.9 %copy-start.10 = (bf16[256,256]{1,0:T(8,128)(2,1)S(1)}, bf16[256,256]{1,0:T(8,128)(2,1)}, u32[]{:S(2)}) copy-start(bf16[256,256]{1,0:T(8,128)(2,1)} %constant.2.clone.shift_ref) | copy-start | bytes 393220
where the time goes:
time: 22.9 us; the launch traced here: 22.6 us
  Pallas kernels  9.71 us (42%)
  starting transfers between devices  7.21 us (31%)
  local copies, waits for them, and re-layouts  5.58 us (24%)
    pallas_call x1, Pallas kernels, per_device(): pl.pallas_call(functools.partial(main_kernel, comps, planes, tiles, nreac...  5.86 us
    unnamed x22, local copies, waits for them, and re-layouts  5.58 us
    ppermute x1, starting transfers between devices, per_device(): ha1 = lax.ppermute(a1, 'gx', outer)  2.98 us
    pallas_call x1, Pallas kernels, per_device(): pl.pallas_call(functools.partial(inner_edges_kernel, comps, planes, tiles...  2.15 us
    ppermute x1, starting transfers between devices, per_device(): zh = lax.ppermute(lo, 'gy', backward)  2.03 us
    pallas_call x1, Pallas kernels, per_device(): pl.pallas_call(functools.partial(outer_edges_kernel, comps, planes, tiles...  1.5 us
    ppermute x1, starting transfers between devices, per_device(): zl = lax.ppermute(hi, 'gy', forward)  1.46 us
    ppermute x1, starting transfers between devices, per_device(): hb = lax.ppermute(b, 'gx', inner)  0.74 us
  transfers between devices with their start and end apart: 5, of which 0 were waited for; matrix products, arithmetic and copies ran while one was open for 0% of the time, Pallas kernels for 35%

commit v1 on v0

--- a/solution.py
+++ b/solution.py
@@ -14,7 +14,6 @@
 far_weight = 1.0 / 12.0
 LOG2E = 1.4426950408889634
 GROUP = 4
-FIRST_CHUNK = 34
 PIECE = 64
 
 VMEM = pltpu.VMEM
@@ -25,39 +24,46 @@
     return pltpu.CompilerParams(vmem_limit_bytes=mib << 20)
 
 
-def high_side(parity_flip):
-    odd = lax.rem(lax.axis_index("gx"), 2)
-    return odd if not parity_flip else 1 - odd
-
-
-def pack_kernel(comps, planes, tiles, split, s_ref, a0_ref, a1_ref, b_ref, lo_ref, hi_ref):
+def odd_place(axis):
+    return lax.rem(lax.axis_index(axis), 2)
+
+
+def outer_kernel(comps, planes, tiles, s_hbm, o_ref, sem):
+    pair = odd_place("gx") * (planes // 2 - 1)
+    total = comps * tiles
+    parts = 6
+    copies = []
+    for i in range(parts):
+        begin, end = total * i // parts, total * (i + 1) // parts
+        where = pl.ds(begin, end - begin)
+        copies.append(
+            pltpu.make_async_copy(s_hbm.at[where, pair], o_ref.at[where], sem.at[i])
+        )
+        copies[-1].start()
+    for copy in copies:
+        copy.wait()
+
+
+def pack_kernel(comps, planes, tiles, s_ref, b_ref, first_ref, second_ref):
     rows = planes * tiles
-    far_side = high_side(False)
+    odd = odd_place("gy")
     lane = lax.broadcasted_iota(jnp.int32, (planes, LANES), 1)
-
-    def plane(c, x):
-        return s_ref[pl.ds(c * rows + x, tiles, stride=planes), :]
-
-    off_a = far_side * (planes - 2)
-    off_b = (1 - far_side) * (planes - 2)
+    off_b = (1 - odd_place("gx")) * (planes - 2)
     for c in range(comps):
         for p in range(2):
-            if c < split:
-                a0_ref[c, p] = plane(c, off_a + p)
-            else:
-                a1_ref[c - split, p] = plane(c, off_a + p)
-    for c in range(comps):
-        for p in range(2):
-            b_ref[c, p] = plane(c, off_b + p)
+            b_ref[c, p] = s_ref[pl.ds(c * rows + off_b + p, tiles, stride=planes), :]
+    swap = jnp.broadcast_to(odd, (planes, LANES)) == 1
+    last = (tiles - 1) * planes
     for k in range(comps // 2):
-        even, odd = 2 * k * rows, (2 * k + 1) * rows
-        last = (tiles - 1) * planes
-        first_even = s_ref[even : even + planes, :]
-        first_odd = s_ref[odd : odd + planes, :]
-        last_even = s_ref[even + last : even + last + planes, :]
-        last_odd = s_ref[odd + last : odd + last + planes, :]
-        lo_ref[k] = jnp.where(lane < 64, first_even, pltpu.roll(first_odd, 64, 1))
-        hi_ref[k] = jnp.where(lane < 64, pltpu.roll(last_even, 64, 1), last_odd)
+        first, second = 2 * k * rows, (2 * k + 1) * rows
+        low_a = s_ref[first : first + planes, :]
+        low_b = s_ref[second : second + planes, :]
+        high_a = s_ref[first + last : first + last + planes, :]
+        high_b = s_ref[second + last : second + last + planes, :]
+        low = jnp.where(lane < 64, low_a, pltpu.roll(low_b, 64, 1))
+        high = jnp.where(lane < 64, pltpu.roll(high_a, 64, 1), high_b)
+        first_ref[k] = jnp.where(swap, low, high)
+        second_ref[k] = jnp.where(swap, high, low)
 
 
 def split3(value):
@@ -253,74 +259,67 @@
         lax.fori_loop(0, (count + (GROUP - 1)) // GROUP, group, 0)
 
 
-def add_plane(planes, tiles, work, weight, c, h_ref, index, side):
-    rows = planes * tiles
-    near = h_ref[index, 1 - side]
-    far = h_ref[index, side]
-    first = pl.ds(c * rows + side * (planes - 1), tiles, stride=planes)
-    second = pl.ds(c * rows + 1 + side * (planes - 3), tiles, stride=planes)
-    work[first, :] = work[first, :] + weight * (near_weight * near - far_weight * far)
-    work[second, :] = work[second, :] - weight * (far_weight * near)
-
-
-def send_out(rows, begin, end, work, out_hbm, sem):
-    where = pl.ds(begin * rows, (end - begin) * rows)
-    copy = pltpu.make_async_copy(work.at[where, :], out_hbm.at[where, :], sem)
-    copy.start()
-    return copy
-
-
-def inner_edges_kernel(
-    comps, planes, tiles, split, part_ref, d_ref, ha_ref, hb_ref, zl_ref, zh_ref, work, out, sem
+def edge_kernel(
+    comps, planes, tiles, part_ref, d_ref, ha_ref, hb_ref, z1_ref, z2_ref, out, work, sem
 ):
     rows = planes * tiles
     lane = lax.broadcasted_iota(jnp.int32, (planes, LANES), 1)
-    side_a = high_side(False)
-    side_b = 1 - side_a
-    last = (tiles - 1) * planes
+    x = lax.broadcasted_iota(jnp.int32, (planes, LANES), 0)
+    side_a = odd_place("gx")
+    swap = jnp.broadcast_to(odd_place("gy"), (planes, LANES)) == 1
+    last = tiles - 1
+
+    def sided(side):
+        low = jnp.broadcast_to(side, (planes, LANES)) == 0
+        place = jnp.where(low, x, planes - 1 - x)
+        near = jnp.where(place == 0, near_weight, jnp.where(place == 1, -far_weight, 0.0))
+        far = jnp.where(place == 0, -far_weight, 0.0)
+        return near, far
+
+    near_a, far_a = sided(side_a)
+    near_b, far_b = sided(1 - side_a)
+    above = jnp.where(lane % 64 < NZ, near_weight, 0.0)
+    below = jnp.where(lane % 64 >= NZ, near_weight, 0.0)
     copies = []
     done = 0
     for k in range(comps // 2):
-        low = zl_ref[k]
-        high = zh_ref[k]
-        low = near_weight * jnp.where(lane % 64 < NZ, pltpu.roll(low, LANES - NZ, 1), 0.0) - (
-            far_weight * low
-        )
-        high = near_weight * jnp.where(lane % 64 >= NZ, pltpu.roll(high, NZ, 1), 0.0) - (
-            far_weight * high
-        )
-        other_low = pltpu.roll(low, 64, 1)
-        other_high = pltpu.roll(high, 64, 1)
+        one, two = z1_ref[k], z2_ref[k]
+        low = jnp.where(swap, one, two)
+        high = jnp.where(swap, two, one)
+        low = pltpu.roll(low, LANES - NZ, 1) * above - far_weight * low
+        high = pltpu.roll(high, NZ, 1) * below - far_weight * high
+        lows = (low, pltpu.roll(low, 64, 1))
+        highs = (pltpu.roll(high, 64, 1), high)
         for j in range(2):
             c = 2 * k + j
             weight = d_ref[c]
-            mine_low = low if j == 0 else other_low
-            mine_high = high if j == 1 else other_high
-            top = slice(c * rows, c * rows + planes)
-            work[top, :] = work[top, :] + jnp.where(lane < 64, weight * mine_low, 0.0)
-            end = slice(c * rows + last, c * rows + last + planes)
-            work[end, :] = work[end, :] + jnp.where(lane >= 64, weight * mine_high, 0.0)
-            add_plane(planes, tiles, work, weight, c, hb_ref, c, side_b)
-            if c < split:
-                add_plane(planes, tiles, work, weight, c, ha_ref, c, side_a)
+            na, fa = near_a * weight, far_a * weight
+            nb, fb = near_b * weight, far_b * weight
+            for t in range(tiles):
+                where = slice(c * rows + t * planes, c * rows + (t + 1) * planes)
+
+                def row(ref, start):
+                    return ref[pl.ds(start, planes, stride=0), :]
+
+                base_a = (c * tiles + t) * 2
+                base_b = c * 2 * tiles + t
+                value = part_ref[where, :]
+                value = value + row(ha_ref, base_a + 1 - side_a) * na
+                value = value + row(ha_ref, base_a + side_a) * fa
+                value = value + row(hb_ref, base_b + side_a * tiles) * nb
+                value = value + row(hb_ref, base_b + (1 - side_a) * tiles) * fb
+                if t == 0:
+                    value = value + jnp.where(lane < 64, weight * lows[j], 0.0)
+                if t == last:
+                    value = value + jnp.where(lane >= 64, weight * highs[j], 0.0)
+                work[where, :] = value
         now = 2 * k + 2
-        if now <= split and (now - done >= 10 or now == split):
-            copies.append(send_out(rows, done, now, work, out, sem.at[len(copies)]))
-            done = now
-    for copy in copies:
-        copy.wait()
-
-
-def outer_edges_kernel(comps, planes, tiles, split, part_ref, d_ref, ha_ref, prev, work, out, sem):
-    rows = planes * tiles
-    side = high_side(False)
-    copies = []
-    done = split
-    for c in range(split, comps):
-        add_plane(planes, tiles, work, d_ref[c], c, ha_ref, c - split, side)
-        now = c + 1
-        if now - done >= 5 or now == comps:
-            copies.append(send_out(rows, done, now, work, out, sem.at[len(copies)]))
+        if now - done >= 8 or now == comps:
+            where = pl.ds(done * rows, (now - done) * rows)
+            copies.append(
+                pltpu.make_async_copy(work.at[where, :], out.at[where, :], sem.at[len(copies)])
+            )
+            copies[-1].start()
             done = now
     for copy in copies:
         copy.wait()
@@ -352,7 +351,6 @@
     tiles = cells // LANES
     rows = planes * tiles
     nreact = log_prefactor.shape[0]
-    split = FIRST_CHUNK
     gx, gy = lax.axis_size("gx"), lax.axis_size("gy")
     f32 = jnp.float32
     flat = (
@@ -364,18 +362,30 @@
     smem = pl.BlockSpec(memory_space=SMEM)
     anywhere = pl.BlockSpec(memory_space=pl.ANY)
 
+    hbm = pl.BlockSpec(memory_space=pltpu.HBM)
     sds = jax.ShapeDtypeStruct
-    a0, a1, b, lo, hi = pl.pallas_call(
-        functools.partial(pack_kernel, comps, planes, tiles, split),
+    a = pl.pallas_call(
+        functools.partial(outer_kernel, comps, planes, tiles),
+        out_shape=sds((comps * tiles, 2, LANES), f32),
+        in_specs=[hbm],
+        out_specs=vmem,
+        scratch_shapes=[pltpu.SemaphoreType.DMA((6,))],
+        compiler_params=params(8),
+        name="outer_planes",
+    )(
+        pltpu.with_memory_space_constraint(
+            flat.reshape(comps * tiles, planes // 2, 2, LANES), pltpu.HBM
+        )
+    )
+    b, first, second = pl.pallas_call(
+        functools.partial(pack_kernel, comps, planes, tiles),
         out_shape=(
-            sds((split, 2, tiles, LANES), f32),
-            sds((comps - split, 2, tiles, LANES), f32),
             sds((comps, 2, tiles, LANES), f32),
             sds((comps // 2, planes, LANES), f32),
             sds((comps // 2, planes, LANES), f32),
         ),
         in_specs=[vmem],
-        out_specs=[vmem] * 5,
+        out_specs=[vmem] * 3,
         compiler_params=params(16),
         name="pack",
     )(flat)
@@ -384,20 +394,21 @@
     outer = outer + [(t, s) for s, t in outer]
     inner = [(i, i + 1) for i in range(0, gx, 2)]
     inner = inner + [(t, s) for s, t in inner]
-    forward = [(i, (i + 1) % gy) for i in range(gy)]
-    backward = [(t, s) for s, t in forward]
-    ha0 = lax.ppermute(a0, "gx", outer)
-    ha1 = lax.ppermute(a1, "gx", outer)
+    along_a = [(i, i + 1) for i in range(0, gy, 2)]
+    along_a = along_a + [(t, s) for s, t in along_a]
+    along_b = [(i, (i + 1) % gy) for i in range(1, gy, 2)]
+    along_b = along_b + [(t, s) for s, t in along_b]
+    ha = lax.ppermute(a, "gx", outer)
     hb = lax.ppermute(b, "gx", inner)
-    zl = lax.ppermute(hi, "gy", forward)
-    zh = lax.ppermute(lo, "gy", backward)
+    z1 = lax.ppermute(first, "gy", along_a)
+    z2 = lax.ppermute(second, "gy", along_b)
 
     padded = pl.cdiv(nreact, LANES) * LANES
     wide = pl.cdiv(nreact, 16) * 16
     part = pl.pallas_call(
         functools.partial(main_kernel, comps, planes, tiles, nreact),
         out_shape=sds((comps * rows, LANES), f32),
-        in_specs=[vmem, smem, vmem] + [anywhere] * 5 + [smem, smem],
+        in_specs=[vmem, smem, vmem] + [hbm] * 5 + [smem, smem],
         out_specs=vmem,
         scratch_shapes=[
             VMEM((nreact,), f32),
@@ -433,30 +444,25 @@
         flame,
     )
 
-    whole = sds((comps * rows, LANES), f32)
-    cost = pl.CostEstimate(flops=1_000_000, bytes_accessed=3_000_000, transcendentals=0)
-    part, out = pl.pallas_call(
-        functools.partial(inner_edges_kernel, comps, planes, tiles, split),
-        out_shape=(whole, whole),
+    out = pl.pallas_call(
+        functools.partial(edge_kernel, comps, planes, tiles),
+        out_shape=sds((comps * rows, LANES), f32),
         in_specs=[vmem, smem, vmem, vmem, vmem, vmem],
-        out_specs=(vmem, anywhere),
-        scratch_shapes=[pltpu.SemaphoreType.DMA((8,))],
-        input_output_aliases={0: 0},
+        out_specs=anywhere,
+        scratch_shapes=[VMEM((comps * rows, LANES), f32), pltpu.SemaphoreType.DMA((8,))],
         compiler_params=params(16),
-        cost_estimate=cost,
-        name="inner_edges",
-    )(part, diffusivity, ha0, hb, zl, zh)
-    part, out = pl.pallas_call(
-        functools.partial(outer_edges_kernel, comps, planes, tiles, split),
-        out_shape=(whole, whole),
-        in_specs=[vmem, smem, vmem, anywhere],
-        out_specs=(vmem, anywhere),
-        scratch_shapes=[pltpu.SemaphoreType.DMA((8,))],
-        input_output_aliases={0: 0, 3: 1},
-        compiler_params=params(16),
-        cost_estimate=cost,
-        name="outer_edges",
-    )(part, diffusivity, ha1, out)
+        cost_estimate=pl.CostEstimate(
+            flops=1_000_000, bytes_accessed=3_000_000, transcendentals=0
+        ),
+        name="edges",
+    )(
+        part,
+        diffusivity,
+        ha.reshape(comps * tiles * 2, LANES),
+        hb.reshape(comps * 2 * tiles, LANES),
+        z1,
+        z2,
+    )
     return (
         out.reshape(comps, tiles, planes, LANES).transpose(0, 2, 1, 3).reshape(comps, planes, cells)
     )

time: 22.9 us -> 17.5 us (0.76)
  the two profiles are of different devices: /device:TPU:7 before, /device:TPU:0 now
where the time goes in v1:
time: 17.5 us; the launch traced here: 17.4 us
  Pallas kernels  8.18 us (47%)
  starting transfers between devices  7.63 us (44%)
  waiting for transfers between devices  1.41 us (8%)
    pallas_call x1, Pallas kernels, per_device(): pl.pallas_call(functools.partial(main_kernel, comps, planes, tiles, nreac...  4.36 us
    ppermute x1, starting transfers between devices, per_device(): ha = lax.ppermute(a, 'gx', outer)  3.44 us
    ppermute x1, starting transfers between devices, per_device(): z2 = lax.ppermute(second, 'gy', along_b)  2.47 us
    pallas_call x1, Pallas kernels, per_device(): pl.pallas_call(functools.partial(edge_kernel, comps, planes, tiles), out_...  2.43 us
    ppermute x1, starting transfers between devices, per_device(): z1 = lax.ppermute(first, 'gy', along_a)  1.64 us
    ppermute x1, waiting for transfers between devices, per_device(): z2 = lax.ppermute(second, 'gy', along_b)  1.4 us
    pallas_call x1, Pallas kernels, per_device(): pl.pallas_call(functools.partial(outer_kernel, comps, planes, tiles), out...  1.27 us
  transfers between devices with their start and end apart: 4, of which 1 were waited for; matrix products, arithmetic and copies ran while one was open for 0% of the time, Pallas kernels for 26%

profile of v1, /device:TPU:0, one launch (start us, length us, event | category | flops | bytes accessed | tf_op | source)
XLA Modules:
  0.0 17.4 jit_solution(8973067692486998693)
XLA Ops:
  0.0 0.0 copy-start
  0.0 0.0 copy-start.1
  0.0 0.0 copy-start.2
  0.0 0.0 copy-start.3
  0.0 0.0 copy-start.4
  0.0 0.0 copy-start.5
  0.0 0.0 copy-start.6
  0.0 0.0 copy-start.7
  0.0 0.0 copy-start.8
  0.1 0.0 copy-start.9
  0.1 1.3 %outer_planes.1 = f32[432,2,128]{2,1,0:T(2,128)S(1)} custom-call(f32[432,4,2,128]{3,2,1,0:T(2,128)} %bitcast.15), custom_call_target="tpu_custom_call" | custom-call | tf_op jit(solution)/shard_map/outer_planes/pallas_call | solution.py:367
  1.3 3.4 %collective-permute-start = (f32[432,2,128]{2,1,0:T(2,128)S(1)}, f32[432,2,128]{2,1,0:T(2,128)S(1)}, u32[]{:S(2)}, u32[]{:S(2)}) collective-permute-start(f32[432,2,128]{2,1,0:T(2,128)S(1)} %outer_planes.1), channel_id=1, source_target_pairs={{4,8},{12,16},{20,24},{28,0},{8,4},{16,12},{24,20},{0,28},{5,9},{1... | collective-permute-start | bytes 1327112 | tf_op jit(solution)/shard_map/ppermute | solution.py:401
  4.8 0.0 copy-done
  4.8 0.1 pack.1
  4.9 0.1 collective-permute-start.1
  5.0 1.6 %collective-permute-start.2 = (f32[27,8,128]{2,1,0:T(8,128)S(1)}, f32[27,8,128]{2,1,0:T(8,128)S(1)}, u32[]{:S(2)}, u32[]{:S(2)}) collective-permute-start(f32[27,8,128]{2,1,0:T(8,128)S(1)} %get-tuple-element.9), channel_id=1, source_target_pairs={{0,1},{2,3},{1,0},{3,2},{4,5},{6,7},{5,4},{7,6},{8,9},{10,11},{9,8... | collective-permute-start | bytes 331784 | tf_op jit(solution)/shard_map/ppermute | solution.py:403
  6.6 2.5 %collective-permute-start.3 = (f32[27,8,128]{2,1,0:T(8,128)S(1)}, f32[27,8,128]{2,1,0:T(8,128)S(1)}, u32[]{:S(2)}, u32[]{:S(2)}) collective-permute-start(f32[27,8,128]{2,1,0:T(8,128)S(1)} %get-tuple-element.10), channel_id=1, source_target_pairs={{1,2},{3,0},{2,1},{0,3},{5,6},{7,4},{6,5},{4,7},{9,10},{11,8},{10,... | collective-permute-start | bytes 331784 | tf_op jit(solution)/shard_map/ppermute | solution.py:404
  9.1 0.0 copy-done.1
  9.1 0.0 copy-done.2
  9.1 0.0 copy-done.3
  9.1 0.0 copy-done.4
  9.1 0.0 copy-done.5
  9.1 0.0 copy-done.6
  9.1 0.0 copy-done.7
  9.2 0.0 copy-done.8
  9.2 0.0 copy-done.9
  9.2 4.4 %main.1.part_ref = f32[3456,128]{1,0:T(8,128)S(1)} custom-call(f32[3456,128]{1,0:T(8,128)S(1)} %bitcast.17, f32[54]{0:T(128)S(1)} %copy-done.1, bf16[256,256]{1,0:T(8,128)(2,1)S(1)} %copy-done.9, f32[325]{0:T(512)S(1)} %copy-done.6, f32[325]{0:T(512)S(1)} %copy-done.7, f32[325]{0:T(512)S(1)} %copy-done.8, f32[53,650]{1,0:T(8,128)S(1)} %bitcast.20, ...), custom_call_target="tpu_custom_call" | custom-call | flops 2000000000 | bytes 16000000 | tf_op jit(solution)/shard_map/main/pallas_call | solution.py:408
  13.5 0.0 collective-permute-done.2.z1_ref
  13.5 1.4 %collective-permute-done.3.z2_ref = f32[27,8,128]{2,1,0:T(8,128)S(1)} collective-permute-done((f32[27,8,128]{2,1,0:T(8,128)S(1)}, f32[27,8,128]{2,1,0:T(8,128)S(1)}, u32[]{:S(2)}, u32[]{:S(2)}) %collective-permute-start.3) | collective-permute-done | bytes 110624 | tf_op jit(solution)/shard_map/ppermute | solution.py:404
  14.9 0.0 collective-permute-done
  15.0 0.0 collective-permute-done.1
  15.0 2.4 %edges.1 = f32[3456,128]{1,0:T(8,128)} custom-call(f32[3456,128]{1,0:T(8,128)S(1)} %main.1.part_ref, f32[54]{0:T(128)S(1)} %copy-done.1, f32[864,128]{1,0:T(8,128)S(1)} %bitcast.18, f32[864,128]{1,0:T(8,128)S(1)} %bitcast.19, f32[27,8,128]{2,1,0:T(8,128)S(1)} %collective-permute-done.2.z1_ref, f32[27,8,128]{2,1,0:T(8,128)S(1)} %collective-permute-done.3.z2_ref), custom_call_target="tpu_custom_call" | custom-call | flops 1000000 | bytes 3000000 | tf_op jit(solution)/shard_map/edges/pallas_call | solution.py:447
Async XLA Ops:
  0.0 4.8 %copy-start = (f32[54,8,1024]{2,1,0:T(8,128)S(1)}, f32[54,8,1024]{2,1,0:T(8,128)}, u32[]{:S(2)}) copy-start(f32[54,8,1024]{2,1,0:T(8,128)} %param.10) | copy-start | bytes 5308420
  0.0 9.1 %copy-start.1 = (f32[54]{0:T(128)S(1)}, f32[54]{0:T(128)}, u32[]{:S(2)}) copy-start(f32[54]{0:T(128)} %d_ref.3) | copy-start | bytes 652
  0.0 9.1 %copy-start.2 = (f32[650,53]{0,1:T(8,128)S(1)}, f32[650,53]{0,1:T(8,128)}, u32[]{:S(2)}) copy-start(f32[650,53]{0,1:T(8,128)} %param.15) | copy-start | bytes 413404
  0.0 9.1 %copy-start.3 = (f32[53,325]{1,0:T(8,128)S(1)}, f32[53,325]{1,0:T(8,128)}, u32[]{:S(2)}) copy-start(f32[53,325]{1,0:T(8,128)} %pr_hbm.1) | copy-start | bytes 206704
  0.0 9.1 %copy-start.4 = (s32[8,8]{1,0:T(8,128)S(1)}, s32[8,8]{1,0:T(8,128)}, u32[]{:S(2)}) copy-start(s32[8,8]{1,0:T(8,128)} %sub_ref.1) | copy-start | bytes 772
  0.0 9.1 %copy-start.5 = (s32[8,8]{1,0:T(8,128)S(1)}, s32[8,8]{1,0:T(8,128)}, u32[]{:S(2)}) copy-start(s32[8,8]{1,0:T(8,128)} %flame_ref.1) | copy-start | bytes 772
  0.0 9.1 %copy-start.6 = (f32[325]{0:T(512)S(1)}, f32[325]{0:T(512)}, u32[]{:S(2)}) copy-start(f32[325]{0:T(512)} %lp_hbm.1) | copy-start | bytes 3904
  0.0 9.1 %copy-start.7 = (f32[325]{0:T(512)S(1)}, f32[325]{0:T(512)}, u32[]{:S(2)}) copy-start(f32[325]{0:T(512)} %act_hbm.1) | copy-start | bytes 3904
  0.0 9.1 %copy-start.8 = (f32[325]{0:T(512)S(1)}, f32[325]{0:T(512)}, u32[]{:S(2)}) copy-start(f32[325]{0:T(512)} %heat_hbm.1) | copy-start | bytes 3904
  0.1 9.1 %copy-start.9 = (bf16[256,256]{1,0:T(8,128)(2,1)S(1)}, bf16[256,256]{1,0:T(8,128)(2,1)}, u32[]{:S(2)}) copy-start(bf16[256,256]{1,0:T(8,128)(2,1)} %constant.2.clone.shift_ref) | copy-start | bytes 393220
  1.3 13.6 %collective-permute-start = (f32[432,2,128]{2,1,0:T(2,128)S(1)}, f32[432,2,128]{2,1,0:T(2,128)S(1)}, u32[]{:S(2)}, u32[]{:S(2)}) collective-permute-start(f32[432,2,128]{2,1,0:T(2,128)S(1)} %outer_planes.1), channel_id=1, source_target_pairs={{4,8},{12,16},{20,24},{28,0},{8,4},{16,12},{24,20},{0,28},{5,9},{1... | collective-permute-start | bytes 1327112 | tf_op jit(solution)/shard_map/ppermute | solution.py:401
  4.9 10.0 %collective-permute-start.1 = (f32[54,2,8,128]{3,2,1,0:T(8,128)S(1)}, f32[54,2,8,128]{3,2,1,0:T(8,128)S(1)}, u32[]{:S(2)}, u32[]{:S(2)}) collective-permute-start(f32[54,2,8,128]{3,2,1,0:T(8,128)S(1)} %get-tuple-element.8), channel_id=1, source_target_pairs={{0,4},{8,12},{16,20},{24,28},{4,0},{12,8},{20,16},{28,24},{1,5},{9... | collective-permute-start | bytes 1327112 | tf_op jit(solution)/shard_map/ppermute | solution.py:402
  5.0 8.5 %collective-permute-start.2 = (f32[27,8,128]{2,1,0:T(8,128)S(1)}, f32[27,8,128]{2,1,0:T(8,128)S(1)}, u32[]{:S(2)}, u32[]{:S(2)}) collective-permute-start(f32[27,8,128]{2,1,0:T(8,128)S(1)} %get-tuple-element.9), channel_id=1, source_target_pairs={{0,1},{2,3},{1,0},{3,2},{4,5},{6,7},{5,4},{7,6},{8,9},{10,11},{9,8... | collective-permute-start | bytes 331784 | tf_op jit(solution)/shard_map/ppermute | solution.py:403
  6.6 8.3 %collective-permute-start.3 = (f32[27,8,128]{2,1,0:T(8,128)S(1)}, f32[27,8,128]{2,1,0:T(8,128)S(1)}, u32[]{:S(2)}, u32[]{:S(2)}) collective-permute-start(f32[27,8,128]{2,1,0:T(8,128)S(1)} %get-tuple-element.10), channel_id=1, source_target_pairs={{1,2},{3,0},{2,1},{0,3},{5,6},{7,4},{6,5},{4,7},{9,10},{11,8},{10,... | collective-permute-start | bytes 331784 | tf_op jit(solution)/shard_map/ppermute | solution.py:404

commit v2 on v1

--- a/solution.py
+++ b/solution.py
@@ -2,7 +2,6 @@
 
 import jax
 import jax.numpy as jnp
-import numpy as np
 from jax import lax
 from jax.experimental import pallas as pl
 from jax.experimental.pallas import tpu as pltpu
@@ -16,6 +15,7 @@
 GROUP = 4
 PIECE = 64
 
+
 VMEM = pltpu.VMEM
 SMEM = pltpu.SMEM
 
@@ -28,30 +28,38 @@
     return lax.rem(lax.axis_index(axis), 2)
 
 
-def outer_kernel(comps, planes, tiles, s_hbm, o_ref, sem):
+def ahead_kernel(comps, planes, tiles, s_hbm, o_ref, sem):
     pair = odd_place("gx") * (planes // 2 - 1)
     total = comps * tiles
-    parts = 6
+    parts = sem.shape[0]
     copies = []
     for i in range(parts):
         begin, end = total * i // parts, total * (i + 1) // parts
         where = pl.ds(begin, end - begin)
-        copies.append(
-            pltpu.make_async_copy(s_hbm.at[where, pair], o_ref.at[where], sem.at[i])
-        )
+        copies.append(pltpu.make_async_copy(s_hbm.at[where, pair], o_ref.at[where], sem.at[i]))
         copies[-1].start()
     for copy in copies:
         copy.wait()
 
 
-def pack_kernel(comps, planes, tiles, s_ref, b_ref, first_ref, second_ref):
+def pack_kernel(comps, planes, tiles, cuts, s_ref, *out_refs):
+    a_refs, (b_ref, first_ref, second_ref) = out_refs[:-3], out_refs[-3:]
     rows = planes * tiles
     odd = odd_place("gy")
     lane = lax.broadcasted_iota(jnp.int32, (planes, LANES), 1)
-    off_b = (1 - odd_place("gx")) * (planes - 2)
+    off_a = odd_place("gx") * (planes - 2)
+    off_b = (planes - 2) - off_a
+
+    def plane(c, x):
+        return s_ref[pl.ds(c * rows + x, tiles, stride=planes), :]
+
+    for a_ref, begin, end in zip(a_refs, cuts, cuts[1:]):
+        for c in range(begin, end):
+            for p in range(2):
+                a_ref[c - begin, p] = plane(c, off_a + p)
     for c in range(comps):
         for p in range(2):
-            b_ref[c, p] = s_ref[pl.ds(c * rows + off_b + p, tiles, stride=planes), :]
+            b_ref[c, p] = plane(c, off_b + p)
     swap = jnp.broadcast_to(odd, (planes, LANES)) == 1
     last = (tiles - 1) * planes
     for k in range(comps // 2):
@@ -74,6 +82,31 @@
     return high, middle, low
 
 
+def shift_matrix():
+    shape = (LANES, LANES)
+    source = lax.broadcasted_iota(jnp.int32, shape, 0)
+    target = lax.broadcasted_iota(jnp.int32, shape, 1)
+    rows = LANES // NZ
+    ys, yt = source // NZ, target // NZ
+    turn = (target - source) & (NZ - 1)
+    same_z = turn == 0
+
+    def weight(distance):
+        return jnp.where(distance == 1, 16.0, jnp.where(distance == 2, -1.0, 0.0))
+
+    turn = jnp.minimum(turn, NZ - turn)
+    along_z = jnp.where(same_z, -90.0, weight(turn))
+    own = jnp.where(ys == yt, along_z, jnp.where(same_z, weight(jnp.abs(yt - ys)), 0.0))
+    apart = jnp.where(target < LANES // 2, yt + rows - ys, ys + rows - yt)
+    cross = jnp.where(same_z, weight(apart), 0.0)
+    one = jnp.concatenate([own, cross], 1).astype(jnp.bfloat16)
+    return jnp.concatenate([one, one], 0)
+
+
+def many_of(comps):
+    return max(n for n in range(1, 7) if comps % n == 0)
+
+
 def main_kernel(
     comps,
     planes,
@@ -81,7 +114,6 @@
     nreact,
     s_ref,
     d_ref,
-    shift_ref,
     lp_hbm,
     act_hbm,
     heat_hbm,
@@ -102,6 +134,9 @@
     a_ref,
     t_ref,
     st_ref,
+    shift_ref,
+    even_ref,
+    odd_ref,
     pos_ref,
     sem,
 ):
@@ -123,46 +158,77 @@
     for load in loads:
         load.start()
 
+    shift_ref[...] = shift_matrix()
+
     count = jnp.int32(0)
     for x in range(planes):
         for b in range(tiles):
             pos_ref[count] = b * planes + x
             count = count + flame_ref[x, b]
 
-    many = max(n for n in range(1, 7) if comps % n == 0)
+    many = many_of(comps)
+    size = many * rows
+    groups = comps // many
     shape = (many, tiles, planes, LANES)
     lane = lax.broadcasted_iota(jnp.int32, (1, 1, planes, LANES), 3)
     x = lax.broadcasted_iota(jnp.int32, (1, 1, planes, LANES), 2)
     zero = jnp.zeros((many, 1, planes, LANES), jnp.float32)
     near, far = near_weight * 12.0, -far_weight * 12.0
-    up1 = jnp.where(x > 0, near, 0.0)
-    down1 = jnp.where(x < planes - 1, near, 0.0)
-    up2 = jnp.where(x > 1, far, 0.0)
-    down2 = jnp.where(x < planes - 2, far, 0.0)
-    shifts = shift_ref[...]
-
-    def components(i, carry):
-        start = pl.multiple_of(i * many * rows, many * rows)
-        flat = s_ref[pl.ds(start, many * rows), :]
+    weights = {
+        -1: jnp.where(x > 0, near, 0.0),
+        1: jnp.where(x < planes - 1, near, 0.0),
+        -2: jnp.where(x > 1, far, 0.0),
+        2: jnp.where(x < planes - 2, far, 0.0),
+    }
+
+    def product(i, buffer):
+        flat = s_ref[pl.ds(pl.multiple_of(i * size, size), size), :]
         high = flat.astype(jnp.bfloat16)
         low = (flat - high.astype(jnp.float32)).astype(jnp.bfloat16)
         both = jnp.concatenate([high, low], 1)
-        out = jnp.dot(both, shifts, preferred_element_type=jnp.float32)
-        v = flat.reshape(shape)
-        own = out[:, :LANES].reshape(shape)
-        cross = out[:, LANES:].reshape(shape)
+        buffer[...] = jnp.dot(both, shift_ref[...], preferred_element_type=jnp.float32)
+
+    def combine(i, buffer, inside):
+        start = pl.multiple_of(i * size, size)
+        v = s_ref[pl.ds(start, size), :].reshape(shape)
+        own = buffer[:, :LANES].reshape(shape)
+        cross = buffer[:, LANES:].reshape(shape)
         before = jnp.concatenate([zero, cross[:, :-1]], 1)
         after = jnp.concatenate([cross[:, 1:], zero], 1)
         own = own + jnp.where(lane < 64, before, after)
-        own = own + (pltpu.roll(v, 1, 2) * up1 + pltpu.roll(v, planes - 1, 2) * down1)
-        own = own + (pltpu.roll(v, 2, 2) * up2 + pltpu.roll(v, planes - 2, 2) * down2)
+        for offset, weight in weights.items():
+            if inside:
+                moved = s_ref[pl.ds(start + offset, size), :].reshape(shape)
+            else:
+                moved = pltpu.roll(v, (-offset) % planes, 2)
+            own = own + moved * weight
         for j in range(many):
             where = pl.ds(pl.multiple_of(start + j * rows, rows), rows)
             scale = d_ref[i * many + j] * (1.0 / 12.0)
             o_ref[where, :] = (v[j] + scale * own[j]).reshape(rows, LANES)
-        return carry
-
-    lax.fori_loop(0, comps // many, components, 0)
+
+    product(0, even_ref)
+    if groups % 2 == 1 and groups > 2:
+        product(1, odd_ref)
+        combine(0, even_ref, False)
+
+        def two(i, carry):
+            g = 2 * i + 1
+            product(g + 1, even_ref)
+            combine(g, odd_ref, True)
+            product(g + 2, odd_ref)
+            combine(g + 1, even_ref, True)
+            return carry
+
+        lax.fori_loop(0, (groups - 3) // 2, two, 0)
+        product(groups - 1, even_ref)
+        combine(groups - 2, odd_ref, True)
+        combine(groups - 1, even_ref, False)
+    else:
+        for i in range(groups):
+            combine(i, even_ref, False)
+            if i < groups - 1:
+                product(i + 1, even_ref)
     for load in loads:
         load.wait()
 
@@ -259,89 +325,86 @@
         lax.fori_loop(0, (count + (GROUP - 1)) // GROUP, group, 0)
 
 
-def edge_kernel(
-    comps, planes, tiles, part_ref, d_ref, ha_ref, hb_ref, z1_ref, z2_ref, out, work, sem
-):
+def add_planes(planes, tiles, work, d_ref, plane, begin, end, side):
+    rows = planes * tiles
+    for c in range(begin, end):
+        near = plane(c, 1 - side)
+        far = plane(c, side)
+        weight = d_ref[c]
+        first = pl.ds(c * rows + side * (planes - 1), tiles, stride=planes)
+        second = pl.ds(c * rows + 1 + side * (planes - 3), tiles, stride=planes)
+        one, two = work[first, :], work[second, :]
+        work[first, :] = one + weight * (near_weight * near - far_weight * far)
+        work[second, :] = two - (weight * far_weight) * near
+
+
+def inner_edges_kernel(comps, planes, tiles, part_ref, d_ref, hb_ref, z1_ref, z2_ref, work):
+    del part_ref
     rows = planes * tiles
     lane = lax.broadcasted_iota(jnp.int32, (planes, LANES), 1)
-    x = lax.broadcasted_iota(jnp.int32, (planes, LANES), 0)
-    side_a = odd_place("gx")
     swap = jnp.broadcast_to(odd_place("gy"), (planes, LANES)) == 1
-    last = tiles - 1
-
-    def sided(side):
-        low = jnp.broadcast_to(side, (planes, LANES)) == 0
-        place = jnp.where(low, x, planes - 1 - x)
-        near = jnp.where(place == 0, near_weight, jnp.where(place == 1, -far_weight, 0.0))
-        far = jnp.where(place == 0, -far_weight, 0.0)
-        return near, far
-
-    near_a, far_a = sided(side_a)
-    near_b, far_b = sided(1 - side_a)
+    last = (tiles - 1) * planes
     above = jnp.where(lane % 64 < NZ, near_weight, 0.0)
     below = jnp.where(lane % 64 >= NZ, near_weight, 0.0)
-    copies = []
-    done = 0
-    for k in range(comps // 2):
+    lower = jnp.where(lane < 64, 1.0, 0.0)
+    upper = jnp.where(lane < 64, 0.0, 1.0)
+
+    def pair(k, carry):
         one, two = z1_ref[k], z2_ref[k]
         low = jnp.where(swap, one, two)
         high = jnp.where(swap, two, one)
         low = pltpu.roll(low, LANES - NZ, 1) * above - far_weight * low
         high = pltpu.roll(high, NZ, 1) * below - far_weight * high
-        lows = (low, pltpu.roll(low, 64, 1))
-        highs = (pltpu.roll(high, 64, 1), high)
+        lows = (low * lower, pltpu.roll(low * upper, 64, 1))
+        highs = (pltpu.roll(high * lower, 64, 1), high * upper)
         for j in range(2):
-            c = 2 * k + j
-            weight = d_ref[c]
-            na, fa = near_a * weight, far_a * weight
-            nb, fb = near_b * weight, far_b * weight
-            for t in range(tiles):
-                where = slice(c * rows + t * planes, c * rows + (t + 1) * planes)
-
-                def row(ref, start):
-                    return ref[pl.ds(start, planes, stride=0), :]
-
-                base_a = (c * tiles + t) * 2
-                base_b = c * 2 * tiles + t
-                value = part_ref[where, :]
-                value = value + row(ha_ref, base_a + 1 - side_a) * na
-                value = value + row(ha_ref, base_a + side_a) * fa
-                value = value + row(hb_ref, base_b + side_a * tiles) * nb
-                value = value + row(hb_ref, base_b + (1 - side_a) * tiles) * fb
-                if t == 0:
-                    value = value + jnp.where(lane < 64, weight * lows[j], 0.0)
-                if t == last:
-                    value = value + jnp.where(lane >= 64, weight * highs[j], 0.0)
-                work[where, :] = value
-        now = 2 * k + 2
-        if now - done >= 8 or now == comps:
-            where = pl.ds(done * rows, (now - done) * rows)
-            copies.append(
-                pltpu.make_async_copy(work.at[where, :], out.at[where, :], sem.at[len(copies)])
+            weight = d_ref[2 * k + j]
+            base = pl.multiple_of((2 * k + j) * rows, planes)
+            top = pl.ds(base, planes)
+            end = pl.ds(pl.multiple_of(base + last, planes), planes)
+            work[top, :] = work[top, :] + weight * lows[j]
+            work[end, :] = work[end, :] + weight * highs[j]
+        return carry
+
+    for k in range(comps // 2):
+        pair(k, 0)
+    odd = odd_place("gx")
+    for side in range(2):
+
+        @pl.when(odd == 1 - side)
+        def _(side=side):
+            add_planes(
+                planes, tiles, work, d_ref, lambda c, p: hb_ref[c, p], 0, comps, side
             )
-            copies[-1].start()
-            done = now
-    for copy in copies:
-        copy.wait()
-
-
-def shift_matrix():
-    source = np.arange(LANES)[:, None]
-    target = np.arange(LANES)[None, :]
-    weights = {1: 16.0, 2: -1.0}
-    ys, yt, zs, zt = source // NZ, target // NZ, source % NZ, target % NZ
-    rows = LANES // NZ
-    own = np.where(source == target, -90.0, 0.0)
-    cross = np.zeros_like(own)
-    for distance, weight in weights.items():
-        turn = (zt - zs) % NZ
-        own += np.where((ys == yt) & ((turn == distance) | (turn == NZ - distance)), weight, 0.0)
-        own += np.where((zs == zt) & (abs(yt - ys) == distance), weight, 0.0)
-        to_next = (target < 64) & (zs == zt) & (yt + rows - ys == distance)
-        to_previous = (target >= 64) & (zs == zt) & (ys + rows - yt == distance)
-        cross += np.where(to_next | to_previous, weight, 0.0)
-    one = np.concatenate([own, cross], 1)
-    return jnp.asarray(np.concatenate([one, one], 0), jnp.bfloat16)
+
+
+def outer_edges_kernel(planes, tiles, cuts, parts, ahead, part_ref, d_ref, *rest):
+    h_refs, (work, out, sem) = rest[: len(cuts) - 1], rest[-3:]
+    rows = planes * tiles
+    odd = odd_place("gx")
+    begin, end = cuts[0], cuts[-1]
+
+    def plane(c, p):
+        i = max(i for i, cut in enumerate(cuts) if cut <= c)
+        if i == 0 and ahead:
+            return h_refs[i][pl.ds((c - cuts[i]) * 2 * tiles + p, tiles, stride=2), :]
+        return h_refs[i][c - cuts[i], p]
+
+    def send(i, first, last):
+        where = pl.ds(first * rows, (last - first) * rows)
+        return pltpu.make_async_copy(work.at[where, :], out.at[where, :], sem.at[i])
+
+    bounds = [begin + (end - begin) * i // parts for i in range(parts + 1)]
+    for i, (first, last) in enumerate(zip(bounds, bounds[1:])):
+        for side in range(2):
+
+            @pl.when(odd == side)
+            def _(side=side, first=first, last=last):
+                add_planes(planes, tiles, work, d_ref, plane, first, last, side)
+
+        send(i, first, last).start()
+    for i, (first, last) in enumerate(zip(bounds, bounds[1:])):
+        send(i, first, last).wait()
 
 
 def per_device(
@@ -358,34 +421,36 @@
         .transpose(0, 2, 1, 3)
         .reshape(comps * rows, LANES)
     )
+
+    def stay(array):
+        return pltpu.with_memory_space_constraint(array, pltpu.HBM)
+
     vmem = pl.BlockSpec(memory_space=VMEM)
     smem = pl.BlockSpec(memory_space=SMEM)
     anywhere = pl.BlockSpec(memory_space=pl.ANY)
 
     hbm = pl.BlockSpec(memory_space=pltpu.HBM)
     sds = jax.ShapeDtypeStruct
-    a = pl.pallas_call(
-        functools.partial(outer_kernel, comps, planes, tiles),
-        out_shape=sds((comps * tiles, 2, LANES), f32),
+    ahead_count, late = comps // 4, comps // 4
+    cuts = (0, ahead_count, comps - late, comps)
+    early = pl.pallas_call(
+        functools.partial(ahead_kernel, ahead_count, planes, tiles),
+        out_shape=sds((ahead_count * tiles, 2, LANES), f32),
         in_specs=[hbm],
         out_specs=vmem,
-        scratch_shapes=[pltpu.SemaphoreType.DMA((6,))],
+        scratch_shapes=[pltpu.SemaphoreType.DMA((4,))],
         compiler_params=params(8),
-        name="outer_planes",
-    )(
-        pltpu.with_memory_space_constraint(
-            flat.reshape(comps * tiles, planes // 2, 2, LANES), pltpu.HBM
-        )
-    )
-    b, first, second = pl.pallas_call(
-        functools.partial(pack_kernel, comps, planes, tiles),
-        out_shape=(
-            sds((comps, 2, tiles, LANES), f32),
-            sds((comps // 2, planes, LANES), f32),
-            sds((comps // 2, planes, LANES), f32),
+        name="ahead",
+    )(stay(flat.reshape(comps * tiles, planes // 2, 2, LANES)))
+    *a, b, first, second = pl.pallas_call(
+        functools.partial(pack_kernel, comps, planes, tiles, cuts[1:]),
+        out_shape=tuple(
+            [sds((end - begin, 2, tiles, LANES), f32) for begin, end in zip(cuts[1:], cuts[2:])]
+            + [sds((comps, 2, tiles, LANES), f32)]
+            + [sds((comps // 2, planes, LANES), f32)] * 2
         ),
         in_specs=[vmem],
-        out_specs=[vmem] * 3,
+        out_specs=[vmem] * 5,
         compiler_params=params(16),
         name="pack",
     )(flat)
@@ -398,7 +463,10 @@
     along_a = along_a + [(t, s) for s, t in along_a]
     along_b = [(i, (i + 1) % gy) for i in range(1, gy, 2)]
     along_b = along_b + [(t, s) for s, t in along_b]
-    ha = lax.ppermute(a, "gx", outer)
+    ha = []
+    for piece in [early, *a]:
+        ha.append(lax.ppermute(piece, "gx", outer))
+    ha[0] = ha[0].reshape(ahead_count * tiles * 2, LANES)
     hb = lax.ppermute(b, "gx", inner)
     z1 = lax.ppermute(first, "gy", along_a)
     z2 = lax.ppermute(second, "gy", along_b)
@@ -408,7 +476,7 @@
     part = pl.pallas_call(
         functools.partial(main_kernel, comps, planes, tiles, nreact),
         out_shape=sds((comps * rows, LANES), f32),
-        in_specs=[vmem, smem, vmem] + [hbm] * 5 + [smem, smem],
+        in_specs=[vmem, smem] + [hbm] * 5 + [smem, smem],
         out_specs=vmem,
         scratch_shapes=[
             VMEM((nreact,), f32),
@@ -423,6 +491,9 @@
             VMEM((PIECE, GROUP * LANES), f32),
             VMEM((1, GROUP * LANES), f32),
             VMEM((1, GROUP * LANES), f32),
+            VMEM((2 * LANES, 2 * LANES), jnp.bfloat16),
+            VMEM((many_of(comps) * rows, 2 * LANES), f32),
+            VMEM((many_of(comps) * rows, 2 * LANES), f32),
             SMEM((rows + 1,), jnp.int32),
             pltpu.SemaphoreType.DMA((5,)),
         ],
@@ -434,35 +505,44 @@
     )(
         flat,
         diffusivity,
-        shift_matrix(),
-        log_prefactor,
-        activation,
-        heat,
-        reactants.T,
-        products,
+        stay(log_prefactor),
+        stay(activation),
+        stay(heat),
+        stay(reactants.T),
+        stay(products),
         substeps,
         flame,
     )
 
-    out = pl.pallas_call(
-        functools.partial(edge_kernel, comps, planes, tiles),
-        out_shape=sds((comps * rows, LANES), f32),
-        in_specs=[vmem, smem, vmem, vmem, vmem, vmem],
-        out_specs=anywhere,
-        scratch_shapes=[VMEM((comps * rows, LANES), f32), pltpu.SemaphoreType.DMA((8,))],
+    whole = sds((comps * rows, LANES), f32)
+    cost = pl.CostEstimate(flops=1_000_000, bytes_accessed=3_000_000, transcendentals=0)
+    part = pl.pallas_call(
+        functools.partial(inner_edges_kernel, comps, planes, tiles),
+        out_shape=whole,
+        in_specs=[vmem, smem, vmem, vmem, vmem],
+        out_specs=vmem,
+        input_output_aliases={0: 0},
         compiler_params=params(16),
-        cost_estimate=pl.CostEstimate(
-            flops=1_000_000, bytes_accessed=3_000_000, transcendentals=0
-        ),
-        name="edges",
-    )(
-        part,
-        diffusivity,
-        ha.reshape(comps * tiles * 2, LANES),
-        hb.reshape(comps * 2 * tiles, LANES),
-        z1,
-        z2,
-    )
+        cost_estimate=cost,
+        name="inner_edges",
+    )(part, diffusivity, hb, z1, z2)
+    out = None
+    for begin, end, parts in ((0, 2, 3), (2, 3, 2)):
+        extra = [] if out is None else [out]
+        count = end - begin
+        part, out = pl.pallas_call(
+            functools.partial(
+                outer_edges_kernel, planes, tiles, cuts[begin : end + 1], parts, begin == 0
+            ),
+            out_shape=(whole, whole),
+            in_specs=[vmem, smem] + [vmem] * count + [anywhere] * len(extra),
+            out_specs=(vmem, anywhere),
+            scratch_shapes=[pltpu.SemaphoreType.DMA((parts,))],
+            input_output_aliases={0: 0, 2 + count: 1} if extra else {0: 0},
+            compiler_params=params(16),
+            cost_estimate=cost,
+            name="outer_edges",
+        )(part, diffusivity, *ha[begin:end], *extra)
     return (
         out.reshape(comps, tiles, planes, LANES).transpose(0, 2, 1, 3).reshape(comps, planes, cells)
     )

time: 17.5 us -> 21.5 us (1.23)
  starting transfers between devices: 7.63 us -> 10.6 us
  local copies, waits for them, and re-layouts: 0.04 us -> 1.49 us
  waiting for transfers between devices: 1.41 us -> 0.7 us
  Pallas kernels: 8.18 us -> 8.49 us
    ppermute x1 -> x3, starting transfers between devices: 3.44 us -> 4.91 us  [per_device(): ha.append(lax.ppermute(piece, 'gx', outer))]
    unnamed x20 -> x10, local copies, waits for them, and re-layouts: 0.04 us -> 1.49 us
    pallas_call x3 -> x5, Pallas kernels: 3.82 us -> 5.02 us  [the longest x2 3.04 us: per_device(): pl.pallas_call(functools.partial(outer_edges_kernel, planes, tiles, cuts[...]
    ppermute x1, starting transfers between devices: 1.64 us -> 2.64 us  [per_device(): z1 = lax.ppermute(first, 'gy', along_a)]
    pallas_call x1, Pallas kernels: 4.36 us -> 3.47 us  [per_device(): pl.pallas_call(functools.partial(main_kernel, comps, planes, tiles, nreac...]
    ppermute x1, waiting for transfers between devices: 1.4 us -> 0.68 us  [per_device(): z2 = lax.ppermute(second, 'gy', along_b)]
    ppermute x1, starting transfers between devices: 0.07 us -> 0.56 us  [per_device(): hb = lax.ppermute(b, 'gx', inner)]
  transfers between devices with their start and end apart: 4 -> 6, of which waited for: 1 -> 1; matrix products, arithmetic and copies ran while one was open for 0% -> 0% of each run, Pallas kernels for 26% -> 32%
where the time goes in v2:
time: 21.5 us; the launch traced here: 21.3 us
  starting transfers between devices  10.6 us (49%)
  Pallas kernels  8.49 us (39%)
  local copies, waits for them, and re-layouts  1.49 us (7%)
  waiting for transfers between devices  0.7 us (3%)
    ppermute x3, starting transfers between devices, per_device(): ha.append(lax.ppermute(piece, 'gx', outer))  4.91 us
    pallas_call x1, Pallas kernels, per_device(): pl.pallas_call(functools.partial(main_kernel, comps, planes, tiles, nreac...  3.47 us
    pallas_call x2, Pallas kernels, per_device(): pl.pallas_call(functools.partial(outer_edges_kernel, planes, tiles, cuts[...  3.04 us
    ppermute x1, starting transfers between devices, per_device(): z1 = lax.ppermute(first, 'gy', along_a)  2.64 us
    ppermute x1, starting transfers between devices, per_device(): z2 = lax.ppermute(second, 'gy', along_b)  2.48 us
    unnamed x10, local copies, waits for them, and re-layouts  1.49 us
    pallas_call x1, Pallas kernels, per_device(): pl.pallas_call(functools.partial(inner_edges_kernel, comps, planes, tiles...  0.91 us
    pallas_call x1, Pallas kernels, per_device(): pl.pallas_call(functools.partial(ahead_kernel, ahead_count, planes, tiles...  0.82 us
  transfers between devices with their start and end apart: 6, of which 1 were waited for; matrix products, arithmetic and copies ran while one was open for 0% of the time, Pallas kernels for 32%

profile of v2, /device:TPU:0, one launch (start us, length us, event | category | flops | bytes accessed | tf_op | source)
XLA Modules:
  0.0 21.3 jit_solution(11429987120518016675)
XLA Ops:
  0.0 0.0 copy-start
  0.0 1.5 %copy-done = f32[54,8,1024]{2,1,0:T(8,128)S(1)} copy-done((f32[54,8,1024]{2,1,0:T(8,128)S(1)}, f32[54,8,1024]{2,1,0:T(8,128)}, u32[]{:S(2)}) %copy-start) | copy-done | bytes 1769496
  1.5 0.0 copy-start.1
  1.5 0.0 copy-start.2
  1.5 0.0 copy-start.3
  1.5 0.0 copy-start.4
  1.5 0.3 %pack.1 = (f32[28,2,8,128]{3,2,1,0:T(8,128)S(1)}, f32[13,2,8,128]{3,2,1,0:T(8,128)S(1)}, f32[54,2,8,128]{3,2,1,0:T(8,128)S(1)}, f32[27,8,128]{2,1,0:T(8,128)S(1)}, f32[27,8,128]{2,1,0:T(8,128)S(1)}) custom-call(f32[3456,128]{1,0:T(8,128)S(1)} %bitcast.15), custom_call_target="tpu_custom_call" | custom-call | tf_op jit(solution)/shard_map/pack/pallas_call | solution.py:445
  1.7 0.6 %collective-permute-start = (f32[54,2,8,128]{3,2,1,0:T(8,128)S(1)}, f32[54,2,8,128]{3,2,1,0:T(8,128)S(1)}, u32[]{:S(2)}, u32[]{:S(2)}) collective-permute-start(f32[54,2,8,128]{3,2,1,0:T(8,128)S(1)} %get-tuple-element.13), channel_id=1, source_target_pairs={{0,4},{8,12},{16,20},{24,28},{4,0},{12,8},{20,16},{28,24},{1,5},{9... | collective-permute-start | bytes 1327112 | tf_op jit(solution)/shard_map/ppermute | solution.py:470
  2.3 2.6 %collective-permute-start.1 = (f32[27,8,128]{2,1,0:T(8,128)S(1)}, f32[27,8,128]{2,1,0:T(8,128)S(1)}, u32[]{:S(2)}, u32[]{:S(2)}) collective-permute-start(f32[27,8,128]{2,1,0:T(8,128)S(1)} %get-tuple-element.14), channel_id=1, source_target_pairs={{0,1},{2,3},{1,0},{3,2},{4,5},{6,7},{5,4},{7,6},{8,9},{10,11},{9,8... | collective-permute-start | bytes 331784 | tf_op jit(solution)/shard_map/ppermute | solution.py:471
  4.9 2.2 %collective-permute-start.4 = (f32[28,2,8,128]{3,2,1,0:T(8,128)S(1)}, f32[28,2,8,128]{3,2,1,0:T(8,128)S(1)}, u32[]{:S(2)}, u32[]{:S(2)}) collective-permute-start(f32[28,2,8,128]{3,2,1,0:T(8,128)S(1)} %get-tuple-element.16), channel_id=1, source_target_pairs={{4,8},{12,16},{20,24},{28,0},{8,4},{16,12},{24,20},{0,28},{5,9},{1... | collective-permute-start | bytes 688136 | tf_op jit(solution)/shard_map/ppermute | solution.py:468
  7.1 0.8 %ahead.1 = f32[104,2,128]{2,1,0:T(2,128)S(1)} custom-call(f32[432,4,2,128]{3,2,1,0:T(2,128)} %bitcast.14), custom_call_target="tpu_custom_call" | custom-call | tf_op jit(solution)/shard_map/ahead/pallas_call | solution.py:436
  8.0 0.5 %collective-permute-start.3 = (f32[104,2,128]{2,1,0:T(2,128)S(1)}, f32[104,2,128]{2,1,0:T(2,128)S(1)}, u32[]{:S(2)}, u32[]{:S(2)}) collective-permute-start(f32[104,2,128]{2,1,0:T(2,128)S(1)} %ahead.1), channel_id=1, source_target_pairs={{4,8},{12,16},{20,24},{28,0},{8,4},{16,12},{24,20},{0,28},{5,9},{1... | collective-permute-start | bytes 319496 | tf_op jit(solution)/shard_map/ppermute | solution.py:468
  8.5 2.2 %collective-permute-start.5 = (f32[13,2,8,128]{3,2,1,0:T(8,128)S(1)}, f32[13,2,8,128]{3,2,1,0:T(8,128)S(1)}, u32[]{:S(2)}, u32[]{:S(2)}) collective-permute-start(f32[13,2,8,128]{3,2,1,0:T(8,128)S(1)} %get-tuple-element.18), channel_id=1, source_target_pairs={{4,8},{12,16},{20,24},{28,0},{8,4},{16,12},{24,20},{0,28},{5,9},{1... | collective-permute-start | bytes 319496 | tf_op jit(solution)/shard_map/ppermute | solution.py:468
  10.7 0.0 collective-permute-done.1.z1_ref
  10.7 2.5 %collective-permute-start.2 = (f32[27,8,128]{2,1,0:T(8,128)S(1)}, f32[27,8,128]{2,1,0:T(8,128)S(1)}, u32[]{:S(2)}, u32[]{:S(2)}) collective-permute-start(f32[27,8,128]{2,1,0:T(8,128)S(1)} %get-tuple-element.15), channel_id=1, source_target_pairs={{1,2},{3,0},{2,1},{0,3},{5,6},{7,4},{6,5},{4,7},{9,10},{11,8},{10,... | collective-permute-start | bytes 331784 | tf_op jit(solution)/shard_map/ppermute | solution.py:472
  13.2 0.0 copy-done.1
  13.2 0.0 copy-done.2
  13.2 0.0 copy-done.3
  13.2 0.0 copy-done.4
  13.2 3.5 %main.1.part_ref = f32[3456,128]{1,0:T(8,128)S(1)} custom-call(f32[3456,128]{1,0:T(8,128)S(1)} %bitcast.16, f32[54]{0:T(128)S(1)} %copy-done.2, f32[325]{0:T(512)} %lp_hbm.1, f32[325]{0:T(512)} %act_hbm.1, f32[325]{0:T(512)} %heat_hbm.1, f32[53,650]{1,0:T(8,128)} %bitcast.18, f32[53,325]{1,0:T(8,128)} %pr_hbm.1, s32[8,8]{1,0:T(8,128)S(1)} %copy-done.3, ...), custom_call_target="tpu_custom_call" | custom-call | flops 2000000000 | bytes 16000000 | tf_op jit(solution)/shard_map/main/pallas_call | solution.py:476
  16.7 0.7 %collective-permute-done.2.z2_ref = f32[27,8,128]{2,1,0:T(8,128)S(1)} collective-permute-done((f32[27,8,128]{2,1,0:T(8,128)S(1)}, f32[27,8,128]{2,1,0:T(8,128)S(1)}, u32[]{:S(2)}, u32[]{:S(2)}) %collective-permute-start.2) | collective-permute-done | bytes 110624 | tf_op jit(solution)/shard_map/ppermute | solution.py:472
  17.3 0.0 collective-permute-done.hb_ref
  17.3 0.9 %inner_edges.1.part_ref = f32[3456,128]{1,0:T(8,128)S(1)} custom-call(f32[3456,128]{1,0:T(8,128)S(1)} %main.1.part_ref, f32[54]{0:T(128)S(1)} %copy-done.2, f32[54,2,8,128]{3,2,1,0:T(8,128)S(1)} %collective-permute-done.hb_ref, f32[27,8,128]{2,1,0:T(8,128)S(1)} %collective-permute-done.1.z1_ref, ...), custom_call_target="tpu_custom_call", output_to_operand_aliasing={{}: (0, {})} | custom-call | flops 1000000 | bytes 3000000 | tf_op jit(solution)/shard_map/inner_edges/pallas_call | solution.py:519
  18.3 0.0 collective-permute-done.3
  18.3 0.0 collective-permute-done.4.rest_1_
  18.3 1.7 %outer_edges.2 = (f32[3456,128]{1,0:T(8,128)S(1)}, f32[3456,128]{1,0:T(8,128)}) custom-call(f32[3456,128]{1,0:T(8,128)S(1)} %inner_edges.1.part_ref, f32[54]{0:T(128)S(1)} %copy-done.2, f32[208,128]{1,0:T(8,128)S(1)} %bitcast.17, f32[28,2,8,128]{3,2,1,0:T(8,128)S(1)} %collective-permute-done.4.rest_1_), custom_call_target="tpu_custom_call", output_to_operand_aliasing={{0}: (0, {})} | custom-call | flops 1000000 | bytes 3000000 | tf_op jit(solution)/shard_map/outer_edges/pallas_call | solution.py:533
  20.0 0.0 collective-permute-done.5.rest_0_
  20.0 1.4 %outer_edges.3 = (f32[3456,128]{1,0:T(8,128)S(1)}, f32[3456,128]{1,0:T(8,128)}) custom-call(f32[3456,128]{1,0:T(8,128)S(1)} %get-tuple-element.17.part_ref, f32[54]{0:T(128)S(1)} %copy-done.2, f32[13,2,8,128]{3,2,1,0:T(8,128)S(1)} %collective-permute-done.5.rest_0_, f32[3456,128]{1,0:T(8,128)} %get-tuple-element.19.rest_1_), custom_call_target="tpu_custom_call", output_to_operand_aliasing={{0}: (0, {}), {1}: (3, {})} | custom-call | flops 1000000 | bytes 3000000 | tf_op jit(solution)/shard_map/outer_edges/pallas_call | solution.py:533
Async XLA Ops:
  0.0 1.5 %copy-start = (f32[54,8,1024]{2,1,0:T(8,128)S(1)}, f32[54,8,1024]{2,1,0:T(8,128)}, u32[]{:S(2)}) copy-start(f32[54,8,1024]{2,1,0:T(8,128)} %param.9) | copy-start | bytes 5308420
  1.5 11.7 %copy-start.1 = (f32[54,8,1024]{2,1,0:T(8,128)S(1)}, f32[54,8,1024]{2,1,0:T(8,128)}, u32[]{:S(2)}) copy-start(f32[54,8,1024]{2,1,0:T(8,128)} %param.9) | copy-start | bytes 5308420
  1.5 11.7 %copy-start.2 = (f32[54]{0:T(128)S(1)}, f32[54]{0:T(128)}, u32[]{:S(2)}) copy-start(f32[54]{0:T(128)} %d_ref.7) | copy-start | bytes 652
  1.5 11.7 %copy-start.3 = (s32[8,8]{1,0:T(8,128)S(1)}, s32[8,8]{1,0:T(8,128)}, u32[]{:S(2)}) copy-start(s32[8,8]{1,0:T(8,128)} %sub_ref.1) | copy-start | bytes 772
  1.5 11.7 %copy-start.4 = (s32[8,8]{1,0:T(8,128)S(1)}, s32[8,8]{1,0:T(8,128)}, u32[]{:S(2)}) copy-start(s32[8,8]{1,0:T(8,128)} %flame_ref.1) | copy-start | bytes 772
  1.7 15.6 %collective-permute-start = (f32[54,2,8,128]{3,2,1,0:T(8,128)S(1)}, f32[54,2,8,128]{3,2,1,0:T(8,128)S(1)}, u32[]{:S(2)}, u32[]{:S(2)}) collective-permute-start(f32[54,2,8,128]{3,2,1,0:T(8,128)S(1)} %get-tuple-element.13), channel_id=1, source_target_pairs={{0,4},{8,12},{16,20},{24,28},{4,0},{12,8},{20,16},{28,24},{1,5},{9... | collective-permute-start | bytes 1327112 | tf_op jit(solution)/shard_map/ppermute | solution.py:470
  2.3 8.4 %collective-permute-start.1 = (f32[27,8,128]{2,1,0:T(8,128)S(1)}, f32[27,8,128]{2,1,0:T(8,128)S(1)}, u32[]{:S(2)}, u32[]{:S(2)}) collective-permute-start(f32[27,8,128]{2,1,0:T(8,128)S(1)} %get-tuple-element.14), channel_id=1, source_target_pairs={{0,1},{2,3},{1,0},{3,2},{4,5},{6,7},{5,4},{7,6},{8,9},{10,11},{9,8... | collective-permute-start | bytes 331784 | tf_op jit(solution)/shard_map/ppermute | solution.py:471
  4.9 13.3 %collective-permute-start.4 = (f32[28,2,8,128]{3,2,1,0:T(8,128)S(1)}, f32[28,2,8,128]{3,2,1,0:T(8,128)S(1)}, u32[]{:S(2)}, u32[]{:S(2)}) collective-permute-start(f32[28,2,8,128]{3,2,1,0:T(8,128)S(1)} %get-tuple-element.16), channel_id=1, source_target_pairs={{4,8},{12,16},{20,24},{28,0},{8,4},{16,12},{24,20},{0,28},{5,9},{1... | collective-permute-start | bytes 688136 | tf_op jit(solution)/shard_map/ppermute | solution.py:468
  8.0 10.3 %collective-permute-start.3 = (f32[104,2,128]{2,1,0:T(2,128)S(1)}, f32[104,2,128]{2,1,0:T(2,128)S(1)}, u32[]{:S(2)}, u32[]{:S(2)}) collective-permute-start(f32[104,2,128]{2,1,0:T(2,128)S(1)} %ahead.1), channel_id=1, source_target_pairs={{4,8},{12,16},{20,24},{28,0},{8,4},{16,12},{24,20},{0,28},{5,9},{1... | collective-permute-start | bytes 319496 | tf_op jit(solution)/shard_map/ppermute | solution.py:468
  8.5 11.5 %collective-permute-start.5 = (f32[13,2,8,128]{3,2,1,0:T(8,128)S(1)}, f32[13,2,8,128]{3,2,1,0:T(8,128)S(1)}, u32[]{:S(2)}, u32[]{:S(2)}) collective-permute-start(f32[13,2,8,128]{3,2,1,0:T(8,128)S(1)} %get-tuple-element.18), channel_id=1, source_target_pairs={{4,8},{12,16},{20,24},{28,0},{8,4},{16,12},{24,20},{0,28},{5,9},{1... | collective-permute-start | bytes 319496 | tf_op jit(solution)/shard_map/ppermute | solution.py:468
  10.7 6.6 %collective-permute-start.2 = (f32[27,8,128]{2,1,0:T(8,128)S(1)}, f32[27,8,128]{2,1,0:T(8,128)S(1)}, u32[]{:S(2)}, u32[]{:S(2)}) collective-permute-start(f32[27,8,128]{2,1,0:T(8,128)S(1)} %get-tuple-element.15), channel_id=1, source_target_pairs={{1,2},{3,0},{2,1},{0,3},{5,6},{7,4},{6,5},{4,7},{9,10},{11,8},{10,... | collective-permute-start | bytes 331784 | tf_op jit(solution)/shard_map/ppermute | solution.py:472

commit v3 on v2

--- a/solution.py
+++ b/solution.py
@@ -42,25 +42,13 @@
         copy.wait()
 
 
-def pack_kernel(comps, planes, tiles, cuts, s_ref, *out_refs):
-    a_refs, (b_ref, first_ref, second_ref) = out_refs[:-3], out_refs[-3:]
+def pack_kernel(comps, planes, tiles, s_ref, b_ref, low_ref, high_ref):
     rows = planes * tiles
-    odd = odd_place("gy")
     lane = lax.broadcasted_iota(jnp.int32, (planes, LANES), 1)
-    off_a = odd_place("gx") * (planes - 2)
-    off_b = (planes - 2) - off_a
-
-    def plane(c, x):
-        return s_ref[pl.ds(c * rows + x, tiles, stride=planes), :]
-
-    for a_ref, begin, end in zip(a_refs, cuts, cuts[1:]):
-        for c in range(begin, end):
-            for p in range(2):
-                a_ref[c - begin, p] = plane(c, off_a + p)
+    off_b = (1 - odd_place("gx")) * (planes - 2)
     for c in range(comps):
         for p in range(2):
-            b_ref[c, p] = plane(c, off_b + p)
-    swap = jnp.broadcast_to(odd, (planes, LANES)) == 1
+            b_ref[c, p] = s_ref[pl.ds(c * rows + off_b + p, tiles, stride=planes), :]
     last = (tiles - 1) * planes
     for k in range(comps // 2):
         first, second = 2 * k * rows, (2 * k + 1) * rows
@@ -68,10 +56,8 @@
         low_b = s_ref[second : second + planes, :]
         high_a = s_ref[first + last : first + last + planes, :]
         high_b = s_ref[second + last : second + last + planes, :]
-        low = jnp.where(lane < 64, low_a, pltpu.roll(low_b, 64, 1))
-        high = jnp.where(lane < 64, pltpu.roll(high_a, 64, 1), high_b)
-        first_ref[k] = jnp.where(swap, low, high)
-        second_ref[k] = jnp.where(swap, high, low)
+        low_ref[k] = jnp.where(lane < 64, low_a, pltpu.roll(low_b, 64, 1))
+        high_ref[k] = jnp.where(lane < 64, pltpu.roll(high_a, 64, 1), high_b)
 
 
 def split3(value):
@@ -338,11 +324,10 @@
         work[second, :] = two - (weight * far_weight) * near
 
 
-def inner_edges_kernel(comps, planes, tiles, part_ref, d_ref, hb_ref, z1_ref, z2_ref, work):
+def inner_edges_kernel(comps, planes, tiles, part_ref, d_ref, hb_ref, zl_ref, zh_ref, work):
     del part_ref
     rows = planes * tiles
     lane = lax.broadcasted_iota(jnp.int32, (planes, LANES), 1)
-    swap = jnp.broadcast_to(odd_place("gy"), (planes, LANES)) == 1
     last = (tiles - 1) * planes
     above = jnp.where(lane % 64 < NZ, near_weight, 0.0)
     below = jnp.where(lane % 64 >= NZ, near_weight, 0.0)
@@ -350,9 +335,7 @@
     upper = jnp.where(lane < 64, 0.0, 1.0)
 
     def pair(k, carry):
-        one, two = z1_ref[k], z2_ref[k]
-        low = jnp.where(swap, one, two)
-        high = jnp.where(swap, two, one)
+        low, high = zl_ref[k], zh_ref[k]
         low = pltpu.roll(low, LANES - NZ, 1) * above - far_weight * low
         high = pltpu.roll(high, NZ, 1) * below - far_weight * high
         lows = (low * lower, pltpu.roll(low * upper, 64, 1))
@@ -378,32 +361,29 @@
             )
 
 
-def outer_edges_kernel(planes, tiles, cuts, parts, ahead, part_ref, d_ref, *rest):
-    h_refs, (work, out, sem) = rest[: len(cuts) - 1], rest[-3:]
+def outer_edges_kernel(comps, planes, tiles, parts, part_ref, d_ref, h_ref, work, out, sem):
+    del part_ref
     rows = planes * tiles
     odd = odd_place("gx")
-    begin, end = cuts[0], cuts[-1]
 
     def plane(c, p):
-        i = max(i for i, cut in enumerate(cuts) if cut <= c)
-        if i == 0 and ahead:
-            return h_refs[i][pl.ds((c - cuts[i]) * 2 * tiles + p, tiles, stride=2), :]
-        return h_refs[i][c - cuts[i], p]
+        return h_ref[pl.ds(c * 2 * tiles + p, tiles, stride=2), :]
 
     def send(i, first, last):
         where = pl.ds(first * rows, (last - first) * rows)
         return pltpu.make_async_copy(work.at[where, :], out.at[where, :], sem.at[i])
 
-    bounds = [begin + (end - begin) * i // parts for i in range(parts + 1)]
-    for i, (first, last) in enumerate(zip(bounds, bounds[1:])):
-        for side in range(2):
-
-            @pl.when(odd == side)
-            def _(side=side, first=first, last=last):
+    bounds = [comps * i // parts for i in range(parts + 1)]
+    spans = list(zip(bounds, bounds[1:]))
+    for side in range(2):
+
+        @pl.when(odd == side)
+        def _(side=side):
+            for i, (first, last) in enumerate(spans):
                 add_planes(planes, tiles, work, d_ref, plane, first, last, side)
-
-        send(i, first, last).start()
-    for i, (first, last) in enumerate(zip(bounds, bounds[1:])):
+                send(i, first, last).start()
+
+    for i, (first, last) in enumerate(spans):
         send(i, first, last).wait()
 
 
@@ -431,26 +411,24 @@
 
     hbm = pl.BlockSpec(memory_space=pltpu.HBM)
     sds = jax.ShapeDtypeStruct
-    ahead_count, late = comps // 4, comps // 4
-    cuts = (0, ahead_count, comps - late, comps)
-    early = pl.pallas_call(
-        functools.partial(ahead_kernel, ahead_count, planes, tiles),
-        out_shape=sds((ahead_count * tiles, 2, LANES), f32),
+    ahead = pl.pallas_call(
+        functools.partial(ahead_kernel, comps, planes, tiles),
+        out_shape=sds((comps * tiles, 2, LANES), f32),
         in_specs=[hbm],
         out_specs=vmem,
-        scratch_shapes=[pltpu.SemaphoreType.DMA((4,))],
+        scratch_shapes=[pltpu.SemaphoreType.DMA((6,))],
         compiler_params=params(8),
         name="ahead",
     )(stay(flat.reshape(comps * tiles, planes // 2, 2, LANES)))
-    *a, b, first, second = pl.pallas_call(
-        functools.partial(pack_kernel, comps, planes, tiles, cuts[1:]),
-        out_shape=tuple(
-            [sds((end - begin, 2, tiles, LANES), f32) for begin, end in zip(cuts[1:], cuts[2:])]
-            + [sds((comps, 2, tiles, LANES), f32)]
-            + [sds((comps // 2, planes, LANES), f32)] * 2
+    beside, low, high = pl.pallas_call(
+        functools.partial(pack_kernel, comps, planes, tiles),
+        out_shape=(
+            sds((comps, 2, tiles, LANES), f32),
+            sds((comps // 2, planes, LANES), f32),
+            sds((comps // 2, planes, LANES), f32),
         ),
         in_specs=[vmem],
-        out_specs=[vmem] * 5,
+        out_specs=[vmem] * 3,
         compiler_params=params(16),
         name="pack",
     )(flat)
@@ -459,17 +437,12 @@
     outer = outer + [(t, s) for s, t in outer]
     inner = [(i, i + 1) for i in range(0, gx, 2)]
     inner = inner + [(t, s) for s, t in inner]
-    along_a = [(i, i + 1) for i in range(0, gy, 2)]
-    along_a = along_a + [(t, s) for s, t in along_a]
-    along_b = [(i, (i + 1) % gy) for i in range(1, gy, 2)]
-    along_b = along_b + [(t, s) for s, t in along_b]
-    ha = []
-    for piece in [early, *a]:
-        ha.append(lax.ppermute(piece, "gx", outer))
-    ha[0] = ha[0].reshape(ahead_count * tiles * 2, LANES)
-    hb = lax.ppermute(b, "gx", inner)
-    z1 = lax.ppermute(first, "gy", along_a)
-    z2 = lax.ppermute(second, "gy", along_b)
+    forward = [(i, (i + 1) % gy) for i in range(gy)]
+    backward = [(t, s) for s, t in forward]
+    ha = lax.ppermute(ahead, "gx", outer)
+    hb = lax.ppermute(beside, "gx", inner)
+    zl = lax.ppermute(high, "gy", forward)
+    zh = lax.ppermute(low, "gy", backward)
 
     padded = pl.cdiv(nreact, LANES) * LANES
     wide = pl.cdiv(nreact, 16) * 16
@@ -525,24 +498,19 @@
         compiler_params=params(16),
         cost_estimate=cost,
         name="inner_edges",
-    )(part, diffusivity, hb, z1, z2)
-    out = None
-    for begin, end, parts in ((0, 2, 3), (2, 3, 2)):
-        extra = [] if out is None else [out]
-        count = end - begin
-        part, out = pl.pallas_call(
-            functools.partial(
-                outer_edges_kernel, planes, tiles, cuts[begin : end + 1], parts, begin == 0
-            ),
-            out_shape=(whole, whole),
-            in_specs=[vmem, smem] + [vmem] * count + [anywhere] * len(extra),
-            out_specs=(vmem, anywhere),
-            scratch_shapes=[pltpu.SemaphoreType.DMA((parts,))],
-            input_output_aliases={0: 0, 2 + count: 1} if extra else {0: 0},
-            compiler_params=params(16),
-            cost_estimate=cost,
-            name="outer_edges",
-        )(part, diffusivity, *ha[begin:end], *extra)
+    )(part, diffusivity, hb, zl, zh)
+    parts = 6
+    _, out = pl.pallas_call(
+        functools.partial(outer_edges_kernel, comps, planes, tiles, parts),
+        out_shape=(whole, whole),
+        in_specs=[vmem, smem, vmem],
+        out_specs=(vmem, anywhere),
+        scratch_shapes=[pltpu.SemaphoreType.DMA((parts,))],
+        input_output_aliases={0: 0},
+        compiler_params=params(16),
+        cost_estimate=cost,
+        name="outer_edges",
+    )(part, diffusivity, ha.reshape(comps * tiles * 2, LANES))
     return (
         out.reshape(comps, tiles, planes, LANES).transpose(0, 2, 1, 3).reshape(comps, planes, cells)
     )

time: 21.5 us -> 18.8 us (0.87)
  starting transfers between devices: 10.6 us -> 7.99 us
  Pallas kernels: 8.49 us -> 7.47 us
  waiting for transfers between devices: 0.7 us -> 1.65 us
    ppermute x6 -> x4, starting transfers between devices: 10.6 us -> 7.99 us  [the longest x1 3.61 us: per_device(): ha = lax.ppermute(ahead, 'gx', outer)]
    pallas_call x4 -> x3, Pallas kernels: 4.11 us -> 3.08 us  [the longest x1 1.84 us: per_device(): pl.pallas_call(functools.partial(outer_edges_kernel, comps, planes, tiles...]
    ppermute x6 -> x4, waiting for transfers between devices: 0.7 us -> 1.65 us  [the longest x1 1.14 us: per_device(): ha = lax.ppermute(ahead, 'gx', outer)]
  transfers between devices with their start and end apart: 6 -> 4, of which waited for: 1 -> 3; matrix products, arithmetic and copies ran while one was open for 0% -> 0% of each run, Pallas kernels for 32% -> 30%
where the time goes in v3:
time: 18.8 us; the launch traced here: 18.6 us
  starting transfers between devices  7.99 us (42%)
  Pallas kernels  7.47 us (40%)
  waiting for transfers between devices  1.65 us (9%)
  local copies, waits for them, and re-layouts  1.49 us (8%)
    ppermute x1, starting transfers between devices, per_device(): ha = lax.ppermute(ahead, 'gx', outer)  3.61 us
    pallas_call x1, Pallas kernels, per_device(): pl.pallas_call(functools.partial(main_kernel, comps, planes, tiles, nreac...  3.46 us
    ppermute x1, starting transfers between devices, per_device(): zh = lax.ppermute(low, 'gy', backward)  2.25 us
    pallas_call x1, Pallas kernels, per_device(): pl.pallas_call(functools.partial(outer_edges_kernel, comps, planes, tiles...  1.84 us
    ppermute x1, starting transfers between devices, per_device(): zl = lax.ppermute(high, 'gy', forward)  1.58 us
    unnamed x10, local copies, waits for them, and re-layouts  1.49 us
    ppermute x1, waiting for transfers between devices, per_device(): ha = lax.ppermute(ahead, 'gx', outer)  1.14 us
    pallas_call x1, Pallas kernels, per_device(): pl.pallas_call(functools.partial(ahead_kernel, comps, planes, tiles), out...  1.11 us
  transfers between devices with their start and end apart: 4, of which 3 were waited for; matrix products, arithmetic and copies ran while one was open for 0% of the time, Pallas kernels for 30%

profile of v3, /device:TPU:0, one launch (start us, length us, event | category | flops | bytes accessed | tf_op | source)
XLA Modules:
  0.0 18.6 jit_solution(68210057587840210)
XLA Ops:
  0.0 0.0 copy-start
  0.0 1.5 %copy-done = f32[54,8,1024]{2,1,0:T(8,128)S(1)} copy-done((f32[54,8,1024]{2,1,0:T(8,128)S(1)}, f32[54,8,1024]{2,1,0:T(8,128)}, u32[]{:S(2)}) %copy-start) | copy-done | bytes 1769496
  1.5 0.0 copy-start.1
  1.5 0.0 copy-start.2
  1.5 0.0 copy-start.3
  1.5 0.0 copy-start.4
  1.5 0.1 pack.1
  1.6 0.6 %collective-permute-start = (f32[54,2,8,128]{3,2,1,0:T(8,128)S(1)}, f32[54,2,8,128]{3,2,1,0:T(8,128)S(1)}, u32[]{:S(2)}, u32[]{:S(2)}) collective-permute-start(f32[54,2,8,128]{3,2,1,0:T(8,128)S(1)} %get-tuple-element.9), channel_id=1, source_target_pairs={{0,4},{8,12},{16,20},{24,28},{4,0},{12,8},{20,16},{28,24},{1,5},{9... | collective-permute-start | bytes 1327112 | tf_op jit(solution)/shard_map/ppermute | solution.py:443
  2.2 1.1 %ahead.1 = f32[432,2,128]{2,1,0:T(2,128)S(1)} custom-call(f32[432,4,2,128]{3,2,1,0:T(2,128)} %bitcast.14), custom_call_target="tpu_custom_call" | custom-call | tf_op jit(solution)/shard_map/ahead/pallas_call | solution.py:414
  3.3 3.6 %collective-permute-start.3 = (f32[432,2,128]{2,1,0:T(2,128)S(1)}, f32[432,2,128]{2,1,0:T(2,128)S(1)}, u32[]{:S(2)}, u32[]{:S(2)}) collective-permute-start(f32[432,2,128]{2,1,0:T(2,128)S(1)} %ahead.1), channel_id=1, source_target_pairs={{4,8},{12,16},{20,24},{28,0},{8,4},{16,12},{24,20},{0,28},{5,9},{1... | collective-permute-start | bytes 1327112 | tf_op jit(solution)/shard_map/ppermute | solution.py:442
  6.9 1.6 %collective-permute-start.1 = (f32[27,8,128]{2,1,0:T(8,128)S(1)}, f32[27,8,128]{2,1,0:T(8,128)S(1)}, u32[]{:S(2)}, u32[]{:S(2)}) collective-permute-start(f32[27,8,128]{2,1,0:T(8,128)S(1)} %get-tuple-element.10), channel_id=1, source_target_pairs={{0,1},{1,2},{2,3},{3,0},{4,5},{5,6},{6,7},{7,4},{8,9},{9,10},{10,1... | collective-permute-start | bytes 331784 | tf_op jit(solution)/shard_map/ppermute | solution.py:444
  8.5 2.2 %collective-permute-start.2 = (f32[27,8,128]{2,1,0:T(8,128)S(1)}, f32[27,8,128]{2,1,0:T(8,128)S(1)}, u32[]{:S(2)}, u32[]{:S(2)}) collective-permute-start(f32[27,8,128]{2,1,0:T(8,128)S(1)} %get-tuple-element.11), channel_id=1, source_target_pairs={{1,0},{2,1},{3,2},{0,3},{5,4},{6,5},{7,6},{4,7},{9,8},{10,9},{11,1... | collective-permute-start | bytes 331784 | tf_op jit(solution)/shard_map/ppermute | solution.py:445
  10.7 0.0 copy-done.1
  10.7 0.0 copy-done.2
  10.7 0.0 copy-done.3
  10.7 0.0 copy-done.4
  10.7 3.5 %main.1.part_ref = f32[3456,128]{1,0:T(8,128)S(1)} custom-call(f32[3456,128]{1,0:T(8,128)S(1)} %bitcast.16, f32[54]{0:T(128)S(1)} %copy-done.2, f32[325]{0:T(512)} %lp_hbm.1, f32[325]{0:T(512)} %act_hbm.1, f32[325]{0:T(512)} %heat_hbm.1, f32[53,650]{1,0:T(8,128)} %bitcast.18, f32[53,325]{1,0:T(8,128)} %pr_hbm.1, s32[8,8]{1,0:T(8,128)S(1)} %copy-done.3, ...), custom_call_target="tpu_custom_call" | custom-call | flops 2000000000 | bytes 16000000 | tf_op jit(solution)/shard_map/main/pallas_call | solution.py:449
  14.2 0.3 %collective-permute-done.1.zl_ref = f32[27,8,128]{2,1,0:T(8,128)S(1)} collective-permute-done((f32[27,8,128]{2,1,0:T(8,128)S(1)}, f32[27,8,128]{2,1,0:T(8,128)S(1)}, u32[]{:S(2)}, u32[]{:S(2)}) %collective-permute-start.1) | collective-permute-done | bytes 110624 | tf_op jit(solution)/shard_map/ppermute | solution.py:444
  14.5 0.2 %collective-permute-done.2.zh_ref = f32[27,8,128]{2,1,0:T(8,128)S(1)} collective-permute-done((f32[27,8,128]{2,1,0:T(8,128)S(1)}, f32[27,8,128]{2,1,0:T(8,128)S(1)}, u32[]{:S(2)}, u32[]{:S(2)}) %collective-permute-start.2) | collective-permute-done | bytes 110624 | tf_op jit(solution)/shard_map/ppermute | solution.py:445
  14.7 0.0 collective-permute-done.hb_ref
  14.7 0.9 %inner_edges.1.part_ref = f32[3456,128]{1,0:T(8,128)S(1)} custom-call(f32[3456,128]{1,0:T(8,128)S(1)} %main.1.part_ref, f32[54]{0:T(128)S(1)} %copy-done.2, f32[54,2,8,128]{3,2,1,0:T(8,128)S(1)} %collective-permute-done.hb_ref, f32[27,8,128]{2,1,0:T(8,128)S(1)} %collective-permute-done.1.zl_ref, ...), custom_call_target="tpu_custom_call", output_to_operand_aliasing={{}: (0, {})} | custom-call | flops 1000000 | bytes 3000000 | tf_op jit(solution)/shard_map/inner_edges/pallas_call | solution.py:492
  15.7 1.1 %collective-permute-done.3 = f32[432,2,128]{2,1,0:T(2,128)S(1)} collective-permute-done((f32[432,2,128]{2,1,0:T(2,128)S(1)}, f32[432,2,128]{2,1,0:T(2,128)S(1)}, u32[]{:S(2)}, u32[]{:S(2)}) %collective-permute-start.3) | collective-permute-done | bytes 442400 | tf_op jit(solution)/shard_map/ppermute | solution.py:442
  16.8 1.8 %outer_edges.1 = (f32[3456,128]{1,0:T(8,128)S(1)}, f32[3456,128]{1,0:T(8,128)}) custom-call(f32[3456,128]{1,0:T(8,128)S(1)} %inner_edges.1.part_ref, f32[54]{0:T(128)S(1)} %copy-done.2, f32[864,128]{1,0:T(8,128)S(1)} %bitcast.17), custom_call_target="tpu_custom_call", output_to_operand_aliasing={{0}: (0, {})} | custom-call | flops 1000000 | bytes 3000000 | tf_op jit(solution)/shard_map/outer_edges/pallas_call | solution.py:503
Async XLA Ops:
  0.0 1.5 %copy-start = (f32[54,8,1024]{2,1,0:T(8,128)S(1)}, f32[54,8,1024]{2,1,0:T(8,128)}, u32[]{:S(2)}) copy-start(f32[54,8,1024]{2,1,0:T(8,128)} %param.9) | copy-start | bytes 5308420
  1.5 9.3 %copy-start.1 = (f32[54,8,1024]{2,1,0:T(8,128)S(1)}, f32[54,8,1024]{2,1,0:T(8,128)}, u32[]{:S(2)}) copy-start(f32[54,8,1024]{2,1,0:T(8,128)} %param.9) | copy-start | bytes 5308420
  1.5 9.3 %copy-start.2 = (f32[54]{0:T(128)S(1)}, f32[54]{0:T(128)}, u32[]{:S(2)}) copy-start(f32[54]{0:T(128)} %d_ref.5) | copy-start | bytes 652
  1.5 9.3 %copy-start.3 = (s32[8,8]{1,0:T(8,128)S(1)}, s32[8,8]{1,0:T(8,128)}, u32[]{:S(2)}) copy-start(s32[8,8]{1,0:T(8,128)} %sub_ref.1) | copy-start | bytes 772
  1.5 9.3 %copy-start.4 = (s32[8,8]{1,0:T(8,128)S(1)}, s32[8,8]{1,0:T(8,128)}, u32[]{:S(2)}) copy-start(s32[8,8]{1,0:T(8,128)} %flame_ref.1) | copy-start | bytes 772
  1.6 13.1 %collective-permute-start = (f32[54,2,8,128]{3,2,1,0:T(8,128)S(1)}, f32[54,2,8,128]{3,2,1,0:T(8,128)S(1)}, u32[]{:S(2)}, u32[]{:S(2)}) collective-permute-start(f32[54,2,8,128]{3,2,1,0:T(8,128)S(1)} %get-tuple-element.9), channel_id=1, source_target_pairs={{0,4},{8,12},{16,20},{24,28},{4,0},{12,8},{20,16},{28,24},{1,5},{9... | collective-permute-start | bytes 1327112 | tf_op jit(solution)/shard_map/ppermute | solution.py:443
  3.3 13.5 %collective-permute-start.3 = (f32[432,2,128]{2,1,0:T(2,128)S(1)}, f32[432,2,128]{2,1,0:T(2,128)S(1)}, u32[]{:S(2)}, u32[]{:S(2)}) collective-permute-start(f32[432,2,128]{2,1,0:T(2,128)S(1)} %ahead.1), channel_id=1, source_target_pairs={{4,8},{12,16},{20,24},{28,0},{8,4},{16,12},{24,20},{0,28},{5,9},{1... | collective-permute-start | bytes 1327112 | tf_op jit(solution)/shard_map/ppermute | solution.py:442
  6.9 7.6 %collective-permute-start.1 = (f32[27,8,128]{2,1,0:T(8,128)S(1)}, f32[27,8,128]{2,1,0:T(8,128)S(1)}, u32[]{:S(2)}, u32[]{:S(2)}) collective-permute-start(f32[27,8,128]{2,1,0:T(8,128)S(1)} %get-tuple-element.10), channel_id=1, source_target_pairs={{0,1},{1,2},{2,3},{3,0},{4,5},{5,6},{6,7},{7,4},{8,9},{9,10},{10,1... | collective-permute-start | bytes 331784 | tf_op jit(solution)/shard_map/ppermute | solution.py:444
  8.5 6.2 %collective-permute-start.2 = (f32[27,8,128]{2,1,0:T(8,128)S(1)}, f32[27,8,128]{2,1,0:T(8,128)S(1)}, u32[]{:S(2)}, u32[]{:S(2)}) collective-permute-start(f32[27,8,128]{2,1,0:T(8,128)S(1)} %get-tuple-element.11), channel_id=1, source_target_pairs={{1,0},{2,1},{3,2},{0,3},{5,4},{6,5},{7,6},{4,7},{9,8},{10,9},{11,1... | collective-permute-start | bytes 331784 | tf_op jit(solution)/shard_map/ppermute | solution.py:445

commit v4 on v3

--- a/solution.py
+++ b/solution.py
@@ -2,6 +2,7 @@
 
 import jax
 import jax.numpy as jnp
+import numpy as np
 from jax import lax
 from jax.experimental import pallas as pl
 from jax.experimental.pallas import tpu as pltpu
@@ -69,24 +70,22 @@
 
 
 def shift_matrix():
-    shape = (LANES, LANES)
-    source = lax.broadcasted_iota(jnp.int32, shape, 0)
-    target = lax.broadcasted_iota(jnp.int32, shape, 1)
+    source = np.arange(LANES)[:, None]
+    target = np.arange(LANES)[None, :]
     rows = LANES // NZ
     ys, yt = source // NZ, target // NZ
-    turn = (target - source) & (NZ - 1)
+    turn = (target - source) % NZ
     same_z = turn == 0
-
-    def weight(distance):
-        return jnp.where(distance == 1, 16.0, jnp.where(distance == 2, -1.0, 0.0))
-
-    turn = jnp.minimum(turn, NZ - turn)
-    along_z = jnp.where(same_z, -90.0, weight(turn))
-    own = jnp.where(ys == yt, along_z, jnp.where(same_z, weight(jnp.abs(yt - ys)), 0.0))
-    apart = jnp.where(target < LANES // 2, yt + rows - ys, ys + rows - yt)
-    cross = jnp.where(same_z, weight(apart), 0.0)
-    one = jnp.concatenate([own, cross], 1).astype(jnp.bfloat16)
-    return jnp.concatenate([one, one], 0)
+    weights = {1: 16.0, 2: -1.0}
+    own = np.where(source == target, -90.0, 0.0)
+    cross = np.zeros_like(own)
+    apart = np.where(target < LANES // 2, yt + rows - ys, ys + rows - yt)
+    for distance, weight in weights.items():
+        own += np.where((ys == yt) & (np.minimum(turn, NZ - turn) == distance), weight, 0.0)
+        own += np.where(same_z & (abs(yt - ys) == distance), weight, 0.0)
+        cross += np.where(same_z & (apart == distance), weight, 0.0)
+    one = np.concatenate([own, cross], 1)
+    return jnp.asarray(np.concatenate([one, one], 0), jnp.bfloat16)
 
 
 def many_of(comps):
@@ -99,15 +98,20 @@
     tiles,
     nreact,
     s_ref,
-    d_ref,
+    shift_ref,
+    d_hbm,
+    sub_hbm,
+    flame_hbm,
     lp_hbm,
     act_hbm,
     heat_hbm,
     rt_hbm,
     pr_hbm,
+    o_ref,
+    dv_ref,
+    d_ref,
     sub_ref,
     flame_ref,
-    o_ref,
     lp_ref,
     act_ref,
     heat_ref,
@@ -118,9 +122,9 @@
     w1_ref,
     w2_ref,
     a_ref,
+    old_ref,
     t_ref,
     st_ref,
-    shift_ref,
     even_ref,
     odd_ref,
     pos_ref,
@@ -133,6 +137,9 @@
         pltpu.make_async_copy(source, target, sem.at[i])
         for i, (source, target) in enumerate(
             (
+                (d_hbm, d_ref),
+                (sub_hbm, sub_ref),
+                (flame_hbm, flame_ref),
                 (lp_hbm, lp_ref),
                 (act_hbm, act_ref),
                 (heat_hbm, heat_ref),
@@ -144,13 +151,42 @@
     for load in loads:
         load.start()
 
-    shift_ref[...] = shift_matrix()
-
-    count = jnp.int32(0)
-    for x in range(planes):
-        for b in range(tiles):
-            pos_ref[count] = b * planes + x
-            count = count + flame_ref[x, b]
+    def scan_blocks():
+        for load in loads[:3]:
+            load.wait()
+        count = jnp.int32(0)
+        for x in range(planes):
+            for b in range(tiles):
+                pos_ref[count] = b * planes + x
+                count = count + flame_ref[x, b]
+        for c in range(comps):
+            dv_ref[c * planes : (c + 1) * planes, :] = jnp.full(
+                (planes, LANES), d_ref[c], jnp.float32
+            )
+        return count
+
+    padded = q_ref.shape[1]
+    wide = w1_ref.shape[0]
+
+    def tables():
+        q_ref[...] = jnp.zeros_like(q_ref)
+        p_ref[...] = jnp.zeros_like(p_ref)
+        q_ref[0:species, 0:nreact] = rt_ref[:, 0:nreact] + rt_ref[:, nreact : 2 * nreact]
+        p_ref[0:species, 0:nreact] = pr_ref[...]
+        p_ref[PIECE : PIECE + species, 0:nreact] = q_ref[0:species, 0:nreact]
+        for i, piece in enumerate(split3(act_ref[...].reshape(1, nreact) * (-LOG2E))):
+            q_ref[species + i : species + i + 1, 0:nreact] = piece.astype(jnp.float32)
+        for i, piece in enumerate(split3(lp_ref[...].reshape(1, nreact) * LOG2E)):
+            q_ref[species + 3 + i : species + 4 + i, 0:nreact] = piece.astype(jnp.float32)
+        for i, piece in enumerate(split3(heat_ref[...].reshape(1, nreact))):
+            p_ref[species + i : species + i + 1, 0:nreact] = piece.astype(jnp.float32)
+        q = q_ref[...]
+        w1 = jnp.transpose(jnp.concatenate([q, q, q], 0))
+        w1_ref[...] = w1[0:wide].astype(jnp.bfloat16)
+        w = p_ref[...].astype(jnp.bfloat16)
+        head, rest = w[:, :256], w[:, 256:padded]
+        w2_ref[...] = jnp.concatenate([head, head, rest, rest], 1)
+        a_ref[...] = jnp.ones_like(a_ref)
 
     many = many_of(comps)
     size = many * rows
@@ -196,6 +232,7 @@
     product(0, even_ref)
     if groups % 2 == 1 and groups > 2:
         product(1, odd_ref)
+        count = scan_blocks()
         combine(0, even_ref, False)
 
         def two(i, carry):
@@ -207,40 +244,24 @@
             return carry
 
         lax.fori_loop(0, (groups - 3) // 2, two, 0)
+        for load in loads[3:]:
+            load.wait()
         product(groups - 1, even_ref)
+        tables()
         combine(groups - 2, odd_ref, True)
         combine(groups - 1, even_ref, False)
     else:
+        count = scan_blocks()
+        for load in loads[3:]:
+            load.wait()
+        tables()
         for i in range(groups):
             combine(i, even_ref, False)
             if i < groups - 1:
                 product(i + 1, even_ref)
-    for load in loads:
-        load.wait()
 
     @pl.when(count > 0)
     def _():
-        padded = q_ref.shape[1]
-        wide = w1_ref.shape[0]
-        q_ref[...] = jnp.zeros_like(q_ref)
-        p_ref[...] = jnp.zeros_like(p_ref)
-        q_ref[0:species, 0:nreact] = rt_ref[:, 0:nreact] + rt_ref[:, nreact : 2 * nreact]
-        p_ref[0:species, 0:nreact] = pr_ref[...]
-        p_ref[PIECE : PIECE + species, 0:nreact] = q_ref[0:species, 0:nreact]
-        for i, piece in enumerate(split3(act_ref[...].reshape(1, nreact) * (-LOG2E))):
-            q_ref[species + i : species + i + 1, 0:nreact] = piece.astype(jnp.float32)
-        for i, piece in enumerate(split3(lp_ref[...].reshape(1, nreact) * LOG2E)):
-            q_ref[species + 3 + i : species + 4 + i, 0:nreact] = piece.astype(jnp.float32)
-        for i, piece in enumerate(split3(heat_ref[...].reshape(1, nreact))):
-            p_ref[species + i : species + i + 1, 0:nreact] = piece.astype(jnp.float32)
-        q = q_ref[...]
-        w1 = jnp.transpose(jnp.concatenate([q, q, q], 0))
-        w1_ref[...] = w1[0:wide].astype(jnp.bfloat16)
-        w = p_ref[...].astype(jnp.bfloat16)
-        head, rest = w[:, :256], w[:, 256:padded]
-        w2_ref[...] = jnp.concatenate([head, head, rest, rest], 1)
-
-        a_ref[...] = jnp.ones_like(a_ref)
         arow = lax.broadcasted_iota(jnp.int32, a_ref.shape, 0)
 
         def group(g, carry):
@@ -255,7 +276,9 @@
                 )
                 most = jnp.maximum(most, n)
                 cols = slice(i * LANES, (i + 1) * LANES)
-                a_ref[0:species, cols] = s_ref[pl.ds(block_rows + at, species, stride=rows), :]
+                mine = s_ref[pl.ds(block_rows + at, species, stride=rows), :]
+                a_ref[0:species, cols] = mine
+                old_ref[0:species, cols] = mine
                 t_ref[:, cols] = s_ref[pl.ds(at, 1), :]
                 pieces.append(jnp.full((1, LANES), n, jnp.int32))
             counts = jnp.concatenate(pieces, 1)
@@ -302,7 +325,8 @@
                     at = pos_ref[slot]
                     cols = slice(i * LANES, (i + 1) * LANES)
                     where = pl.ds(block_rows + at, species, stride=rows)
-                    o_ref[where, :] = o_ref[where, :] + (a_ref[0:species, cols] - s_ref[where, :])
+                    change = a_ref[0:species, cols] - old_ref[0:species, cols]
+                    o_ref[where, :] = o_ref[where, :] + change
                     top = pl.ds(at, 1)
                     o_ref[top, :] = o_ref[top, :] + (t_ref[:, cols] - s_ref[top, :])
 
@@ -311,12 +335,12 @@
         lax.fori_loop(0, (count + (GROUP - 1)) // GROUP, group, 0)
 
 
-def add_planes(planes, tiles, work, d_ref, plane, begin, end, side):
+def add_planes(planes, tiles, work, dv_ref, plane, begin, end, side):
     rows = planes * tiles
     for c in range(begin, end):
         near = plane(c, 1 - side)
         far = plane(c, side)
-        weight = d_ref[c]
+        weight = dv_ref[c * planes : (c + 1) * planes, :]
         first = pl.ds(c * rows + side * (planes - 1), tiles, stride=planes)
         second = pl.ds(c * rows + 1 + side * (planes - 3), tiles, stride=planes)
         one, two = work[first, :], work[second, :]
@@ -324,7 +348,7 @@
         work[second, :] = two - (weight * far_weight) * near
 
 
-def inner_edges_kernel(comps, planes, tiles, part_ref, d_ref, hb_ref, zl_ref, zh_ref, work):
+def inner_edges_kernel(comps, planes, tiles, part_ref, dv_ref, hb_ref, zl_ref, zh_ref, work):
     del part_ref
     rows = planes * tiles
     lane = lax.broadcasted_iota(jnp.int32, (planes, LANES), 1)
@@ -341,7 +365,7 @@
         lows = (low * lower, pltpu.roll(low * upper, 64, 1))
         highs = (pltpu.roll(high * lower, 64, 1), high * upper)
         for j in range(2):
-            weight = d_ref[2 * k + j]
+            weight = dv_ref[pl.ds(pl.multiple_of((2 * k + j) * planes, planes), planes), :]
             base = pl.multiple_of((2 * k + j) * rows, planes)
             top = pl.ds(base, planes)
             end = pl.ds(pl.multiple_of(base + last, planes), planes)
@@ -357,11 +381,11 @@
         @pl.when(odd == 1 - side)
         def _(side=side):
             add_planes(
-                planes, tiles, work, d_ref, lambda c, p: hb_ref[c, p], 0, comps, side
+                planes, tiles, work, dv_ref, lambda c, p: hb_ref[c, p], 0, comps, side
             )
 
 
-def outer_edges_kernel(comps, planes, tiles, parts, part_ref, d_ref, h_ref, work, out, sem):
+def outer_edges_kernel(comps, planes, tiles, parts, part_ref, dv_ref, h_ref, work, out, sem):
     del part_ref
     rows = planes * tiles
     odd = odd_place("gx")
@@ -380,7 +404,7 @@
         @pl.when(odd == side)
         def _(side=side):
             for i, (first, last) in enumerate(spans):
-                add_planes(planes, tiles, work, d_ref, plane, first, last, side)
+                add_planes(planes, tiles, work, dv_ref, plane, first, last, side)
                 send(i, first, last).start()
 
     for i, (first, last) in enumerate(spans):
@@ -406,7 +430,6 @@
         return pltpu.with_memory_space_constraint(array, pltpu.HBM)
 
     vmem = pl.BlockSpec(memory_space=VMEM)
-    smem = pl.BlockSpec(memory_space=SMEM)
     anywhere = pl.BlockSpec(memory_space=pl.ANY)
 
     hbm = pl.BlockSpec(memory_space=pltpu.HBM)
@@ -416,7 +439,7 @@
         out_shape=sds((comps * tiles, 2, LANES), f32),
         in_specs=[hbm],
         out_specs=vmem,
-        scratch_shapes=[pltpu.SemaphoreType.DMA((6,))],
+        scratch_shapes=[pltpu.SemaphoreType.DMA((1,))],
         compiler_params=params(8),
         name="ahead",
     )(stay(flat.reshape(comps * tiles, planes // 2, 2, LANES)))
@@ -446,12 +469,15 @@
 
     padded = pl.cdiv(nreact, LANES) * LANES
     wide = pl.cdiv(nreact, 16) * 16
-    part = pl.pallas_call(
+    part, dv = pl.pallas_call(
         functools.partial(main_kernel, comps, planes, tiles, nreact),
-        out_shape=sds((comps * rows, LANES), f32),
-        in_specs=[vmem, smem] + [hbm] * 5 + [smem, smem],
-        out_specs=vmem,
+        out_shape=(sds((comps * rows, LANES), f32), sds((comps * planes, LANES), f32)),
+        in_specs=[vmem, vmem] + [hbm] * 8,
+        out_specs=(vmem, vmem),
         scratch_shapes=[
+            SMEM((comps,), f32),
+            SMEM(substeps.shape, jnp.int32),
+            SMEM(flame.shape, jnp.int32),
             VMEM((nreact,), f32),
             VMEM((nreact,), f32),
             VMEM((nreact,), f32),
@@ -462,13 +488,13 @@
             VMEM((wide, 3 * PIECE), jnp.bfloat16),
             VMEM((2 * PIECE, 2 * padded), jnp.bfloat16),
             VMEM((PIECE, GROUP * LANES), f32),
+            VMEM((PIECE, GROUP * LANES), f32),
             VMEM((1, GROUP * LANES), f32),
             VMEM((1, GROUP * LANES), f32),
-            VMEM((2 * LANES, 2 * LANES), jnp.bfloat16),
             VMEM((many_of(comps) * rows, 2 * LANES), f32),
             VMEM((many_of(comps) * rows, 2 * LANES), f32),
             SMEM((rows + 1,), jnp.int32),
-            pltpu.SemaphoreType.DMA((5,)),
+            pltpu.SemaphoreType.DMA((8,)),
         ],
         compiler_params=params(24),
         cost_estimate=pl.CostEstimate(
@@ -477,14 +503,20 @@
         name="main",
     )(
         flat,
-        diffusivity,
-        stay(log_prefactor),
-        stay(activation),
-        stay(heat),
-        stay(reactants.T),
-        stay(products),
-        substeps,
-        flame,
+        shift_matrix(),
+        *map(
+            stay,
+            (
+                diffusivity,
+                substeps,
+                flame,
+                log_prefactor,
+                activation,
+                heat,
+                reactants.T,
+                products,
+            ),
+        ),
     )
 
     whole = sds((comps * rows, LANES), f32)
@@ -492,25 +524,25 @@
     part = pl.pallas_call(
         functools.partial(inner_edges_kernel, comps, planes, tiles),
         out_shape=whole,
-        in_specs=[vmem, smem, vmem, vmem, vmem],
+        in_specs=[vmem] * 5,
         out_specs=vmem,
         input_output_aliases={0: 0},
         compiler_params=params(16),
         cost_estimate=cost,
         name="inner_edges",
-    )(part, diffusivity, hb, zl, zh)
-    parts = 6
+    )(part, dv, hb, zl, zh)
+    parts = 3
     _, out = pl.pallas_call(
         functools.partial(outer_edges_kernel, comps, planes, tiles, parts),
         out_shape=(whole, whole),
-        in_specs=[vmem, smem, vmem],
+        in_specs=[vmem] * 3,
         out_specs=(vmem, anywhere),
         scratch_shapes=[pltpu.SemaphoreType.DMA((parts,))],
         input_output_aliases={0: 0},
         compiler_params=params(16),
         cost_estimate=cost,
         name="outer_edges",
-    )(part, diffusivity, ha.reshape(comps * tiles * 2, LANES))
+    )(part, dv, ha.reshape(comps * tiles * 2, LANES))
     return (
         out.reshape(comps, tiles, planes, LANES).transpose(0, 2, 1, 3).reshape(comps, planes, cells)
     )

time: 18.8 us -> 18.2 us (0.968)
  Pallas kernels: 7.47 us -> 6.03 us
  waiting for transfers between devices: 1.65 us -> 2.46 us
    pallas_call x1, Pallas kernels: 1.84 us -> 1.29 us  [per_device(): pl.pallas_call(functools.partial(outer_edges_kernel, comps, planes, tiles...]
    ppermute x1, waiting for transfers between devices: 1.14 us -> 1.68 us  [per_device(): ha = lax.ppermute(ahead, 'gx', outer)]
    pallas_call x1, Pallas kernels: 0.93 us -> 0.39 us  [per_device(): pl.pallas_call(functools.partial(inner_edges_kernel, comps, planes, tiles...]
    ppermute x1, waiting for transfers between devices: 0.27 us -> 0.54 us  [per_device(): zl = lax.ppermute(high, 'gy', forward)]
    pallas_call x1, Pallas kernels: 3.46 us -> 3.2 us  [per_device(): pl.pallas_call(functools.partial(main_kernel, comps, planes, tiles, nreac...]
    unnamed x10 -> x6, local copies, waits for them, and re-layouts: 1.49 us -> 1.48 us
  transfers between devices with their start and end apart: 4 -> 4, of which waited for: 3 -> 3; matrix products, arithmetic and copies ran while one was open for 0% -> 0% of each run, Pallas kernels for 30% -> 26%
where the time goes in v4:
time: 18.2 us; the launch traced here: 18 us
  starting transfers between devices  7.99 us (44%)
  Pallas kernels  6.03 us (33%)
  waiting for transfers between devices  2.46 us (14%)
  local copies, waits for them, and re-layouts  1.48 us (8%)
    ppermute x1, starting transfers between devices, per_device(): ha = lax.ppermute(ahead, 'gx', outer)  3.61 us
    pallas_call x1, Pallas kernels, per_device(): pl.pallas_call(functools.partial(main_kernel, comps, planes, tiles, nreac...  3.2 us
    ppermute x1, starting transfers between devices, per_device(): zh = lax.ppermute(low, 'gy', backward)  2.25 us
    ppermute x1, waiting for transfers between devices, per_device(): ha = lax.ppermute(ahead, 'gx', outer)  1.68 us
    ppermute x1, starting transfers between devices, per_device(): zl = lax.ppermute(high, 'gy', forward)  1.58 us
    unnamed x6, local copies, waits for them, and re-layouts  1.48 us
    pallas_call x1, Pallas kernels, per_device(): pl.pallas_call(functools.partial(outer_edges_kernel, comps, planes, tiles...  1.29 us
    pallas_call x1, Pallas kernels, per_device(): pl.pallas_call(functools.partial(ahead_kernel, comps, planes, tiles), out...  1.02 us
  transfers between devices with their start and end apart: 4, of which 3 were waited for; matrix products, arithmetic and copies ran while one was open for 0% of the time, Pallas kernels for 26%

profile of v4, /device:TPU:0, one launch (start us, length us, event | category | flops | bytes accessed | tf_op | source)
XLA Modules:
  0.0 18.0 jit_solution(831246939195292163)
XLA Ops:
  0.0 0.0 copy-start
  0.0 1.5 %copy-done = f32[54,8,1024]{2,1,0:T(8,128)S(1)} copy-done((f32[54,8,1024]{2,1,0:T(8,128)S(1)}, f32[54,8,1024]{2,1,0:T(8,128)}, u32[]{:S(2)}) %copy-start) | copy-done | bytes 1769496
  1.5 0.0 copy-start.1
  1.5 0.0 copy-start.2
  1.5 0.1 pack.1
  1.6 0.6 %collective-permute-start = (f32[54,2,8,128]{3,2,1,0:T(8,128)S(1)}, f32[54,2,8,128]{3,2,1,0:T(8,128)S(1)}, u32[]{:S(2)}, u32[]{:S(2)}) collective-permute-start(f32[54,2,8,128]{3,2,1,0:T(8,128)S(1)} %get-tuple-element.13), channel_id=1, source_target_pairs={{0,4},{8,12},{16,20},{24,28},{4,0},{12,8},{20,16},{28,24},{1,5},{9... | collective-permute-start | bytes 1327112 | tf_op jit(solution)/shard_map/ppermute | solution.py:466
  2.2 1.0 %ahead.1 = f32[432,2,128]{2,1,0:T(2,128)S(1)} custom-call(f32[432,4,2,128]{3,2,1,0:T(2,128)} %bitcast.14), custom_call_target="tpu_custom_call" | custom-call | tf_op jit(solution)/shard_map/ahead/pallas_call | solution.py:437
  3.2 3.6 %collective-permute-start.3 = (f32[432,2,128]{2,1,0:T(2,128)S(1)}, f32[432,2,128]{2,1,0:T(2,128)S(1)}, u32[]{:S(2)}, u32[]{:S(2)}) collective-permute-start(f32[432,2,128]{2,1,0:T(2,128)S(1)} %ahead.1), channel_id=1, source_target_pairs={{4,8},{12,16},{20,24},{28,0},{8,4},{16,12},{24,20},{0,28},{5,9},{1... | collective-permute-start | bytes 1327112 | tf_op jit(solution)/shard_map/ppermute | solution.py:465
  6.8 1.6 %collective-permute-start.1 = (f32[27,8,128]{2,1,0:T(8,128)S(1)}, f32[27,8,128]{2,1,0:T(8,128)S(1)}, u32[]{:S(2)}, u32[]{:S(2)}) collective-permute-start(f32[27,8,128]{2,1,0:T(8,128)S(1)} %get-tuple-element.14), channel_id=1, source_target_pairs={{0,1},{1,2},{2,3},{3,0},{4,5},{5,6},{6,7},{7,4},{8,9},{9,10},{10,1... | collective-permute-start | bytes 331784 | tf_op jit(solution)/shard_map/ppermute | solution.py:467
  8.4 2.2 %collective-permute-start.2 = (f32[27,8,128]{2,1,0:T(8,128)S(1)}, f32[27,8,128]{2,1,0:T(8,128)S(1)}, u32[]{:S(2)}, u32[]{:S(2)}) collective-permute-start(f32[27,8,128]{2,1,0:T(8,128)S(1)} %get-tuple-element.15), channel_id=1, source_target_pairs={{1,0},{2,1},{3,2},{0,3},{5,4},{6,5},{7,6},{4,7},{9,8},{10,9},{11,1... | collective-permute-start | bytes 331784 | tf_op jit(solution)/shard_map/ppermute | solution.py:468
  10.6 0.0 copy-done.1
  10.6 0.0 copy-done.2
  10.6 3.2 %main.1 = (f32[3456,128]{1,0:T(8,128)S(1)}, f32[432,128]{1,0:T(8,128)S(1)}) custom-call(f32[3456,128]{1,0:T(8,128)S(1)} %bitcast.16, bf16[256,256]{1,0:T(8,128)(2,1)S(1)} %copy-done.2, f32[54]{0:T(128)} %d_hbm.1, s32[8,8]{1,0:T(8,128)} %sub_hbm.1, s32[8,8]{1,0:T(8,128)} %flame_hbm.1, f32[325]{0:T(512)} %lp_hbm.1, f32[325]{0:T(512)} %act_hbm.1, f32[325]{0:T(512)} %heat_hbm.1, ...), custom_call_target="tpu_custom_call" | custom-call | flops 2000000000 | bytes 16000000 | tf_op jit(solution)/shard_map/main/pallas_call | solution.py:472
  13.8 0.5 %collective-permute-done.1.zl_ref = f32[27,8,128]{2,1,0:T(8,128)S(1)} collective-permute-done((f32[27,8,128]{2,1,0:T(8,128)S(1)}, f32[27,8,128]{2,1,0:T(8,128)S(1)}, u32[]{:S(2)}, u32[]{:S(2)}) %collective-permute-start.1) | collective-permute-done | bytes 110624 | tf_op jit(solution)/shard_map/ppermute | solution.py:467
  14.4 0.2 %collective-permute-done.2.zh_ref = f32[27,8,128]{2,1,0:T(8,128)S(1)} collective-permute-done((f32[27,8,128]{2,1,0:T(8,128)S(1)}, f32[27,8,128]{2,1,0:T(8,128)S(1)}, u32[]{:S(2)}, u32[]{:S(2)}) %collective-permute-start.2) | collective-permute-done | bytes 110624 | tf_op jit(solution)/shard_map/ppermute | solution.py:468
  14.6 0.0 collective-permute-done.hb_ref
  14.6 0.4 %inner_edges.1.part_ref = f32[3456,128]{1,0:T(8,128)S(1)} custom-call(f32[3456,128]{1,0:T(8,128)S(1)} %get-tuple-element.11.part_ref, f32[432,128]{1,0:T(8,128)S(1)} %get-tuple-element.12.dv_ref, f32[54,2,8,128]{3,2,1,0:T(8,128)S(1)} %collective-permute-done.hb_ref, f32[27,8,128]{2,1,0:T(8,128)S(1)} %collective-permute-done.1.zl_ref, ...), custom_call_target="tpu_custom_call", output_to_operand_aliasing={{}: (0, {})} | custom-call | flops 1000000 | bytes 3000000 | tf_op jit(solution)/shard_map/inner_edges/pallas_call | solution.py:524
  15.0 1.7 %collective-permute-done.3 = f32[432,2,128]{2,1,0:T(2,128)S(1)} collective-permute-done((f32[432,2,128]{2,1,0:T(2,128)S(1)}, f32[432,2,128]{2,1,0:T(2,128)S(1)}, u32[]{:S(2)}, u32[]{:S(2)}) %collective-permute-start.3) | collective-permute-done | bytes 442400 | tf_op jit(solution)/shard_map/ppermute | solution.py:465
  16.7 1.3 %outer_edges.1 = (f32[3456,128]{1,0:T(8,128)S(1)}, f32[3456,128]{1,0:T(8,128)}) custom-call(f32[3456,128]{1,0:T(8,128)S(1)} %inner_edges.1.part_ref, f32[432,128]{1,0:T(8,128)S(1)} %get-tuple-element.12.dv_ref, f32[864,128]{1,0:T(8,128)S(1)} %bitcast.17), custom_call_target="tpu_custom_call", output_to_operand_aliasing={{0}: (0, {})} | custom-call | flops 1000000 | bytes 3000000 | tf_op jit(solution)/shard_map/outer_edges/pallas_call | solution.py:535
Async XLA Ops:
  0.0 1.5 %copy-start = (f32[54,8,1024]{2,1,0:T(8,128)S(1)}, f32[54,8,1024]{2,1,0:T(8,128)}, u32[]{:S(2)}) copy-start(f32[54,8,1024]{2,1,0:T(8,128)} %param.10) | copy-start | bytes 5308420
  1.5 9.2 %copy-start.1 = (f32[54,8,1024]{2,1,0:T(8,128)S(1)}, f32[54,8,1024]{2,1,0:T(8,128)}, u32[]{:S(2)}) copy-start(f32[54,8,1024]{2,1,0:T(8,128)} %param.10) | copy-start | bytes 5308420
  1.5 9.2 %copy-start.2 = (bf16[256,256]{1,0:T(8,128)(2,1)S(1)}, bf16[256,256]{1,0:T(8,128)(2,1)}, u32[]{:S(2)}) copy-start(bf16[256,256]{1,0:T(8,128)(2,1)} %constant.2.clone.shift_ref) | copy-start | bytes 393220
  1.6 13.0 %collective-permute-start = (f32[54,2,8,128]{3,2,1,0:T(8,128)S(1)}, f32[54,2,8,128]{3,2,1,0:T(8,128)S(1)}, u32[]{:S(2)}, u32[]{:S(2)}) collective-permute-start(f32[54,2,8,128]{3,2,1,0:T(8,128)S(1)} %get-tuple-element.13), channel_id=1, source_target_pairs={{0,4},{8,12},{16,20},{24,28},{4,0},{12,8},{20,16},{28,24},{1,5},{9... | collective-permute-start | bytes 1327112 | tf_op jit(solution)/shard_map/ppermute | solution.py:466
  3.2 13.5 %collective-permute-start.3 = (f32[432,2,128]{2,1,0:T(2,128)S(1)}, f32[432,2,128]{2,1,0:T(2,128)S(1)}, u32[]{:S(2)}, u32[]{:S(2)}) collective-permute-start(f32[432,2,128]{2,1,0:T(2,128)S(1)} %ahead.1), channel_id=1, source_target_pairs={{4,8},{12,16},{20,24},{28,0},{8,4},{16,12},{24,20},{0,28},{5,9},{1... | collective-permute-start | bytes 1327112 | tf_op jit(solution)/shard_map/ppermute | solution.py:465
  6.8 7.6 %collective-permute-start.1 = (f32[27,8,128]{2,1,0:T(8,128)S(1)}, f32[27,8,128]{2,1,0:T(8,128)S(1)}, u32[]{:S(2)}, u32[]{:S(2)}) collective-permute-start(f32[27,8,128]{2,1,0:T(8,128)S(1)} %get-tuple-element.14), channel_id=1, source_target_pairs={{0,1},{1,2},{2,3},{3,0},{4,5},{5,6},{6,7},{7,4},{8,9},{9,10},{10,1... | collective-permute-start | bytes 331784 | tf_op jit(solution)/shard_map/ppermute | solution.py:467
  8.4 6.2 %collective-permute-start.2 = (f32[27,8,128]{2,1,0:T(8,128)S(1)}, f32[27,8,128]{2,1,0:T(8,128)S(1)}, u32[]{:S(2)}, u32[]{:S(2)}) collective-permute-start(f32[27,8,128]{2,1,0:T(8,128)S(1)} %get-tuple-element.15), channel_id=1, source_target_pairs={{1,0},{2,1},{3,2},{0,3},{5,4},{6,5},{7,6},{4,7},{9,8},{10,9},{11,1... | collective-permute-start | bytes 331784 | tf_op jit(solution)/shard_map/ppermute | solution.py:468

commit v5 on v4

--- a/solution.py
+++ b/solution.py
@@ -385,7 +385,7 @@
             )
 
 
-def outer_edges_kernel(comps, planes, tiles, parts, part_ref, dv_ref, h_ref, work, out, sem):
+def outer_edges_kernel(comps, planes, tiles, part_ref, dv_ref, h_ref, work, out, sem):
     del part_ref
     rows = planes * tiles
     odd = odd_place("gx")
@@ -397,7 +397,7 @@
         where = pl.ds(first * rows, (last - first) * rows)
         return pltpu.make_async_copy(work.at[where, :], out.at[where, :], sem.at[i])
 
-    bounds = [comps * i // parts for i in range(parts + 1)]
+    bounds = [0, comps // 9, comps // 3, comps]
     spans = list(zip(bounds, bounds[1:]))
     for side in range(2):
 
@@ -531,13 +531,12 @@
         cost_estimate=cost,
         name="inner_edges",
     )(part, dv, hb, zl, zh)
-    parts = 3
     _, out = pl.pallas_call(
-        functools.partial(outer_edges_kernel, comps, planes, tiles, parts),
+        functools.partial(outer_edges_kernel, comps, planes, tiles),
         out_shape=(whole, whole),
         in_specs=[vmem] * 3,
         out_specs=(vmem, anywhere),
-        scratch_shapes=[pltpu.SemaphoreType.DMA((parts,))],
+        scratch_shapes=[pltpu.SemaphoreType.DMA((3,))],
         input_output_aliases={0: 0},
         compiler_params=params(16),
         cost_estimate=cost,

time: 18.2 us -> 18.1 us (level)
  no operation moved by 1% of the time
where the time goes in v5:
time: 18.1 us; the launch traced here: 18 us
  starting transfers between devices  7.99 us (44%)
  Pallas kernels  5.99 us (33%)
  waiting for transfers between devices  2.46 us (14%)
  local copies, waits for them, and re-layouts  1.48 us (8%)
    ppermute x1, starting transfers between devices, per_device(): ha = lax.ppermute(ahead, 'gx', outer)  3.61 us
    pallas_call x1, Pallas kernels, per_device(): pl.pallas_call(functools.partial(main_kernel, comps, planes, tiles, nreac...  3.2 us
    ppermute x1, starting transfers between devices, per_device(): zh = lax.ppermute(low, 'gy', backward)  2.25 us
    ppermute x1, waiting for transfers between devices, per_device(): ha = lax.ppermute(ahead, 'gx', outer)  1.68 us
    ppermute x1, starting transfers between devices, per_device(): zl = lax.ppermute(high, 'gy', forward)  1.58 us
    unnamed x6, local copies, waits for them, and re-layouts  1.48 us
    pallas_call x1, Pallas kernels, per_device(): pl.pallas_call(functools.partial(outer_edges_kernel, comps, planes, tiles...  1.25 us
    pallas_call x1, Pallas kernels, per_device(): pl.pallas_call(functools.partial(ahead_kernel, comps, planes, tiles), out...  1.02 us
  transfers between devices with their start and end apart: 4, of which 3 were waited for; matrix products, arithmetic and copies ran while one was open for 0% of the time, Pallas kernels for 26%

profile of v5, /device:TPU:0, one launch (start us, length us, event | category | flops | bytes accessed | tf_op | source)
XLA Modules:
  0.0 18.0 jit_solution(5006950856788013945)
XLA Ops:
  0.0 0.0 copy-start
  0.0 1.5 %copy-done = f32[54,8,1024]{2,1,0:T(8,128)S(1)} copy-done((f32[54,8,1024]{2,1,0:T(8,128)S(1)}, f32[54,8,1024]{2,1,0:T(8,128)}, u32[]{:S(2)}) %copy-start) | copy-done | bytes 1769496
  1.5 0.0 copy-start.1
  1.5 0.0 copy-start.2
  1.5 0.1 pack.1
  1.6 0.6 %collective-permute-start = (f32[54,2,8,128]{3,2,1,0:T(8,128)S(1)}, f32[54,2,8,128]{3,2,1,0:T(8,128)S(1)}, u32[]{:S(2)}, u32[]{:S(2)}) collective-permute-start(f32[54,2,8,128]{3,2,1,0:T(8,128)S(1)} %get-tuple-element.13), channel_id=1, source_target_pairs={{0,4},{8,12},{16,20},{24,28},{4,0},{12,8},{20,16},{28,24},{1,5},{9... | collective-permute-start | bytes 1327112 | tf_op jit(solution)/shard_map/ppermute | solution.py:466
  2.2 1.0 %ahead.1 = f32[432,2,128]{2,1,0:T(2,128)S(1)} custom-call(f32[432,4,2,128]{3,2,1,0:T(2,128)} %bitcast.14), custom_call_target="tpu_custom_call" | custom-call | tf_op jit(solution)/shard_map/ahead/pallas_call | solution.py:437
  3.2 3.6 %collective-permute-start.3 = (f32[432,2,128]{2,1,0:T(2,128)S(1)}, f32[432,2,128]{2,1,0:T(2,128)S(1)}, u32[]{:S(2)}, u32[]{:S(2)}) collective-permute-start(f32[432,2,128]{2,1,0:T(2,128)S(1)} %ahead.1), channel_id=1, source_target_pairs={{4,8},{12,16},{20,24},{28,0},{8,4},{16,12},{24,20},{0,28},{5,9},{1... | collective-permute-start | bytes 1327112 | tf_op jit(solution)/shard_map/ppermute | solution.py:465
  6.8 1.6 %collective-permute-start.1 = (f32[27,8,128]{2,1,0:T(8,128)S(1)}, f32[27,8,128]{2,1,0:T(8,128)S(1)}, u32[]{:S(2)}, u32[]{:S(2)}) collective-permute-start(f32[27,8,128]{2,1,0:T(8,128)S(1)} %get-tuple-element.14), channel_id=1, source_target_pairs={{0,1},{1,2},{2,3},{3,0},{4,5},{5,6},{6,7},{7,4},{8,9},{9,10},{10,1... | collective-permute-start | bytes 331784 | tf_op jit(solution)/shard_map/ppermute | solution.py:467
  8.4 2.2 %collective-permute-start.2 = (f32[27,8,128]{2,1,0:T(8,128)S(1)}, f32[27,8,128]{2,1,0:T(8,128)S(1)}, u32[]{:S(2)}, u32[]{:S(2)}) collective-permute-start(f32[27,8,128]{2,1,0:T(8,128)S(1)} %get-tuple-element.15), channel_id=1, source_target_pairs={{1,0},{2,1},{3,2},{0,3},{5,4},{6,5},{7,6},{4,7},{9,8},{10,9},{11,1... | collective-permute-start | bytes 331784 | tf_op jit(solution)/shard_map/ppermute | solution.py:468
  10.6 0.0 copy-done.1
  10.6 0.0 copy-done.2
  10.6 3.2 %main.1 = (f32[3456,128]{1,0:T(8,128)S(1)}, f32[432,128]{1,0:T(8,128)S(1)}) custom-call(f32[3456,128]{1,0:T(8,128)S(1)} %bitcast.16, bf16[256,256]{1,0:T(8,128)(2,1)S(1)} %copy-done.2, f32[54]{0:T(128)} %d_hbm.1, s32[8,8]{1,0:T(8,128)} %sub_hbm.1, s32[8,8]{1,0:T(8,128)} %flame_hbm.1, f32[325]{0:T(512)} %lp_hbm.1, f32[325]{0:T(512)} %act_hbm.1, f32[325]{0:T(512)} %heat_hbm.1, ...), custom_call_target="tpu_custom_call" | custom-call | flops 2000000000 | bytes 16000000 | tf_op jit(solution)/shard_map/main/pallas_call | solution.py:472
  13.8 0.5 %collective-permute-done.1.zl_ref = f32[27,8,128]{2,1,0:T(8,128)S(1)} collective-permute-done((f32[27,8,128]{2,1,0:T(8,128)S(1)}, f32[27,8,128]{2,1,0:T(8,128)S(1)}, u32[]{:S(2)}, u32[]{:S(2)}) %collective-permute-start.1) | collective-permute-done | bytes 110624 | tf_op jit(solution)/shard_map/ppermute | solution.py:467
  14.4 0.2 %collective-permute-done.2.zh_ref = f32[27,8,128]{2,1,0:T(8,128)S(1)} collective-permute-done((f32[27,8,128]{2,1,0:T(8,128)S(1)}, f32[27,8,128]{2,1,0:T(8,128)S(1)}, u32[]{:S(2)}, u32[]{:S(2)}) %collective-permute-start.2) | collective-permute-done | bytes 110624 | tf_op jit(solution)/shard_map/ppermute | solution.py:468
  14.6 0.0 collective-permute-done.hb_ref
  14.6 0.4 %inner_edges.1.part_ref = f32[3456,128]{1,0:T(8,128)S(1)} custom-call(f32[3456,128]{1,0:T(8,128)S(1)} %get-tuple-element.11.part_ref, f32[432,128]{1,0:T(8,128)S(1)} %get-tuple-element.12.dv_ref, f32[54,2,8,128]{3,2,1,0:T(8,128)S(1)} %collective-permute-done.hb_ref, f32[27,8,128]{2,1,0:T(8,128)S(1)} %collective-permute-done.1.zl_ref, ...), custom_call_target="tpu_custom_call", output_to_operand_aliasing={{}: (0, {})} | custom-call | flops 1000000 | bytes 3000000 | tf_op jit(solution)/shard_map/inner_edges/pallas_call | solution.py:524
  15.0 1.7 %collective-permute-done.3 = f32[432,2,128]{2,1,0:T(2,128)S(1)} collective-permute-done((f32[432,2,128]{2,1,0:T(2,128)S(1)}, f32[432,2,128]{2,1,0:T(2,128)S(1)}, u32[]{:S(2)}, u32[]{:S(2)}) %collective-permute-start.3) | collective-permute-done | bytes 442400 | tf_op jit(solution)/shard_map/ppermute | solution.py:465
  16.7 1.3 %outer_edges.1 = (f32[3456,128]{1,0:T(8,128)S(1)}, f32[3456,128]{1,0:T(8,128)}) custom-call(f32[3456,128]{1,0:T(8,128)S(1)} %inner_edges.1.part_ref, f32[432,128]{1,0:T(8,128)S(1)} %get-tuple-element.12.dv_ref, f32[864,128]{1,0:T(8,128)S(1)} %bitcast.17), custom_call_target="tpu_custom_call", output_to_operand_aliasing={{0}: (0, {})} | custom-call | flops 1000000 | bytes 3000000 | tf_op jit(solution)/shard_map/outer_edges/pallas_call | solution.py:534
Async XLA Ops:
  0.0 1.5 %copy-start = (f32[54,8,1024]{2,1,0:T(8,128)S(1)}, f32[54,8,1024]{2,1,0:T(8,128)}, u32[]{:S(2)}) copy-start(f32[54,8,1024]{2,1,0:T(8,128)} %param.10) | copy-start | bytes 5308420
  1.5 9.2 %copy-start.1 = (f32[54,8,1024]{2,1,0:T(8,128)S(1)}, f32[54,8,1024]{2,1,0:T(8,128)}, u32[]{:S(2)}) copy-start(f32[54,8,1024]{2,1,0:T(8,128)} %param.10) | copy-start | bytes 5308420
  1.5 9.2 %copy-start.2 = (bf16[256,256]{1,0:T(8,128)(2,1)S(1)}, bf16[256,256]{1,0:T(8,128)(2,1)}, u32[]{:S(2)}) copy-start(bf16[256,256]{1,0:T(8,128)(2,1)} %constant.2.clone.shift_ref) | copy-start | bytes 393220
  1.6 13.0 %collective-permute-start = (f32[54,2,8,128]{3,2,1,0:T(8,128)S(1)}, f32[54,2,8,128]{3,2,1,0:T(8,128)S(1)}, u32[]{:S(2)}, u32[]{:S(2)}) collective-permute-start(f32[54,2,8,128]{3,2,1,0:T(8,128)S(1)} %get-tuple-element.13), channel_id=1, source_target_pairs={{0,4},{8,12},{16,20},{24,28},{4,0},{12,8},{20,16},{28,24},{1,5},{9... | collective-permute-start | bytes 1327112 | tf_op jit(solution)/shard_map/ppermute | solution.py:466
  3.2 13.5 %collective-permute-start.3 = (f32[432,2,128]{2,1,0:T(2,128)S(1)}, f32[432,2,128]{2,1,0:T(2,128)S(1)}, u32[]{:S(2)}, u32[]{:S(2)}) collective-permute-start(f32[432,2,128]{2,1,0:T(2,128)S(1)} %ahead.1), channel_id=1, source_target_pairs={{4,8},{12,16},{20,24},{28,0},{8,4},{16,12},{24,20},{0,28},{5,9},{1... | collective-permute-start | bytes 1327112 | tf_op jit(solution)/shard_map/ppermute | solution.py:465
  6.8 7.6 %collective-permute-start.1 = (f32[27,8,128]{2,1,0:T(8,128)S(1)}, f32[27,8,128]{2,1,0:T(8,128)S(1)}, u32[]{:S(2)}, u32[]{:S(2)}) collective-permute-start(f32[27,8,128]{2,1,0:T(8,128)S(1)} %get-tuple-element.14), channel_id=1, source_target_pairs={{0,1},{1,2},{2,3},{3,0},{4,5},{5,6},{6,7},{7,4},{8,9},{9,10},{10,1... | collective-permute-start | bytes 331784 | tf_op jit(solution)/shard_map/ppermute | solution.py:467
  8.4 6.2 %collective-permute-start.2 = (f32[27,8,128]{2,1,0:T(8,128)S(1)}, f32[27,8,128]{2,1,0:T(8,128)S(1)}, u32[]{:S(2)}, u32[]{:S(2)}) collective-permute-start(f32[27,8,128]{2,1,0:T(8,128)S(1)} %get-tuple-element.15), channel_id=1, source_target_pairs={{1,0},{2,1},{3,2},{0,3},{5,4},{6,5},{7,6},{4,7},{9,8},{10,9},{11,1... | collective-permute-start | bytes 331784 | tf_op jit(solution)/shard_map/ppermute | solution.py:468

commit v6 on v5

--- a/solution.py
+++ b/solution.py
@@ -348,7 +348,19 @@
         work[second, :] = two - (weight * far_weight) * near
 
 
-def inner_edges_kernel(comps, planes, tiles, part_ref, dv_ref, hb_ref, zl_ref, zh_ref, work):
+def write_out(planes, tiles, work, out, sem, first, last, side=None):
+    where = pl.ds(first * tiles, (last - first) * tiles)
+    kept = pl.ds(0, planes) if side is None else pl.ds(side * (planes - 2), 2)
+    rows = work.shape[0]
+    shape = (rows // planes, planes, LANES)
+    return pltpu.make_async_copy(
+        work.reshape(*shape).at[where, kept], out.reshape(*shape).at[where, kept], sem
+    )
+
+
+def inner_edges_kernel(
+    comps, planes, tiles, part_ref, dv_ref, hb_ref, zl_ref, zh_ref, work, out, sem
+):
     del part_ref
     rows = planes * tiles
     lane = lax.broadcasted_iota(jnp.int32, (planes, LANES), 1)
@@ -358,46 +370,48 @@
     lower = jnp.where(lane < 64, 1.0, 0.0)
     upper = jnp.where(lane < 64, 0.0, 1.0)
 
-    def pair(k, carry):
+    def pair(k):
         low, high = zl_ref[k], zh_ref[k]
         low = pltpu.roll(low, LANES - NZ, 1) * above - far_weight * low
         high = pltpu.roll(high, NZ, 1) * below - far_weight * high
         lows = (low * lower, pltpu.roll(low * upper, 64, 1))
         highs = (pltpu.roll(high * lower, 64, 1), high * upper)
         for j in range(2):
-            weight = dv_ref[pl.ds(pl.multiple_of((2 * k + j) * planes, planes), planes), :]
-            base = pl.multiple_of((2 * k + j) * rows, planes)
-            top = pl.ds(base, planes)
-            end = pl.ds(pl.multiple_of(base + last, planes), planes)
+            c = 2 * k + j
+            weight = dv_ref[c * planes : (c + 1) * planes, :]
+            top = slice(c * rows, c * rows + planes)
+            end = slice(c * rows + last, c * rows + last + planes)
             work[top, :] = work[top, :] + weight * lows[j]
             work[end, :] = work[end, :] + weight * highs[j]
-        return carry
-
-    for k in range(comps // 2):
-        pair(k, 0)
+
+    half = comps // 2
+    cuts = (0, 2 * (half // 6), 2 * (half // 2), comps)
+    spans = list(zip(cuts, cuts[1:]))
     odd = odd_place("gx")
     for side in range(2):
 
         @pl.when(odd == 1 - side)
         def _(side=side):
-            add_planes(
-                planes, tiles, work, dv_ref, lambda c, p: hb_ref[c, p], 0, comps, side
-            )
-
-
-def outer_edges_kernel(comps, planes, tiles, part_ref, dv_ref, h_ref, work, out, sem):
-    del part_ref
-    rows = planes * tiles
+            for i, (first, end) in enumerate(spans):
+                for k in range(first // 2, end // 2):
+                    pair(k)
+                add_planes(
+                    planes, tiles, work, dv_ref, lambda c, p: hb_ref[c, p], first, end, side
+                )
+                write_out(planes, tiles, work, out, sem.at[i], first, end).start()
+
+    for i, (first, end) in enumerate(spans):
+        write_out(planes, tiles, work, out, sem.at[i], first, end).wait()
+
+
+def outer_edges_kernel(comps, planes, tiles, part_ref, dv_ref, h_ref, prev, work, out, sem):
+    del part_ref, prev
     odd = odd_place("gx")
 
     def plane(c, p):
         return h_ref[pl.ds(c * 2 * tiles + p, tiles, stride=2), :]
 
-    def send(i, first, last):
-        where = pl.ds(first * rows, (last - first) * rows)
-        return pltpu.make_async_copy(work.at[where, :], out.at[where, :], sem.at[i])
-
-    bounds = [0, comps // 9, comps // 3, comps]
+    bounds = [0, comps // 3, comps]
     spans = list(zip(bounds, bounds[1:]))
     for side in range(2):
 
@@ -405,10 +419,9 @@
         def _(side=side):
             for i, (first, last) in enumerate(spans):
                 add_planes(planes, tiles, work, dv_ref, plane, first, last, side)
-                send(i, first, last).start()
-
-    for i, (first, last) in enumerate(spans):
-        send(i, first, last).wait()
+                write_out(planes, tiles, work, out, sem.at[i], first, last, side).start()
+            for i, (first, last) in enumerate(spans):
+                write_out(planes, tiles, work, out, sem.at[i], first, last, side).wait()
 
 
 def per_device(
@@ -521,11 +534,12 @@
 
     whole = sds((comps * rows, LANES), f32)
     cost = pl.CostEstimate(flops=1_000_000, bytes_accessed=3_000_000, transcendentals=0)
-    part = pl.pallas_call(
+    part, out = pl.pallas_call(
         functools.partial(inner_edges_kernel, comps, planes, tiles),
-        out_shape=whole,
+        out_shape=(whole, whole),
         in_specs=[vmem] * 5,
-        out_specs=vmem,
+        out_specs=(vmem, anywhere),
+        scratch_shapes=[pltpu.SemaphoreType.DMA((3,))],
         input_output_aliases={0: 0},
         compiler_params=params(16),
         cost_estimate=cost,
@@ -534,14 +548,14 @@
     _, out = pl.pallas_call(
         functools.partial(outer_edges_kernel, comps, planes, tiles),
         out_shape=(whole, whole),
-        in_specs=[vmem] * 3,
+        in_specs=[vmem] * 3 + [anywhere],
         out_specs=(vmem, anywhere),
-        scratch_shapes=[pltpu.SemaphoreType.DMA((3,))],
-        input_output_aliases={0: 0},
+        scratch_shapes=[pltpu.SemaphoreType.DMA((2,))],
+        input_output_aliases={0: 0, 3: 1},
         compiler_params=params(16),
         cost_estimate=cost,
         name="outer_edges",
-    )(part, dv, ha.reshape(comps * tiles * 2, LANES))
+    )(part, dv, ha.reshape(comps * tiles * 2, LANES), out)
     return (
         out.reshape(comps, tiles, planes, LANES).transpose(0, 2, 1, 3).reshape(comps, planes, cells)
     )

time: 18.1 us -> 17.8 us (0.983)
  waiting for transfers between devices: 2.46 us -> 1.43 us
  Pallas kernels: 5.99 us -> 6.68 us
    ppermute x1, waiting for transfers between devices: 1.68 us -> 0.65 us  [per_device(): ha = lax.ppermute(ahead, 'gx', outer)]
    pallas_call x1, Pallas kernels: 0.39 us -> 1.43 us  [per_device(): pl.pallas_call(functools.partial(inner_edges_kernel, comps, planes, tiles...]
    pallas_call x1, Pallas kernels: 1.25 us -> 0.91 us  [per_device(): pl.pallas_call(functools.partial(outer_edges_kernel, comps, planes, tiles...]
  transfers between devices with their start and end apart: 4 -> 4, of which waited for: 3 -> 3; matrix products, arithmetic and copies ran while one was open for 0% -> 0% of each run, Pallas kernels for 26% -> 32%
where the time goes in v6:
time: 17.8 us; the launch traced here: 17.6 us
  starting transfers between devices  7.99 us (45%)
  Pallas kernels  6.68 us (38%)
  local copies, waits for them, and re-layouts  1.48 us (8%)
  waiting for transfers between devices  1.43 us (8%)
    ppermute x1, starting transfers between devices, per_device(): ha = lax.ppermute(ahead, 'gx', outer)  3.61 us
    pallas_call x1, Pallas kernels, per_device(): pl.pallas_call(functools.partial(main_kernel, comps, planes, tiles, nreac...  3.2 us
    ppermute x1, starting transfers between devices, per_device(): zh = lax.ppermute(low, 'gy', backward)  2.25 us
    ppermute x1, starting transfers between devices, per_device(): zl = lax.ppermute(high, 'gy', forward)  1.58 us
    unnamed x6, local copies, waits for them, and re-layouts  1.48 us
    pallas_call x1, Pallas kernels, per_device(): pl.pallas_call(functools.partial(inner_edges_kernel, comps, planes, tiles...  1.43 us
    pallas_call x1, Pallas kernels, per_device(): pl.pallas_call(functools.partial(ahead_kernel, comps, planes, tiles), out...  1.02 us
    pallas_call x1, Pallas kernels, per_device(): pl.pallas_call(functools.partial(outer_edges_kernel, comps, planes, tiles...  0.91 us
  transfers between devices with their start and end apart: 4, of which 3 were waited for; matrix products, arithmetic and copies ran while one was open for 0% of the time, Pallas kernels for 32%

profile of v6, /device:TPU:0, one launch (start us, length us, event | category | flops | bytes accessed | tf_op | source)
XLA Modules:
  0.0 17.6 jit_solution(13365605987521140989)
XLA Ops:
  0.0 0.0 copy-start
  0.0 1.5 %copy-done = f32[54,8,1024]{2,1,0:T(8,128)S(1)} copy-done((f32[54,8,1024]{2,1,0:T(8,128)S(1)}, f32[54,8,1024]{2,1,0:T(8,128)}, u32[]{:S(2)}) %copy-start) | copy-done | bytes 1769496
  1.5 0.0 copy-start.1
  1.5 0.0 copy-start.2
  1.5 0.1 pack.1
  1.6 0.6 %collective-permute-start = (f32[54,2,8,128]{3,2,1,0:T(8,128)S(1)}, f32[54,2,8,128]{3,2,1,0:T(8,128)S(1)}, u32[]{:S(2)}, u32[]{:S(2)}) collective-permute-start(f32[54,2,8,128]{3,2,1,0:T(8,128)S(1)} %get-tuple-element.15), channel_id=1, source_target_pairs={{0,4},{8,12},{16,20},{24,28},{4,0},{12,8},{20,16},{28,24},{1,5},{9... | collective-permute-start | bytes 1327112 | tf_op jit(solution)/shard_map/ppermute | solution.py:479
  2.2 1.0 %ahead.1 = f32[432,2,128]{2,1,0:T(2,128)S(1)} custom-call(f32[432,4,2,128]{3,2,1,0:T(2,128)} %bitcast.14), custom_call_target="tpu_custom_call" | custom-call | tf_op jit(solution)/shard_map/ahead/pallas_call | solution.py:450
  3.2 3.6 %collective-permute-start.3 = (f32[432,2,128]{2,1,0:T(2,128)S(1)}, f32[432,2,128]{2,1,0:T(2,128)S(1)}, u32[]{:S(2)}, u32[]{:S(2)}) collective-permute-start(f32[432,2,128]{2,1,0:T(2,128)S(1)} %ahead.1), channel_id=1, source_target_pairs={{4,8},{12,16},{20,24},{28,0},{8,4},{16,12},{24,20},{0,28},{5,9},{1... | collective-permute-start | bytes 1327112 | tf_op jit(solution)/shard_map/ppermute | solution.py:478
  6.8 1.6 %collective-permute-start.1 = (f32[27,8,128]{2,1,0:T(8,128)S(1)}, f32[27,8,128]{2,1,0:T(8,128)S(1)}, u32[]{:S(2)}, u32[]{:S(2)}) collective-permute-start(f32[27,8,128]{2,1,0:T(8,128)S(1)} %get-tuple-element.16), channel_id=1, source_target_pairs={{0,1},{1,2},{2,3},{3,0},{4,5},{5,6},{6,7},{7,4},{8,9},{9,10},{10,1... | collective-permute-start | bytes 331784 | tf_op jit(solution)/shard_map/ppermute | solution.py:480
  8.4 2.2 %collective-permute-start.2 = (f32[27,8,128]{2,1,0:T(8,128)S(1)}, f32[27,8,128]{2,1,0:T(8,128)S(1)}, u32[]{:S(2)}, u32[]{:S(2)}) collective-permute-start(f32[27,8,128]{2,1,0:T(8,128)S(1)} %get-tuple-element.17), channel_id=1, source_target_pairs={{1,0},{2,1},{3,2},{0,3},{5,4},{6,5},{7,6},{4,7},{9,8},{10,9},{11,1... | collective-permute-start | bytes 331784 | tf_op jit(solution)/shard_map/ppermute | solution.py:481
  10.6 0.0 copy-done.1
  10.6 0.0 copy-done.2
  10.6 3.2 %main.1 = (f32[3456,128]{1,0:T(8,128)S(1)}, f32[432,128]{1,0:T(8,128)S(1)}) custom-call(f32[3456,128]{1,0:T(8,128)S(1)} %bitcast.16, bf16[256,256]{1,0:T(8,128)(2,1)S(1)} %copy-done.2, f32[54]{0:T(128)} %d_hbm.1, s32[8,8]{1,0:T(8,128)} %sub_hbm.1, s32[8,8]{1,0:T(8,128)} %flame_hbm.1, f32[325]{0:T(512)} %lp_hbm.1, f32[325]{0:T(512)} %act_hbm.1, f32[325]{0:T(512)} %heat_hbm.1, ...), custom_call_target="tpu_custom_call" | custom-call | flops 2000000000 | bytes 16000000 | tf_op jit(solution)/shard_map/main/pallas_call | solution.py:485
  13.8 0.5 %collective-permute-done.1.zl_ref = f32[27,8,128]{2,1,0:T(8,128)S(1)} collective-permute-done((f32[27,8,128]{2,1,0:T(8,128)S(1)}, f32[27,8,128]{2,1,0:T(8,128)S(1)}, u32[]{:S(2)}, u32[]{:S(2)}) %collective-permute-start.1) | collective-permute-done | bytes 110624 | tf_op jit(solution)/shard_map/ppermute | solution.py:480
  14.4 0.2 %collective-permute-done.2.zh_ref = f32[27,8,128]{2,1,0:T(8,128)S(1)} collective-permute-done((f32[27,8,128]{2,1,0:T(8,128)S(1)}, f32[27,8,128]{2,1,0:T(8,128)S(1)}, u32[]{:S(2)}, u32[]{:S(2)}) %collective-permute-start.2) | collective-permute-done | bytes 110624 | tf_op jit(solution)/shard_map/ppermute | solution.py:481
  14.6 0.0 collective-permute-done.hb_ref
  14.6 1.4 %inner_edges.1 = (f32[3456,128]{1,0:T(8,128)S(1)}, f32[3456,128]{1,0:T(8,128)}) custom-call(f32[3456,128]{1,0:T(8,128)S(1)} %get-tuple-element.13.part_ref, f32[432,128]{1,0:T(8,128)S(1)} %get-tuple-element.14.dv_ref, f32[54,2,8,128]{3,2,1,0:T(8,128)S(1)} %collective-permute-done.hb_ref, ...), custom_call_target="tpu_custom_call", output_to_operand_aliasing={{0}: (0, {})} | custom-call | flops 1000000 | bytes 3000000 | tf_op jit(solution)/shard_map/inner_edges/pallas_call | solution.py:537
  16.1 0.6 %collective-permute-done.3 = f32[432,2,128]{2,1,0:T(2,128)S(1)} collective-permute-done((f32[432,2,128]{2,1,0:T(2,128)S(1)}, f32[432,2,128]{2,1,0:T(2,128)S(1)}, u32[]{:S(2)}, u32[]{:S(2)}) %collective-permute-start.3) | collective-permute-done | bytes 442400 | tf_op jit(solution)/shard_map/ppermute | solution.py:478
  16.7 0.9 %outer_edges.1 = (f32[3456,128]{1,0:T(8,128)S(1)}, f32[3456,128]{1,0:T(8,128)}) custom-call(f32[3456,128]{1,0:T(8,128)S(1)} %get-tuple-element.18.part_ref, f32[432,128]{1,0:T(8,128)S(1)} %get-tuple-element.14.dv_ref, f32[864,128]{1,0:T(8,128)S(1)} %bitcast.17, f32[3456,128]{1,0:T(8,128)} %get-tuple-element.19.prev), custom_call_target="tpu_custom_call", output_to_operand_aliasing={{0}: (0, {}), {1}: (3, {})} | custom-call | flops 1000000 | bytes 3000000 | tf_op jit(solution)/shard_map/outer_edges/pallas_call | solution.py:548
Async XLA Ops:
  0.0 1.5 %copy-start = (f32[54,8,1024]{2,1,0:T(8,128)S(1)}, f32[54,8,1024]{2,1,0:T(8,128)}, u32[]{:S(2)}) copy-start(f32[54,8,1024]{2,1,0:T(8,128)} %param.10) | copy-start | bytes 5308420
  1.5 9.2 %copy-start.1 = (f32[54,8,1024]{2,1,0:T(8,128)S(1)}, f32[54,8,1024]{2,1,0:T(8,128)}, u32[]{:S(2)}) copy-start(f32[54,8,1024]{2,1,0:T(8,128)} %param.10) | copy-start | bytes 5308420
  1.5 9.2 %copy-start.2 = (bf16[256,256]{1,0:T(8,128)(2,1)S(1)}, bf16[256,256]{1,0:T(8,128)(2,1)}, u32[]{:S(2)}) copy-start(bf16[256,256]{1,0:T(8,128)(2,1)} %constant.2.clone.shift_ref) | copy-start | bytes 393220
  1.6 13.0 %collective-permute-start = (f32[54,2,8,128]{3,2,1,0:T(8,128)S(1)}, f32[54,2,8,128]{3,2,1,0:T(8,128)S(1)}, u32[]{:S(2)}, u32[]{:S(2)}) collective-permute-start(f32[54,2,8,128]{3,2,1,0:T(8,128)S(1)} %get-tuple-element.15), channel_id=1, source_target_pairs={{0,4},{8,12},{16,20},{24,28},{4,0},{12,8},{20,16},{28,24},{1,5},{9... | collective-permute-start | bytes 1327112 | tf_op jit(solution)/shard_map/ppermute | solution.py:479
  3.2 13.5 %collective-permute-start.3 = (f32[432,2,128]{2,1,0:T(2,128)S(1)}, f32[432,2,128]{2,1,0:T(2,128)S(1)}, u32[]{:S(2)}, u32[]{:S(2)}) collective-permute-start(f32[432,2,128]{2,1,0:T(2,128)S(1)} %ahead.1), channel_id=1, source_target_pairs={{4,8},{12,16},{20,24},{28,0},{8,4},{16,12},{24,20},{0,28},{5,9},{1... | collective-permute-start | bytes 1327112 | tf_op jit(solution)/shard_map/ppermute | solution.py:478
  6.8 7.6 %collective-permute-start.1 = (f32[27,8,128]{2,1,0:T(8,128)S(1)}, f32[27,8,128]{2,1,0:T(8,128)S(1)}, u32[]{:S(2)}, u32[]{:S(2)}) collective-permute-start(f32[27,8,128]{2,1,0:T(8,128)S(1)} %get-tuple-element.16), channel_id=1, source_target_pairs={{0,1},{1,2},{2,3},{3,0},{4,5},{5,6},{6,7},{7,4},{8,9},{9,10},{10,1... | collective-permute-start | bytes 331784 | tf_op jit(solution)/shard_map/ppermute | solution.py:480
  8.4 6.2 %collective-permute-start.2 = (f32[27,8,128]{2,1,0:T(8,128)S(1)}, f32[27,8,128]{2,1,0:T(8,128)S(1)}, u32[]{:S(2)}, u32[]{:S(2)}) collective-permute-start(f32[27,8,128]{2,1,0:T(8,128)S(1)} %get-tuple-element.17), channel_id=1, source_target_pairs={{1,0},{2,1},{3,2},{0,3},{5,4},{6,5},{7,6},{4,7},{9,8},{10,9},{11,1... | collective-permute-start | bytes 331784 | tf_op jit(solution)/shard_map/ppermute | solution.py:481

commit v7 on v6

--- a/solution.py
+++ b/solution.py
@@ -348,13 +348,11 @@
         work[second, :] = two - (weight * far_weight) * near
 
 
-def write_out(planes, tiles, work, out, sem, first, last, side=None):
-    where = pl.ds(first * tiles, (last - first) * tiles)
-    kept = pl.ds(0, planes) if side is None else pl.ds(side * (planes - 2), 2)
-    rows = work.shape[0]
-    shape = (rows // planes, planes, LANES)
+def write_out(planes, tiles, work, out, sem, first, last, x, count):
+    shape = (work.shape[0] // planes, planes, LANES)
+    where = (pl.ds(first * tiles, (last - first) * tiles), pl.ds(x, count))
     return pltpu.make_async_copy(
-        work.reshape(*shape).at[where, kept], out.reshape(*shape).at[where, kept], sem
+        work.reshape(*shape).at[where], out.reshape(*shape).at[where], sem
     )
 
 
@@ -385,23 +383,23 @@
             work[end, :] = work[end, :] + weight * highs[j]
 
     half = comps // 2
-    cuts = (0, 2 * (half // 6), 2 * (half // 2), comps)
+    cuts = (0, 2 * (half // 7), 2 * (half // 2), 2 * (half * 5 // 6), comps)
     spans = list(zip(cuts, cuts[1:]))
     odd = odd_place("gx")
     for side in range(2):
 
         @pl.when(odd == 1 - side)
         def _(side=side):
+            kept = (2 * side, planes - 2)
             for i, (first, end) in enumerate(spans):
                 for k in range(first // 2, end // 2):
                     pair(k)
                 add_planes(
                     planes, tiles, work, dv_ref, lambda c, p: hb_ref[c, p], first, end, side
                 )
-                write_out(planes, tiles, work, out, sem.at[i], first, end).start()
-
-    for i, (first, end) in enumerate(spans):
-        write_out(planes, tiles, work, out, sem.at[i], first, end).wait()
+                write_out(planes, tiles, work, out, sem.at[i], first, end, *kept).start()
+            for i, (first, end) in enumerate(spans):
+                write_out(planes, tiles, work, out, sem.at[i], first, end, *kept).wait()
 
 
 def outer_edges_kernel(comps, planes, tiles, part_ref, dv_ref, h_ref, prev, work, out, sem):
@@ -417,11 +415,12 @@
 
         @pl.when(odd == side)
         def _(side=side):
+            kept = (side * (planes - 2), 2)
             for i, (first, last) in enumerate(spans):
                 add_planes(planes, tiles, work, dv_ref, plane, first, last, side)
-                write_out(planes, tiles, work, out, sem.at[i], first, last, side).start()
+                write_out(planes, tiles, work, out, sem.at[i], first, last, *kept).start()
             for i, (first, last) in enumerate(spans):
-                write_out(planes, tiles, work, out, sem.at[i], first, last, side).wait()
+                write_out(planes, tiles, work, out, sem.at[i], first, last, *kept).wait()
 
 
 def per_device(
@@ -539,7 +538,7 @@
         out_shape=(whole, whole),
         in_specs=[vmem] * 5,
         out_specs=(vmem, anywhere),
-        scratch_shapes=[pltpu.SemaphoreType.DMA((3,))],
+        scratch_shapes=[pltpu.SemaphoreType.DMA((4,))],
         input_output_aliases={0: 0},
         compiler_params=params(16),
         cost_estimate=cost,

time: 17.8 us -> 17.8 us (level)
  transfers between devices with their start and end apart: 4 -> 4, of which waited for: 3 -> 3; matrix products, arithmetic and copies ran while one was open for 0% -> 0% of each run, Pallas kernels for 32% -> 31%
where the time goes in v7:
time: 17.8 us; the launch traced here: 17.6 us
  starting transfers between devices  7.99 us (45%)
  Pallas kernels  6.56 us (37%)
  waiting for transfers between devices  1.55 us (9%)
  local copies, waits for them, and re-layouts  1.48 us (8%)
    ppermute x1, starting transfers between devices, per_device(): ha = lax.ppermute(ahead, 'gx', outer)  3.61 us
    pallas_call x1, Pallas kernels, per_device(): pl.pallas_call(functools.partial(main_kernel, comps, planes, tiles, nreac...  3.2 us
    ppermute x1, starting transfers between devices, per_device(): zh = lax.ppermute(low, 'gy', backward)  2.25 us
    ppermute x1, starting transfers between devices, per_device(): zl = lax.ppermute(high, 'gy', forward)  1.58 us
    unnamed x6, local copies, waits for them, and re-layouts  1.48 us
    pallas_call x1, Pallas kernels, per_device(): pl.pallas_call(functools.partial(inner_edges_kernel, comps, planes, tiles...  1.3 us
    pallas_call x1, Pallas kernels, per_device(): pl.pallas_call(functools.partial(ahead_kernel, comps, planes, tiles), out...  1.02 us
    pallas_call x1, Pallas kernels, per_device(): pl.pallas_call(functools.partial(outer_edges_kernel, comps, planes, tiles...  0.91 us
  transfers between devices with their start and end apart: 4, of which 3 were waited for; matrix products, arithmetic and copies ran while one was open for 0% of the time, Pallas kernels for 31%

profile of v7, /device:TPU:0, one launch (start us, length us, event | category | flops | bytes accessed | tf_op | source)
XLA Modules:
  0.0 17.6 jit_solution(12086209409460633378)
XLA Ops:
  0.0 0.0 copy-start
  0.0 1.5 %copy-done = f32[54,8,1024]{2,1,0:T(8,128)S(1)} copy-done((f32[54,8,1024]{2,1,0:T(8,128)S(1)}, f32[54,8,1024]{2,1,0:T(8,128)}, u32[]{:S(2)}) %copy-start) | copy-done | bytes 1769496
  1.5 0.0 copy-start.1
  1.5 0.0 copy-start.2
  1.5 0.1 pack.1
  1.6 0.6 %collective-permute-start = (f32[54,2,8,128]{3,2,1,0:T(8,128)S(1)}, f32[54,2,8,128]{3,2,1,0:T(8,128)S(1)}, u32[]{:S(2)}, u32[]{:S(2)}) collective-permute-start(f32[54,2,8,128]{3,2,1,0:T(8,128)S(1)} %get-tuple-element.15), channel_id=1, source_target_pairs={{0,4},{8,12},{16,20},{24,28},{4,0},{12,8},{20,16},{28,24},{1,5},{9... | collective-permute-start | bytes 1327112 | tf_op jit(solution)/shard_map/ppermute | solution.py:478
  2.2 1.0 %ahead.1 = f32[432,2,128]{2,1,0:T(2,128)S(1)} custom-call(f32[432,4,2,128]{3,2,1,0:T(2,128)} %bitcast.14), custom_call_target="tpu_custom_call" | custom-call | tf_op jit(solution)/shard_map/ahead/pallas_call | solution.py:449
  3.2 3.6 %collective-permute-start.3 = (f32[432,2,128]{2,1,0:T(2,128)S(1)}, f32[432,2,128]{2,1,0:T(2,128)S(1)}, u32[]{:S(2)}, u32[]{:S(2)}) collective-permute-start(f32[432,2,128]{2,1,0:T(2,128)S(1)} %ahead.1), channel_id=1, source_target_pairs={{4,8},{12,16},{20,24},{28,0},{8,4},{16,12},{24,20},{0,28},{5,9},{1... | collective-permute-start | bytes 1327112 | tf_op jit(solution)/shard_map/ppermute | solution.py:477
  6.8 1.6 %collective-permute-start.1 = (f32[27,8,128]{2,1,0:T(8,128)S(1)}, f32[27,8,128]{2,1,0:T(8,128)S(1)}, u32[]{:S(2)}, u32[]{:S(2)}) collective-permute-start(f32[27,8,128]{2,1,0:T(8,128)S(1)} %get-tuple-element.16), channel_id=1, source_target_pairs={{0,1},{1,2},{2,3},{3,0},{4,5},{5,6},{6,7},{7,4},{8,9},{9,10},{10,1... | collective-permute-start | bytes 331784 | tf_op jit(solution)/shard_map/ppermute | solution.py:479
  8.4 2.2 %collective-permute-start.2 = (f32[27,8,128]{2,1,0:T(8,128)S(1)}, f32[27,8,128]{2,1,0:T(8,128)S(1)}, u32[]{:S(2)}, u32[]{:S(2)}) collective-permute-start(f32[27,8,128]{2,1,0:T(8,128)S(1)} %get-tuple-element.17), channel_id=1, source_target_pairs={{1,0},{2,1},{3,2},{0,3},{5,4},{6,5},{7,6},{4,7},{9,8},{10,9},{11,1... | collective-permute-start | bytes 331784 | tf_op jit(solution)/shard_map/ppermute | solution.py:480
  10.6 0.0 copy-done.1
  10.6 0.0 copy-done.2
  10.6 3.2 %main.1 = (f32[3456,128]{1,0:T(8,128)S(1)}, f32[432,128]{1,0:T(8,128)S(1)}) custom-call(f32[3456,128]{1,0:T(8,128)S(1)} %bitcast.16, bf16[256,256]{1,0:T(8,128)(2,1)S(1)} %copy-done.2, f32[54]{0:T(128)} %d_hbm.1, s32[8,8]{1,0:T(8,128)} %sub_hbm.1, s32[8,8]{1,0:T(8,128)} %flame_hbm.1, f32[325]{0:T(512)} %lp_hbm.1, f32[325]{0:T(512)} %act_hbm.1, f32[325]{0:T(512)} %heat_hbm.1, ...), custom_call_target="tpu_custom_call" | custom-call | flops 2000000000 | bytes 16000000 | tf_op jit(solution)/shard_map/main/pallas_call | solution.py:484
  13.8 0.5 %collective-permute-done.1.zl_ref = f32[27,8,128]{2,1,0:T(8,128)S(1)} collective-permute-done((f32[27,8,128]{2,1,0:T(8,128)S(1)}, f32[27,8,128]{2,1,0:T(8,128)S(1)}, u32[]{:S(2)}, u32[]{:S(2)}) %collective-permute-start.1) | collective-permute-done | bytes 110624 | tf_op jit(solution)/shard_map/ppermute | solution.py:479
  14.4 0.2 %collective-permute-done.2.zh_ref = f32[27,8,128]{2,1,0:T(8,128)S(1)} collective-permute-done((f32[27,8,128]{2,1,0:T(8,128)S(1)}, f32[27,8,128]{2,1,0:T(8,128)S(1)}, u32[]{:S(2)}, u32[]{:S(2)}) %collective-permute-start.2) | collective-permute-done | bytes 110624 | tf_op jit(solution)/shard_map/ppermute | solution.py:480
  14.6 0.0 collective-permute-done.hb_ref
  14.6 1.3 %inner_edges.1 = (f32[3456,128]{1,0:T(8,128)S(1)}, f32[3456,128]{1,0:T(8,128)}) custom-call(f32[3456,128]{1,0:T(8,128)S(1)} %get-tuple-element.13.part_ref, f32[432,128]{1,0:T(8,128)S(1)} %get-tuple-element.14.dv_ref, f32[54,2,8,128]{3,2,1,0:T(8,128)S(1)} %collective-permute-done.hb_ref, ...), custom_call_target="tpu_custom_call", output_to_operand_aliasing={{0}: (0, {})} | custom-call | flops 1000000 | bytes 3000000 | tf_op jit(solution)/shard_map/inner_edges/pallas_call | solution.py:536
  15.9 0.8 %collective-permute-done.3 = f32[432,2,128]{2,1,0:T(2,128)S(1)} collective-permute-done((f32[432,2,128]{2,1,0:T(2,128)S(1)}, f32[432,2,128]{2,1,0:T(2,128)S(1)}, u32[]{:S(2)}, u32[]{:S(2)}) %collective-permute-start.3) | collective-permute-done | bytes 442400 | tf_op jit(solution)/shard_map/ppermute | solution.py:477
  16.7 0.9 %outer_edges.1 = (f32[3456,128]{1,0:T(8,128)S(1)}, f32[3456,128]{1,0:T(8,128)}) custom-call(f32[3456,128]{1,0:T(8,128)S(1)} %get-tuple-element.18.part_ref, f32[432,128]{1,0:T(8,128)S(1)} %get-tuple-element.14.dv_ref, f32[864,128]{1,0:T(8,128)S(1)} %bitcast.17, f32[3456,128]{1,0:T(8,128)} %get-tuple-element.19.prev), custom_call_target="tpu_custom_call", output_to_operand_aliasing={{0}: (0, {}), {1}: (3, {})} | custom-call | flops 1000000 | bytes 3000000 | tf_op jit(solution)/shard_map/outer_edges/pallas_call | solution.py:547
Async XLA Ops:
  0.0 1.5 %copy-start = (f32[54,8,1024]{2,1,0:T(8,128)S(1)}, f32[54,8,1024]{2,1,0:T(8,128)}, u32[]{:S(2)}) copy-start(f32[54,8,1024]{2,1,0:T(8,128)} %param.10) | copy-start | bytes 5308420
  1.5 9.2 %copy-start.1 = (f32[54,8,1024]{2,1,0:T(8,128)S(1)}, f32[54,8,1024]{2,1,0:T(8,128)}, u32[]{:S(2)}) copy-start(f32[54,8,1024]{2,1,0:T(8,128)} %param.10) | copy-start | bytes 5308420
  1.5 9.2 %copy-start.2 = (bf16[256,256]{1,0:T(8,128)(2,1)S(1)}, bf16[256,256]{1,0:T(8,128)(2,1)}, u32[]{:S(2)}) copy-start(bf16[256,256]{1,0:T(8,128)(2,1)} %constant.2.clone.shift_ref) | copy-start | bytes 393220
  1.6 13.0 %collective-permute-start = (f32[54,2,8,128]{3,2,1,0:T(8,128)S(1)}, f32[54,2,8,128]{3,2,1,0:T(8,128)S(1)}, u32[]{:S(2)}, u32[]{:S(2)}) collective-permute-start(f32[54,2,8,128]{3,2,1,0:T(8,128)S(1)} %get-tuple-element.15), channel_id=1, source_target_pairs={{0,4},{8,12},{16,20},{24,28},{4,0},{12,8},{20,16},{28,24},{1,5},{9... | collective-permute-start | bytes 1327112 | tf_op jit(solution)/shard_map/ppermute | solution.py:478
  3.2 13.5 %collective-permute-start.3 = (f32[432,2,128]{2,1,0:T(2,128)S(1)}, f32[432,2,128]{2,1,0:T(2,128)S(1)}, u32[]{:S(2)}, u32[]{:S(2)}) collective-permute-start(f32[432,2,128]{2,1,0:T(2,128)S(1)} %ahead.1), channel_id=1, source_target_pairs={{4,8},{12,16},{20,24},{28,0},{8,4},{16,12},{24,20},{0,28},{5,9},{1... | collective-permute-start | bytes 1327112 | tf_op jit(solution)/shard_map/ppermute | solution.py:477
  6.8 7.6 %collective-permute-start.1 = (f32[27,8,128]{2,1,0:T(8,128)S(1)}, f32[27,8,128]{2,1,0:T(8,128)S(1)}, u32[]{:S(2)}, u32[]{:S(2)}) collective-permute-start(f32[27,8,128]{2,1,0:T(8,128)S(1)} %get-tuple-element.16), channel_id=1, source_target_pairs={{0,1},{1,2},{2,3},{3,0},{4,5},{5,6},{6,7},{7,4},{8,9},{9,10},{10,1... | collective-permute-start | bytes 331784 | tf_op jit(solution)/shard_map/ppermute | solution.py:479
  8.4 6.2 %collective-permute-start.2 = (f32[27,8,128]{2,1,0:T(8,128)S(1)}, f32[27,8,128]{2,1,0:T(8,128)S(1)}, u32[]{:S(2)}, u32[]{:S(2)}) collective-permute-start(f32[27,8,128]{2,1,0:T(8,128)S(1)} %get-tuple-element.17), channel_id=1, source_target_pairs={{1,0},{2,1},{3,2},{0,3},{5,4},{6,5},{7,6},{4,7},{9,8},{10,9},{11,1... | collective-permute-start | bytes 331784 | tf_op jit(solution)/shard_map/ppermute | solution.py:480

commit v8 on v7

--- a/solution.py
+++ b/solution.py
@@ -99,6 +99,7 @@
     nreact,
     s_ref,
     shift_ref,
+    s_hbm,
     d_hbm,
     sub_hbm,
     flame_hbm,
@@ -122,13 +123,14 @@
     w1_ref,
     w2_ref,
     a_ref,
-    old_ref,
+    start_ref,
     t_ref,
     st_ref,
     even_ref,
     odd_ref,
     pos_ref,
     sem,
+    row_sem,
 ):
     rows = planes * tiles
     species = comps - 1
@@ -165,6 +167,17 @@
             )
         return count
 
+    def slot_place(g, i, count):
+        slot = g * GROUP + i
+        return pos_ref[jnp.where(slot < count, slot, 0)]
+
+    def gather(g, i, count):
+        return pltpu.make_async_copy(
+            s_hbm.reshape(comps, rows, LANES).at[:, slot_place(g, i, count)],
+            start_ref.at[i],
+            row_sem.at[i],
+        )
+
     padded = q_ref.shape[1]
     wide = w1_ref.shape[0]
 
@@ -233,6 +246,8 @@
     if groups % 2 == 1 and groups > 2:
         product(1, odd_ref)
         count = scan_blocks()
+        for i in range(GROUP):
+            gather(0, i, count).start()
         combine(0, even_ref, False)
 
         def two(i, carry):
@@ -252,6 +267,8 @@
         combine(groups - 1, even_ref, False)
     else:
         count = scan_blocks()
+        for i in range(GROUP):
+            gather(0, i, count).start()
         for load in loads[3:]:
             load.wait()
         tables()
@@ -260,26 +277,32 @@
             if i < groups - 1:
                 product(i + 1, even_ref)
 
+    for i in range(GROUP):
+        gather(0, i, count).wait()
+
     @pl.when(count > 0)
     def _():
         arow = lax.broadcasted_iota(jnp.int32, a_ref.shape, 0)
 
         def group(g, carry):
+            @pl.when(g > 0)
+            def _():
+                for i in range(GROUP):
+                    gather(g, i, count).start()
+                for i in range(GROUP):
+                    gather(g, i, count).wait()
+
             most = jnp.int32(0)
             pieces = []
             for i in range(GROUP):
-                slot = g * GROUP + i
-                here = jnp.where(slot < count, slot, 0)
-                at = pos_ref[here]
+                at = slot_place(g, i, count)
                 n = jnp.where(
-                    slot < count, sub_ref[lax.rem(at, planes), lax.div(at, planes)], 0
+                    g * GROUP + i < count, sub_ref[lax.rem(at, planes), lax.div(at, planes)], 0
                 )
                 most = jnp.maximum(most, n)
                 cols = slice(i * LANES, (i + 1) * LANES)
-                mine = s_ref[pl.ds(block_rows + at, species, stride=rows), :]
-                a_ref[0:species, cols] = mine
-                old_ref[0:species, cols] = mine
-                t_ref[:, cols] = s_ref[pl.ds(at, 1), :]
+                a_ref[0:species, cols] = start_ref[i, 1:comps, :]
+                t_ref[:, cols] = start_ref[i, 0:1, :]
                 pieces.append(jnp.full((1, LANES), n, jnp.int32))
             counts = jnp.concatenate(pieces, 1)
             st_ref[...] = 1.0 / jnp.maximum(counts, 1).astype(jnp.float32)
@@ -325,10 +348,11 @@
                     at = pos_ref[slot]
                     cols = slice(i * LANES, (i + 1) * LANES)
                     where = pl.ds(block_rows + at, species, stride=rows)
-                    change = a_ref[0:species, cols] - old_ref[0:species, cols]
+                    change = a_ref[0:species, cols] - start_ref[i, 1:comps, :]
                     o_ref[where, :] = o_ref[where, :] + change
+                    warmer = t_ref[:, cols] - start_ref[i, 0:1, :]
                     top = pl.ds(at, 1)
-                    o_ref[top, :] = o_ref[top, :] + (t_ref[:, cols] - s_ref[top, :])
+                    o_ref[top, :] = o_ref[top, :] + warmer
 
             return carry
 
@@ -484,7 +508,7 @@
     part, dv = pl.pallas_call(
         functools.partial(main_kernel, comps, planes, tiles, nreact),
         out_shape=(sds((comps * rows, LANES), f32), sds((comps * planes, LANES), f32)),
-        in_specs=[vmem, vmem] + [hbm] * 8,
+        in_specs=[vmem, vmem] + [hbm] * 9,
         out_specs=(vmem, vmem),
         scratch_shapes=[
             SMEM((comps,), f32),
@@ -500,13 +524,14 @@
             VMEM((wide, 3 * PIECE), jnp.bfloat16),
             VMEM((2 * PIECE, 2 * padded), jnp.bfloat16),
             VMEM((PIECE, GROUP * LANES), f32),
-            VMEM((PIECE, GROUP * LANES), f32),
+            VMEM((GROUP, comps, LANES), f32),
             VMEM((1, GROUP * LANES), f32),
             VMEM((1, GROUP * LANES), f32),
             VMEM((many_of(comps) * rows, 2 * LANES), f32),
             VMEM((many_of(comps) * rows, 2 * LANES), f32),
             SMEM((rows + 1,), jnp.int32),
             pltpu.SemaphoreType.DMA((8,)),
+            pltpu.SemaphoreType.DMA((GROUP,)),
         ],
         compiler_params=params(24),
         cost_estimate=pl.CostEstimate(
@@ -519,6 +544,7 @@
         *map(
             stay,
             (
+                flat,
                 diffusivity,
                 substeps,
                 flame,

time: 17.8 us -> 17.9 us (level)
  Pallas kernels: 6.56 us -> 8.16 us
  waiting for transfers between devices: 1.55 us -> 0.01 us
    pallas_call x1, Pallas kernels: 3.2 us -> 4.77 us  [per_device(): pl.pallas_call(functools.partial(main_kernel, comps, planes, tiles, nreac...]
    ppermute x1, waiting for transfers between devices: 0.77 us -> 0.01 us  [per_device(): ha = lax.ppermute(ahead, 'gx', outer)]
    ppermute x1, waiting for transfers between devices: 0.54 us -> 0.01 us  [per_device(): zl = lax.ppermute(high, 'gy', forward)]
    ppermute x1, waiting for transfers between devices: 0.24 us -> 0.01 us  [per_device(): zh = lax.ppermute(low, 'gy', backward)]
    unnamed x6 -> x4, local copies, waits for them, and re-layouts: 1.48 us -> 1.48 us
  transfers between devices with their start and end apart: 4 -> 4, of which waited for: 3 -> 0; matrix products, arithmetic and copies ran while one was open for 0% -> 0% of each run, Pallas kernels for 31% -> 40%
where the time goes in v8:
time: 17.9 us; the launch traced here: 17.7 us
  Pallas kernels  8.16 us (46%)
  starting transfers between devices  7.99 us (45%)
  local copies, waits for them, and re-layouts  1.48 us (8%)
    pallas_call x1, Pallas kernels, per_device(): pl.pallas_call(functools.partial(main_kernel, comps, planes, tiles, nreac...  4.77 us
    ppermute x1, starting transfers between devices, per_device(): ha = lax.ppermute(ahead, 'gx', outer)  3.61 us
    ppermute x1, starting transfers between devices, per_device(): zh = lax.ppermute(low, 'gy', backward)  2.25 us
    ppermute x1, starting transfers between devices, per_device(): zl = lax.ppermute(high, 'gy', forward)  1.58 us
    unnamed x4, local copies, waits for them, and re-layouts  1.48 us
    pallas_call x1, Pallas kernels, per_device(): pl.pallas_call(functools.partial(inner_edges_kernel, comps, planes, tiles...  1.32 us
    pallas_call x1, Pallas kernels, per_device(): pl.pallas_call(functools.partial(ahead_kernel, comps, planes, tiles), out...  1.02 us
    pallas_call x1, Pallas kernels, per_device(): pl.pallas_call(functools.partial(outer_edges_kernel, comps, planes, tiles...  0.92 us
  transfers between devices with their start and end apart: 4, of which 0 were waited for; matrix products, arithmetic and copies ran while one was open for 0% of the time, Pallas kernels for 40%

profile of v8, /device:TPU:0, one launch (start us, length us, event | category | flops | bytes accessed | tf_op | source)
XLA Modules:
  0.0 17.7 jit_solution(6009805840308418670)
XLA Ops:
  0.0 0.0 copy-start
  0.0 1.5 %copy-done = f32[54,8,1024]{2,1,0:T(8,128)S(1)} copy-done((f32[54,8,1024]{2,1,0:T(8,128)S(1)}, f32[54,8,1024]{2,1,0:T(8,128)}, u32[]{:S(2)}) %copy-start) | copy-done | bytes 1769496
  1.5 0.0 copy-start.1
  1.5 0.1 pack.1
  1.6 0.6 %collective-permute-start = (f32[54,2,8,128]{3,2,1,0:T(8,128)S(1)}, f32[54,2,8,128]{3,2,1,0:T(8,128)S(1)}, u32[]{:S(2)}, u32[]{:S(2)}) collective-permute-start(f32[54,2,8,128]{3,2,1,0:T(8,128)S(1)} %get-tuple-element.15), channel_id=1, source_target_pairs={{0,4},{8,12},{16,20},{24,28},{4,0},{12,8},{20,16},{28,24},{1,5},{9... | collective-permute-start | bytes 1327112 | tf_op jit(solution)/shard_map/ppermute | solution.py:502
  2.2 1.0 %ahead.1 = f32[432,2,128]{2,1,0:T(2,128)S(1)} custom-call(f32[432,4,2,128]{3,2,1,0:T(2,128)} %bitcast.14), custom_call_target="tpu_custom_call" | custom-call | tf_op jit(solution)/shard_map/ahead/pallas_call | solution.py:473
  3.2 3.6 %collective-permute-start.3 = (f32[432,2,128]{2,1,0:T(2,128)S(1)}, f32[432,2,128]{2,1,0:T(2,128)S(1)}, u32[]{:S(2)}, u32[]{:S(2)}) collective-permute-start(f32[432,2,128]{2,1,0:T(2,128)S(1)} %ahead.1), channel_id=1, source_target_pairs={{4,8},{12,16},{20,24},{28,0},{8,4},{16,12},{24,20},{0,28},{5,9},{1... | collective-permute-start | bytes 1327112 | tf_op jit(solution)/shard_map/ppermute | solution.py:501
  6.8 1.6 %collective-permute-start.1 = (f32[27,8,128]{2,1,0:T(8,128)S(1)}, f32[27,8,128]{2,1,0:T(8,128)S(1)}, u32[]{:S(2)}, u32[]{:S(2)}) collective-permute-start(f32[27,8,128]{2,1,0:T(8,128)S(1)} %get-tuple-element.16), channel_id=1, source_target_pairs={{0,1},{1,2},{2,3},{3,0},{4,5},{5,6},{6,7},{7,4},{8,9},{9,10},{10,1... | collective-permute-start | bytes 331784 | tf_op jit(solution)/shard_map/ppermute | solution.py:503
  8.4 2.2 %collective-permute-start.2 = (f32[27,8,128]{2,1,0:T(8,128)S(1)}, f32[27,8,128]{2,1,0:T(8,128)S(1)}, u32[]{:S(2)}, u32[]{:S(2)}) collective-permute-start(f32[27,8,128]{2,1,0:T(8,128)S(1)} %get-tuple-element.17), channel_id=1, source_target_pairs={{1,0},{2,1},{3,2},{0,3},{5,4},{6,5},{7,6},{4,7},{9,8},{10,9},{11,1... | collective-permute-start | bytes 331784 | tf_op jit(solution)/shard_map/ppermute | solution.py:504
  10.6 0.0 copy-done.1
  10.6 4.8 %main.1 = (f32[3456,128]{1,0:T(8,128)S(1)}, f32[432,128]{1,0:T(8,128)S(1)}) custom-call(f32[3456,128]{1,0:T(8,128)} %bitcast.15, bf16[256,256]{1,0:T(8,128)(2,1)S(1)} %copy-done.1, f32[3456,128]{1,0:T(8,128)} %bitcast.16, f32[54]{0:T(128)} %d_hbm.1, s32[8,8]{1,0:T(8,128)} %sub_hbm.1, s32[8,8]{1,0:T(8,128)} %flame_hbm.1, f32[325]{0:T(512)} %lp_hbm.1, ...), custom_call_target="tpu_custom_call" | custom-call | flops 2000000000 | bytes 16000000 | tf_op jit(solution)/shard_map/main/pallas_call | solution.py:508
  15.4 0.0 collective-permute-done.1.zl_ref
  15.4 0.0 collective-permute-done.2.zh_ref
  15.4 0.0 collective-permute-done.hb_ref
  15.4 1.3 %inner_edges.1 = (f32[3456,128]{1,0:T(8,128)S(1)}, f32[3456,128]{1,0:T(8,128)}) custom-call(f32[3456,128]{1,0:T(8,128)S(1)} %get-tuple-element.13.part_ref, f32[432,128]{1,0:T(8,128)S(1)} %get-tuple-element.14.dv_ref, f32[54,2,8,128]{3,2,1,0:T(8,128)S(1)} %collective-permute-done.hb_ref, ...), custom_call_target="tpu_custom_call", output_to_operand_aliasing={{0}: (0, {})} | custom-call | flops 1000000 | bytes 3000000 | tf_op jit(solution)/shard_map/inner_edges/pallas_call | solution.py:562
  16.8 0.0 collective-permute-done.3
  16.8 0.9 %outer_edges.1 = (f32[3456,128]{1,0:T(8,128)S(1)}, f32[3456,128]{1,0:T(8,128)}) custom-call(f32[3456,128]{1,0:T(8,128)S(1)} %get-tuple-element.18.part_ref, f32[432,128]{1,0:T(8,128)S(1)} %get-tuple-element.14.dv_ref, f32[864,128]{1,0:T(8,128)S(1)} %bitcast.18, f32[3456,128]{1,0:T(8,128)} %get-tuple-element.19.prev), custom_call_target="tpu_custom_call", output_to_operand_aliasing={{0}: (0, {}), {1}: (3, {})} | custom-call | flops 1000000 | bytes 3000000 | tf_op jit(solution)/shard_map/outer_edges/pallas_call | solution.py:573
Async XLA Ops:
  0.0 1.5 %copy-start = (f32[54,8,1024]{2,1,0:T(8,128)S(1)}, f32[54,8,1024]{2,1,0:T(8,128)}, u32[]{:S(2)}) copy-start(f32[54,8,1024]{2,1,0:T(8,128)} %param.10) | copy-start | bytes 5308420
  1.5 9.2 %copy-start.1 = (bf16[256,256]{1,0:T(8,128)(2,1)S(1)}, bf16[256,256]{1,0:T(8,128)(2,1)}, u32[]{:S(2)}) copy-start(bf16[256,256]{1,0:T(8,128)(2,1)} %constant.2.clone.shift_ref) | copy-start | bytes 393220
  1.6 13.8 %collective-permute-start = (f32[54,2,8,128]{3,2,1,0:T(8,128)S(1)}, f32[54,2,8,128]{3,2,1,0:T(8,128)S(1)}, u32[]{:S(2)}, u32[]{:S(2)}) collective-permute-start(f32[54,2,8,128]{3,2,1,0:T(8,128)S(1)} %get-tuple-element.15), channel_id=1, source_target_pairs={{0,4},{8,12},{16,20},{24,28},{4,0},{12,8},{20,16},{28,24},{1,5},{9... | collective-permute-start | bytes 1327112 | tf_op jit(solution)/shard_map/ppermute | solution.py:502
  3.2 13.6 %collective-permute-start.3 = (f32[432,2,128]{2,1,0:T(2,128)S(1)}, f32[432,2,128]{2,1,0:T(2,128)S(1)}, u32[]{:S(2)}, u32[]{:S(2)}) collective-permute-start(f32[432,2,128]{2,1,0:T(2,128)S(1)} %ahead.1), channel_id=1, source_target_pairs={{4,8},{12,16},{20,24},{28,0},{8,4},{16,12},{24,20},{0,28},{5,9},{1... | collective-permute-start | bytes 1327112 | tf_op jit(solution)/shard_map/ppermute | solution.py:501
  6.8 8.6 %collective-permute-start.1 = (f32[27,8,128]{2,1,0:T(8,128)S(1)}, f32[27,8,128]{2,1,0:T(8,128)S(1)}, u32[]{:S(2)}, u32[]{:S(2)}) collective-permute-start(f32[27,8,128]{2,1,0:T(8,128)S(1)} %get-tuple-element.16), channel_id=1, source_target_pairs={{0,1},{1,2},{2,3},{3,0},{4,5},{5,6},{6,7},{7,4},{8,9},{9,10},{10,1... | collective-permute-start | bytes 331784 | tf_op jit(solution)/shard_map/ppermute | solution.py:503
  8.4 7.0 %collective-permute-start.2 = (f32[27,8,128]{2,1,0:T(8,128)S(1)}, f32[27,8,128]{2,1,0:T(8,128)S(1)}, u32[]{:S(2)}, u32[]{:S(2)}) collective-permute-start(f32[27,8,128]{2,1,0:T(8,128)S(1)} %get-tuple-element.17), channel_id=1, source_target_pairs={{1,0},{2,1},{3,2},{0,3},{5,4},{6,5},{7,6},{4,7},{9,8},{10,9},{11,1... | collective-permute-start | bytes 331784 | tf_op jit(solution)/shard_map/ppermute | solution.py:504

commit v9 on v7

--- a/solution.py
+++ b/solution.py
@@ -127,6 +127,7 @@
     st_ref,
     even_ref,
     odd_ref,
+    third_ref,
     pos_ref,
     sem,
 ):
@@ -152,8 +153,6 @@
         load.start()
 
     def scan_blocks():
-        for load in loads[:3]:
-            load.wait()
         count = jnp.int32(0)
         for x in range(planes):
             for b in range(tiles):
@@ -229,36 +228,40 @@
             scale = d_ref[i * many + j] * (1.0 / 12.0)
             o_ref[where, :] = (v[j] + scale * own[j]).reshape(rows, LANES)
 
-    product(0, even_ref)
-    if groups % 2 == 1 and groups > 2:
-        product(1, odd_ref)
-        count = scan_blocks()
-        combine(0, even_ref, False)
-
-        def two(i, carry):
-            g = 2 * i + 1
-            product(g + 1, even_ref)
-            combine(g, odd_ref, True)
-            product(g + 2, odd_ref)
-            combine(g + 1, even_ref, True)
-            return carry
-
-        lax.fori_loop(0, (groups - 3) // 2, two, 0)
-        for load in loads[3:]:
-            load.wait()
-        product(groups - 1, even_ref)
+    buffers = (even_ref, odd_ref, third_ref)
+
+    def make(i):
+        if i < groups:
+            product(i, buffers[i % 3])
+
+    def use(i):
+        combine(i, buffers[i % 3], 0 < i < groups - 1)
+
+    make(0)
+    make(1)
+    for load in loads[:3]:
+        load.wait()
+    turn = groups // 2
+    always = flame_ref[0, 0] >= 0
+
+    @pl.when(always)
+    def _():
+        pos_ref[rows] = scan_blocks()
+        for i in range(turn):
+            make(i + 2)
+            use(i)
+
+    for load in loads[3:]:
+        load.wait()
+
+    @pl.when(always)
+    def _():
         tables()
-        combine(groups - 2, odd_ref, True)
-        combine(groups - 1, even_ref, False)
-    else:
-        count = scan_blocks()
-        for load in loads[3:]:
-            load.wait()
-        tables()
-        for i in range(groups):
-            combine(i, even_ref, False)
-            if i < groups - 1:
-                product(i + 1, even_ref)
+        for i in range(turn, groups):
+            make(i + 2)
+            use(i)
+
+    count = pos_ref[rows]
 
     @pl.when(count > 0)
     def _():
@@ -505,6 +508,7 @@
             VMEM((1, GROUP * LANES), f32),
             VMEM((many_of(comps) * rows, 2 * LANES), f32),
             VMEM((many_of(comps) * rows, 2 * LANES), f32),
+            VMEM((many_of(comps) * rows, 2 * LANES), f32),
             SMEM((rows + 1,), jnp.int32),
             pltpu.SemaphoreType.DMA((8,)),
         ],

time: 17.8 us -> 17.8 us (level)
  Pallas kernels: 6.56 us -> 6.32 us
  waiting for transfers between devices: 1.55 us -> 1.78 us
    pallas_call x1, Pallas kernels: 3.2 us -> 2.96 us  [per_device(): pl.pallas_call(functools.partial(main_kernel, comps, planes, tiles, nreac...]
    ppermute x1, waiting for transfers between devices: 0.54 us -> 0.77 us  [per_device(): zl = lax.ppermute(high, 'gy', forward)]
  transfers between devices with their start and end apart: 4 -> 4, of which waited for: 3 -> 3; matrix products, arithmetic and copies ran while one was open for 0% -> 0% of each run, Pallas kernels for 31% -> 30%
where the time goes in v9:
time: 17.8 us; the launch traced here: 17.6 us
  starting transfers between devices  7.99 us (45%)
  Pallas kernels  6.32 us (36%)
  waiting for transfers between devices  1.78 us (10%)
  local copies, waits for them, and re-layouts  1.48 us (8%)
    ppermute x1, starting transfers between devices, per_device(): ha = lax.ppermute(ahead, 'gx', outer)  3.61 us
    pallas_call x1, Pallas kernels, per_device(): pl.pallas_call(functools.partial(main_kernel, comps, planes, tiles, nreac...  2.96 us
    ppermute x1, starting transfers between devices, per_device(): zh = lax.ppermute(low, 'gy', backward)  2.25 us
    ppermute x1, starting transfers between devices, per_device(): zl = lax.ppermute(high, 'gy', forward)  1.58 us
    unnamed x6, local copies, waits for them, and re-layouts  1.48 us
    pallas_call x1, Pallas kernels, per_device(): pl.pallas_call(functools.partial(inner_edges_kernel, comps, planes, tiles...  1.3 us
    pallas_call x1, Pallas kernels, per_device(): pl.pallas_call(functools.partial(ahead_kernel, comps, planes, tiles), out...  1.02 us
    pallas_call x1, Pallas kernels, per_device(): pl.pallas_call(functools.partial(outer_edges_kernel, comps, planes, tiles...  0.91 us
  transfers between devices with their start and end apart: 4, of which 3 were waited for; matrix products, arithmetic and copies ran while one was open for 0% of the time, Pallas kernels for 30%

profile of v9, /device:TPU:0, one launch (start us, length us, event | category | flops | bytes accessed | tf_op | source)
XLA Modules:
  0.0 17.6 jit_solution(10444569894935532281)
XLA Ops:
  0.0 0.0 copy-start
  0.0 1.5 %copy-done = f32[54,8,1024]{2,1,0:T(8,128)S(1)} copy-done((f32[54,8,1024]{2,1,0:T(8,128)S(1)}, f32[54,8,1024]{2,1,0:T(8,128)}, u32[]{:S(2)}) %copy-start) | copy-done | bytes 1769496
  1.5 0.0 copy-start.1
  1.5 0.0 copy-start.2
  1.5 0.1 pack.1
  1.6 0.6 %collective-permute-start = (f32[54,2,8,128]{3,2,1,0:T(8,128)S(1)}, f32[54,2,8,128]{3,2,1,0:T(8,128)S(1)}, u32[]{:S(2)}, u32[]{:S(2)}) collective-permute-start(f32[54,2,8,128]{3,2,1,0:T(8,128)S(1)} %get-tuple-element.15), channel_id=1, source_target_pairs={{0,4},{8,12},{16,20},{24,28},{4,0},{12,8},{20,16},{28,24},{1,5},{9... | collective-permute-start | bytes 1327112 | tf_op jit(solution)/shard_map/ppermute | solution.py:481
  2.2 1.0 %ahead.1 = f32[432,2,128]{2,1,0:T(2,128)S(1)} custom-call(f32[432,4,2,128]{3,2,1,0:T(2,128)} %bitcast.14), custom_call_target="tpu_custom_call" | custom-call | tf_op jit(solution)/shard_map/ahead/pallas_call | solution.py:452
  3.2 3.6 %collective-permute-start.3 = (f32[432,2,128]{2,1,0:T(2,128)S(1)}, f32[432,2,128]{2,1,0:T(2,128)S(1)}, u32[]{:S(2)}, u32[]{:S(2)}) collective-permute-start(f32[432,2,128]{2,1,0:T(2,128)S(1)} %ahead.1), channel_id=1, source_target_pairs={{4,8},{12,16},{20,24},{28,0},{8,4},{16,12},{24,20},{0,28},{5,9},{1... | collective-permute-start | bytes 1327112 | tf_op jit(solution)/shard_map/ppermute | solution.py:480
  6.8 1.6 %collective-permute-start.1 = (f32[27,8,128]{2,1,0:T(8,128)S(1)}, f32[27,8,128]{2,1,0:T(8,128)S(1)}, u32[]{:S(2)}, u32[]{:S(2)}) collective-permute-start(f32[27,8,128]{2,1,0:T(8,128)S(1)} %get-tuple-element.16), channel_id=1, source_target_pairs={{0,1},{1,2},{2,3},{3,0},{4,5},{5,6},{6,7},{7,4},{8,9},{9,10},{10,1... | collective-permute-start | bytes 331784 | tf_op jit(solution)/shard_map/ppermute | solution.py:482
  8.4 2.2 %collective-permute-start.2 = (f32[27,8,128]{2,1,0:T(8,128)S(1)}, f32[27,8,128]{2,1,0:T(8,128)S(1)}, u32[]{:S(2)}, u32[]{:S(2)}) collective-permute-start(f32[27,8,128]{2,1,0:T(8,128)S(1)} %get-tuple-element.17), channel_id=1, source_target_pairs={{1,0},{2,1},{3,2},{0,3},{5,4},{6,5},{7,6},{4,7},{9,8},{10,9},{11,1... | collective-permute-start | bytes 331784 | tf_op jit(solution)/shard_map/ppermute | solution.py:483
  10.6 0.0 copy-done.1
  10.6 0.0 copy-done.2
  10.6 3.0 %main.1 = (f32[3456,128]{1,0:T(8,128)S(1)}, f32[432,128]{1,0:T(8,128)S(1)}) custom-call(f32[3456,128]{1,0:T(8,128)S(1)} %bitcast.16, bf16[256,256]{1,0:T(8,128)(2,1)S(1)} %copy-done.2, f32[54]{0:T(128)} %d_hbm.1, s32[8,8]{1,0:T(8,128)} %sub_hbm.1, s32[8,8]{1,0:T(8,128)} %flame_hbm.1, f32[325]{0:T(512)} %lp_hbm.1, f32[325]{0:T(512)} %act_hbm.1, f32[325]{0:T(512)} %heat_hbm.1, ...), custom_call_target="tpu_custom_call" | custom-call | flops 2000000000 | bytes 16000000 | tf_op jit(solution)/shard_map/main/pallas_call | solution.py:487
  13.6 0.8 %collective-permute-done.1.zl_ref = f32[27,8,128]{2,1,0:T(8,128)S(1)} collective-permute-done((f32[27,8,128]{2,1,0:T(8,128)S(1)}, f32[27,8,128]{2,1,0:T(8,128)S(1)}, u32[]{:S(2)}, u32[]{:S(2)}) %collective-permute-start.1) | collective-permute-done | bytes 110624 | tf_op jit(solution)/shard_map/ppermute | solution.py:482
  14.4 0.2 %collective-permute-done.2.zh_ref = f32[27,8,128]{2,1,0:T(8,128)S(1)} collective-permute-done((f32[27,8,128]{2,1,0:T(8,128)S(1)}, f32[27,8,128]{2,1,0:T(8,128)S(1)}, u32[]{:S(2)}, u32[]{:S(2)}) %collective-permute-start.2) | collective-permute-done | bytes 110624 | tf_op jit(solution)/shard_map/ppermute | solution.py:483
  14.6 0.0 collective-permute-done.hb_ref
  14.6 1.3 %inner_edges.1 = (f32[3456,128]{1,0:T(8,128)S(1)}, f32[3456,128]{1,0:T(8,128)}) custom-call(f32[3456,128]{1,0:T(8,128)S(1)} %get-tuple-element.13.part_ref, f32[432,128]{1,0:T(8,128)S(1)} %get-tuple-element.14.dv_ref, f32[54,2,8,128]{3,2,1,0:T(8,128)S(1)} %collective-permute-done.hb_ref, ...), custom_call_target="tpu_custom_call", output_to_operand_aliasing={{0}: (0, {})} | custom-call | flops 1000000 | bytes 3000000 | tf_op jit(solution)/shard_map/inner_edges/pallas_call | solution.py:540
  15.9 0.8 %collective-permute-done.3 = f32[432,2,128]{2,1,0:T(2,128)S(1)} collective-permute-done((f32[432,2,128]{2,1,0:T(2,128)S(1)}, f32[432,2,128]{2,1,0:T(2,128)S(1)}, u32[]{:S(2)}, u32[]{:S(2)}) %collective-permute-start.3) | collective-permute-done | bytes 442400 | tf_op jit(solution)/shard_map/ppermute | solution.py:480
  16.7 0.9 %outer_edges.1 = (f32[3456,128]{1,0:T(8,128)S(1)}, f32[3456,128]{1,0:T(8,128)}) custom-call(f32[3456,128]{1,0:T(8,128)S(1)} %get-tuple-element.18.part_ref, f32[432,128]{1,0:T(8,128)S(1)} %get-tuple-element.14.dv_ref, f32[864,128]{1,0:T(8,128)S(1)} %bitcast.17, f32[3456,128]{1,0:T(8,128)} %get-tuple-element.19.prev), custom_call_target="tpu_custom_call", output_to_operand_aliasing={{0}: (0, {}), {1}: (3, {})} | custom-call | flops 1000000 | bytes 3000000 | tf_op jit(solution)/shard_map/outer_edges/pallas_call | solution.py:551
Async XLA Ops:
  0.0 1.5 %copy-start = (f32[54,8,1024]{2,1,0:T(8,128)S(1)}, f32[54,8,1024]{2,1,0:T(8,128)}, u32[]{:S(2)}) copy-start(f32[54,8,1024]{2,1,0:T(8,128)} %param.10) | copy-start | bytes 5308420
  1.5 9.2 %copy-start.1 = (f32[54,8,1024]{2,1,0:T(8,128)S(1)}, f32[54,8,1024]{2,1,0:T(8,128)}, u32[]{:S(2)}) copy-start(f32[54,8,1024]{2,1,0:T(8,128)} %param.10) | copy-start | bytes 5308420
  1.5 9.2 %copy-start.2 = (bf16[256,256]{1,0:T(8,128)(2,1)S(1)}, bf16[256,256]{1,0:T(8,128)(2,1)}, u32[]{:S(2)}) copy-start(bf16[256,256]{1,0:T(8,128)(2,1)} %constant.2.clone.shift_ref) | copy-start | bytes 393220
  1.6 13.0 %collective-permute-start = (f32[54,2,8,128]{3,2,1,0:T(8,128)S(1)}, f32[54,2,8,128]{3,2,1,0:T(8,128)S(1)}, u32[]{:S(2)}, u32[]{:S(2)}) collective-permute-start(f32[54,2,8,128]{3,2,1,0:T(8,128)S(1)} %get-tuple-element.15), channel_id=1, source_target_pairs={{0,4},{8,12},{16,20},{24,28},{4,0},{12,8},{20,16},{28,24},{1,5},{9... | collective-permute-start | bytes 1327112 | tf_op jit(solution)/shard_map/ppermute | solution.py:481
  3.2 13.5 %collective-permute-start.3 = (f32[432,2,128]{2,1,0:T(2,128)S(1)}, f32[432,2,128]{2,1,0:T(2,128)S(1)}, u32[]{:S(2)}, u32[]{:S(2)}) collective-permute-start(f32[432,2,128]{2,1,0:T(2,128)S(1)} %ahead.1), channel_id=1, source_target_pairs={{4,8},{12,16},{20,24},{28,0},{8,4},{16,12},{24,20},{0,28},{5,9},{1... | collective-permute-start | bytes 1327112 | tf_op jit(solution)/shard_map/ppermute | solution.py:480
  6.8 7.6 %collective-permute-start.1 = (f32[27,8,128]{2,1,0:T(8,128)S(1)}, f32[27,8,128]{2,1,0:T(8,128)S(1)}, u32[]{:S(2)}, u32[]{:S(2)}) collective-permute-start(f32[27,8,128]{2,1,0:T(8,128)S(1)} %get-tuple-element.16), channel_id=1, source_target_pairs={{0,1},{1,2},{2,3},{3,0},{4,5},{5,6},{6,7},{7,4},{8,9},{9,10},{10,1... | collective-permute-start | bytes 331784 | tf_op jit(solution)/shard_map/ppermute | solution.py:482
  8.4 6.2 %collective-permute-start.2 = (f32[27,8,128]{2,1,0:T(8,128)S(1)}, f32[27,8,128]{2,1,0:T(8,128)S(1)}, u32[]{:S(2)}, u32[]{:S(2)}) collective-permute-start(f32[27,8,128]{2,1,0:T(8,128)S(1)} %get-tuple-element.17), channel_id=1, source_target_pairs={{1,0},{2,1},{3,2},{0,3},{5,4},{6,5},{7,6},{4,7},{9,8},{10,9},{11,1... | collective-permute-start | bytes 331784 | tf_op jit(solution)/shard_map/ppermute | solution.py:483

commit v10 on v9

--- a/solution.py
+++ b/solution.py
@@ -89,7 +89,7 @@
 
 
 def many_of(comps):
-    return max(n for n in range(1, 7) if comps % n == 0)
+    return max(n for n in range(1, 4) if comps % n == 0)
 
 
 def main_kernel(
@@ -386,7 +386,7 @@
             work[end, :] = work[end, :] + weight * highs[j]
 
     half = comps // 2
-    cuts = (0, 2 * (half // 7), 2 * (half // 2), 2 * (half * 5 // 6), comps)
+    cuts = (0, 2 * (half // 5), 2 * (half // 2), 2 * (half * 7 // 9), comps)
     spans = list(zip(cuts, cuts[1:]))
     odd = odd_place("gx")
     for side in range(2):
@@ -412,7 +412,7 @@
     def plane(c, p):
         return h_ref[pl.ds(c * 2 * tiles + p, tiles, stride=2), :]
 
-    bounds = [0, comps // 3, comps]
+    bounds = [0, comps // 3, comps * 3 // 4, comps]
     spans = list(zip(bounds, bounds[1:]))
     for side in range(2):
 
@@ -553,7 +553,7 @@
         out_shape=(whole, whole),
         in_specs=[vmem] * 3 + [anywhere],
         out_specs=(vmem, anywhere),
-        scratch_shapes=[pltpu.SemaphoreType.DMA((2,))],
+        scratch_shapes=[pltpu.SemaphoreType.DMA((3,))],
         input_output_aliases={0: 0, 3: 1},
         compiler_params=params(16),
         cost_estimate=cost,

time: 17.8 us -> 17.7 us (level)
  no operation moved by 1% of the time
where the time goes in v10:
time: 17.7 us; the launch traced here: 17.6 us
  starting transfers between devices  7.99 us (45%)
  Pallas kernels  6.3 us (36%)
  waiting for transfers between devices  1.76 us (10%)
  local copies, waits for them, and re-layouts  1.48 us (8%)
    ppermute x1, starting transfers between devices, per_device(): ha = lax.ppermute(ahead, 'gx', outer)  3.61 us
    pallas_call x1, Pallas kernels, per_device(): pl.pallas_call(functools.partial(main_kernel, comps, planes, tiles, nreac...  3 us
    ppermute x1, starting transfers between devices, per_device(): zh = lax.ppermute(low, 'gy', backward)  2.25 us
    ppermute x1, starting transfers between devices, per_device(): zl = lax.ppermute(high, 'gy', forward)  1.58 us
    unnamed x6, local copies, waits for them, and re-layouts  1.48 us
    pallas_call x1, Pallas kernels, per_device(): pl.pallas_call(functools.partial(inner_edges_kernel, comps, planes, tiles...  1.29 us
    pallas_call x1, Pallas kernels, per_device(): pl.pallas_call(functools.partial(ahead_kernel, comps, planes, tiles), out...  1.02 us
    pallas_call x1, Pallas kernels, per_device(): pl.pallas_call(functools.partial(outer_edges_kernel, comps, planes, tiles...  0.86 us
  transfers between devices with their start and end apart: 4, of which 3 were waited for; matrix products, arithmetic and copies ran while one was open for 0% of the time, Pallas kernels for 30%

profile of v10, /device:TPU:0, one launch (start us, length us, event | category | flops | bytes accessed | tf_op | source)
XLA Modules:
  0.0 17.6 jit_solution(16390718813267729894)
XLA Ops:
  0.0 0.0 copy-start
  0.0 1.5 %copy-done = f32[54,8,1024]{2,1,0:T(8,128)S(1)} copy-done((f32[54,8,1024]{2,1,0:T(8,128)S(1)}, f32[54,8,1024]{2,1,0:T(8,128)}, u32[]{:S(2)}) %copy-start) | copy-done | bytes 1769496
  1.5 0.0 copy-start.1
  1.5 0.0 copy-start.2
  1.5 0.1 pack.1
  1.6 0.6 %collective-permute-start = (f32[54,2,8,128]{3,2,1,0:T(8,128)S(1)}, f32[54,2,8,128]{3,2,1,0:T(8,128)S(1)}, u32[]{:S(2)}, u32[]{:S(2)}) collective-permute-start(f32[54,2,8,128]{3,2,1,0:T(8,128)S(1)} %get-tuple-element.15), channel_id=1, source_target_pairs={{0,4},{8,12},{16,20},{24,28},{4,0},{12,8},{20,16},{28,24},{1,5},{9... | collective-permute-start | bytes 1327112 | tf_op jit(solution)/shard_map/ppermute | solution.py:481
  2.2 1.0 %ahead.1 = f32[432,2,128]{2,1,0:T(2,128)S(1)} custom-call(f32[432,4,2,128]{3,2,1,0:T(2,128)} %bitcast.14), custom_call_target="tpu_custom_call" | custom-call | tf_op jit(solution)/shard_map/ahead/pallas_call | solution.py:452
  3.2 3.6 %collective-permute-start.3 = (f32[432,2,128]{2,1,0:T(2,128)S(1)}, f32[432,2,128]{2,1,0:T(2,128)S(1)}, u32[]{:S(2)}, u32[]{:S(2)}) collective-permute-start(f32[432,2,128]{2,1,0:T(2,128)S(1)} %ahead.1), channel_id=1, source_target_pairs={{4,8},{12,16},{20,24},{28,0},{8,4},{16,12},{24,20},{0,28},{5,9},{1... | collective-permute-start | bytes 1327112 | tf_op jit(solution)/shard_map/ppermute | solution.py:480
  6.8 1.6 %collective-permute-start.1 = (f32[27,8,128]{2,1,0:T(8,128)S(1)}, f32[27,8,128]{2,1,0:T(8,128)S(1)}, u32[]{:S(2)}, u32[]{:S(2)}) collective-permute-start(f32[27,8,128]{2,1,0:T(8,128)S(1)} %get-tuple-element.16), channel_id=1, source_target_pairs={{0,1},{1,2},{2,3},{3,0},{4,5},{5,6},{6,7},{7,4},{8,9},{9,10},{10,1... | collective-permute-start | bytes 331784 | tf_op jit(solution)/shard_map/ppermute | solution.py:482
  8.4 2.2 %collective-permute-start.2 = (f32[27,8,128]{2,1,0:T(8,128)S(1)}, f32[27,8,128]{2,1,0:T(8,128)S(1)}, u32[]{:S(2)}, u32[]{:S(2)}) collective-permute-start(f32[27,8,128]{2,1,0:T(8,128)S(1)} %get-tuple-element.17), channel_id=1, source_target_pairs={{1,0},{2,1},{3,2},{0,3},{5,4},{6,5},{7,6},{4,7},{9,8},{10,9},{11,1... | collective-permute-start | bytes 331784 | tf_op jit(solution)/shard_map/ppermute | solution.py:483
  10.6 0.0 copy-done.1
  10.6 0.0 copy-done.2
  10.6 3.0 %main.1 = (f32[3456,128]{1,0:T(8,128)S(1)}, f32[432,128]{1,0:T(8,128)S(1)}) custom-call(f32[3456,128]{1,0:T(8,128)S(1)} %bitcast.16, bf16[256,256]{1,0:T(8,128)(2,1)S(1)} %copy-done.2, f32[54]{0:T(128)} %d_hbm.1, s32[8,8]{1,0:T(8,128)} %sub_hbm.1, s32[8,8]{1,0:T(8,128)} %flame_hbm.1, f32[325]{0:T(512)} %lp_hbm.1, f32[325]{0:T(512)} %act_hbm.1, f32[325]{0:T(512)} %heat_hbm.1, ...), custom_call_target="tpu_custom_call" | custom-call | flops 2000000000 | bytes 16000000 | tf_op jit(solution)/shard_map/main/pallas_call | solution.py:487
  13.7 0.7 %collective-permute-done.1.zl_ref = f32[27,8,128]{2,1,0:T(8,128)S(1)} collective-permute-done((f32[27,8,128]{2,1,0:T(8,128)S(1)}, f32[27,8,128]{2,1,0:T(8,128)S(1)}, u32[]{:S(2)}, u32[]{:S(2)}) %collective-permute-start.1) | collective-permute-done | bytes 110624 | tf_op jit(solution)/shard_map/ppermute | solution.py:482
  14.4 0.2 %collective-permute-done.2.zh_ref = f32[27,8,128]{2,1,0:T(8,128)S(1)} collective-permute-done((f32[27,8,128]{2,1,0:T(8,128)S(1)}, f32[27,8,128]{2,1,0:T(8,128)S(1)}, u32[]{:S(2)}, u32[]{:S(2)}) %collective-permute-start.2) | collective-permute-done | bytes 110624 | tf_op jit(solution)/shard_map/ppermute | solution.py:483
  14.6 0.0 collective-permute-done.hb_ref
  14.6 1.3 %inner_edges.1 = (f32[3456,128]{1,0:T(8,128)S(1)}, f32[3456,128]{1,0:T(8,128)}) custom-call(f32[3456,128]{1,0:T(8,128)S(1)} %get-tuple-element.13.part_ref, f32[432,128]{1,0:T(8,128)S(1)} %get-tuple-element.14.dv_ref, f32[54,2,8,128]{3,2,1,0:T(8,128)S(1)} %collective-permute-done.hb_ref, ...), custom_call_target="tpu_custom_call", output_to_operand_aliasing={{0}: (0, {})} | custom-call | flops 1000000 | bytes 3000000 | tf_op jit(solution)/shard_map/inner_edges/pallas_call | solution.py:540
  15.9 0.8 %collective-permute-done.3 = f32[432,2,128]{2,1,0:T(2,128)S(1)} collective-permute-done((f32[432,2,128]{2,1,0:T(2,128)S(1)}, f32[432,2,128]{2,1,0:T(2,128)S(1)}, u32[]{:S(2)}, u32[]{:S(2)}) %collective-permute-start.3) | collective-permute-done | bytes 442400 | tf_op jit(solution)/shard_map/ppermute | solution.py:480
  16.7 0.9 %outer_edges.1 = (f32[3456,128]{1,0:T(8,128)S(1)}, f32[3456,128]{1,0:T(8,128)}) custom-call(f32[3456,128]{1,0:T(8,128)S(1)} %get-tuple-element.18.part_ref, f32[432,128]{1,0:T(8,128)S(1)} %get-tuple-element.14.dv_ref, f32[864,128]{1,0:T(8,128)S(1)} %bitcast.17, f32[3456,128]{1,0:T(8,128)} %get-tuple-element.19.prev), custom_call_target="tpu_custom_call", output_to_operand_aliasing={{0}: (0, {}), {1}: (3, {})} | custom-call | flops 1000000 | bytes 3000000 | tf_op jit(solution)/shard_map/outer_edges/pallas_call | solution.py:551
Async XLA Ops:
  0.0 1.5 %copy-start = (f32[54,8,1024]{2,1,0:T(8,128)S(1)}, f32[54,8,1024]{2,1,0:T(8,128)}, u32[]{:S(2)}) copy-start(f32[54,8,1024]{2,1,0:T(8,128)} %param.10) | copy-start | bytes 5308420
  1.5 9.2 %copy-start.1 = (f32[54,8,1024]{2,1,0:T(8,128)S(1)}, f32[54,8,1024]{2,1,0:T(8,128)}, u32[]{:S(2)}) copy-start(f32[54,8,1024]{2,1,0:T(8,128)} %param.10) | copy-start | bytes 5308420
  1.5 9.2 %copy-start.2 = (bf16[256,256]{1,0:T(8,128)(2,1)S(1)}, bf16[256,256]{1,0:T(8,128)(2,1)}, u32[]{:S(2)}) copy-start(bf16[256,256]{1,0:T(8,128)(2,1)} %constant.2.clone.shift_ref) | copy-start | bytes 393220
  1.6 13.0 %collective-permute-start = (f32[54,2,8,128]{3,2,1,0:T(8,128)S(1)}, f32[54,2,8,128]{3,2,1,0:T(8,128)S(1)}, u32[]{:S(2)}, u32[]{:S(2)}) collective-permute-start(f32[54,2,8,128]{3,2,1,0:T(8,128)S(1)} %get-tuple-element.15), channel_id=1, source_target_pairs={{0,4},{8,12},{16,20},{24,28},{4,0},{12,8},{20,16},{28,24},{1,5},{9... | collective-permute-start | bytes 1327112 | tf_op jit(solution)/shard_map/ppermute | solution.py:481
  3.2 13.5 %collective-permute-start.3 = (f32[432,2,128]{2,1,0:T(2,128)S(1)}, f32[432,2,128]{2,1,0:T(2,128)S(1)}, u32[]{:S(2)}, u32[]{:S(2)}) collective-permute-start(f32[432,2,128]{2,1,0:T(2,128)S(1)} %ahead.1), channel_id=1, source_target_pairs={{4,8},{12,16},{20,24},{28,0},{8,4},{16,12},{24,20},{0,28},{5,9},{1... | collective-permute-start | bytes 1327112 | tf_op jit(solution)/shard_map/ppermute | solution.py:480
  6.8 7.6 %collective-permute-start.1 = (f32[27,8,128]{2,1,0:T(8,128)S(1)}, f32[27,8,128]{2,1,0:T(8,128)S(1)}, u32[]{:S(2)}, u32[]{:S(2)}) collective-permute-start(f32[27,8,128]{2,1,0:T(8,128)S(1)} %get-tuple-element.16), channel_id=1, source_target_pairs={{0,1},{1,2},{2,3},{3,0},{4,5},{5,6},{6,7},{7,4},{8,9},{9,10},{10,1... | collective-permute-start | bytes 331784 | tf_op jit(solution)/shard_map/ppermute | solution.py:482
  8.4 6.2 %collective-permute-start.2 = (f32[27,8,128]{2,1,0:T(8,128)S(1)}, f32[27,8,128]{2,1,0:T(8,128)S(1)}, u32[]{:S(2)}, u32[]{:S(2)}) collective-permute-start(f32[27,8,128]{2,1,0:T(8,128)S(1)} %get-tuple-element.17), channel_id=1, source_target_pairs={{1,0},{2,1},{3,2},{0,3},{5,4},{6,5},{7,6},{4,7},{9,8},{10,9},{11,1... | collective-permute-start | bytes 331784 | tf_op jit(solution)/shard_map/ppermute | solution.py:483
